TPU v7x, 768 devices: a whole 4x8x12 slice. The times are simulated.
768 devices in a mesh: dp: 192 (over x, y_lo, z, core), pipe: 4 (over y_hi).
Axes of the slice: x: 4, y: 8 (y_hi: 4, y_lo: 2; y = y_hi * 2 + y_lo), z: 12, core: 2. Of those that a mesh axis runs over, the one named last changes fastest.
Arguments:
- acts: bfloat16 [4, 2, 12288, 4224], P('pipe', None, 'dp'), may hold values from -6 to 6
- out_grad: bfloat16 [2, 12288, 4224], P(None, 'dp'), may hold values from -6 to 6
- params: bfloat16 [4, 768, 4224], P('pipe'), may hold values from -0.09375 to 0.09375
- moment: float32 [4, 1081344], P('pipe', 'dp'), may hold values from -2 to 2
- second: float32 [4, 1081344], P('pipe', 'dp'), may hold values from 0.0001 to 0.01
Outputs:
- in_grad: bfloat16 [4, 2, 12288, 4224], P('pipe', None, 'dp')
- new_moment: float32 [4, 1081344], P('pipe', 'dp')
- new_second: float32 [4, 1081344], P('pipe', 'dp')
- update: float32 [4, 1081344], P('pipe', 'dp')
All inputs are finite; a program needn't handle non-finite values.
Results may differ from a plain program's by a relative error of at most 0.0056.
Values may be sent and summed in bfloat16 or wider, within the bound.
No kernel may reach another device: no remote copies, remote signals or barrier semaphores. Data moves between devices by JAX's collectives and lax.ppermute only.
A program may use at most 64 MiB of HBM per device.

v0:
```python
import jax
import jax.numpy as jnp
from jax import lax
from jax.sharding import PartitionSpec as P


def from_behind(value, axis, steps):
    count = lax.axis_size(axis)
    leading, last = (max(0, -steps), min(count, count - steps))
    return lax.ppermute(value, axis, [(source, source + steps) for source in range(leading, last)])


def backward(inputs, grad_rows, weights_in, weights_down):
    block_size = weights_down.shape[0]
    gate_up = lax.dot_general(
        inputs, weights_in, (((1,), (1,)), ((), ())), preferred_element_type=jnp.float32
    )
    gate_values = gate_up[:, :block_size]
    up_values = gate_up[:, block_size:]
    sigmoid_gate = jax.nn.sigmoid(gate_values)
    activated = gate_values * sigmoid_gate
    d_hidden = lax.dot_general(
        grad_rows, weights_down, (((1,), (1,)), ((), ())), preferred_element_type=jnp.float32
    )
    d_gate = d_hidden * up_values * sigmoid_gate * (1.0 + gate_values * (1.0 - sigmoid_gate))
    d_up = d_hidden * activated
    d_gate_up = jnp.concatenate([d_gate, d_up], axis=1).astype(jnp.bfloat16)
    hidden = (activated * up_values).astype(jnp.bfloat16)
    passed = grad_rows.astype(jnp.float32) + jnp.dot(
        d_gate_up, weights_in, preferred_element_type=jnp.float32
    )
    return (passed.astype(jnp.bfloat16), hidden)


def place_slot(stack, value, slot_index, active):
    previous = lax.dynamic_index_in_dim(stack, slot_index, 0, keepdims=False)
    return lax.dynamic_update_index_in_dim(stack, jnp.where(active, value, previous), slot_index, 0)


def weight_terms(hidden, grad_rows):
    lower = lax.dot_general(
        hidden, grad_rows, (((0,), (0,)), ((), ())), preferred_element_type=jnp.float32
    )
    return lower.reshape(-1)


def local(acts, out_grad, params, moment, second):
    sections = lax.axis_size("pipe")
    section_index = lax.axis_index("pipe")
    inputs = acts[0]
    micro_count = inputs.shape[0]
    tok_rows = inputs.shape[1]
    weights = params[0]
    block_size = weights.shape[0] // 3
    weights_in = weights[: 2 * block_size]
    weights_down = weights[2 * block_size :]
    in_grads = jnp.zeros_like(inputs)
    arrived = jnp.zeros_like(inputs)
    hiddens = jnp.zeros((micro_count, tok_rows, block_size), jnp.bfloat16)
    incoming = jnp.zeros_like(inputs[0])
    tick_count = sections + micro_count - 1
    for tick_index in range(tick_count):
        offset = tick_index - (sections - 1) + section_index
        active = jnp.logical_and(offset >= 0, offset < micro_count)
        slot_index = jnp.clip(offset, 0, micro_count - 1)
        current = lax.dynamic_index_in_dim(inputs, slot_index, 0, keepdims=False)
        top_grad = lax.dynamic_index_in_dim(out_grad, slot_index, 0, keepdims=False)
        grad_rows = jnp.where(section_index == sections - 1, top_grad, incoming)

        def working(current=current, grad_rows=grad_rows):
            return backward(current, grad_rows, weights_in, weights_down)

        def resting(current=current):
            return (jnp.zeros_like(current), jnp.zeros((tok_rows, block_size), jnp.bfloat16))

        passed, hidden = lax.cond(active, working, resting)
        in_grads = place_slot(in_grads, passed, slot_index, active)
        arrived = place_slot(arrived, grad_rows, slot_index, active)
        hiddens = place_slot(hiddens, hidden, slot_index, active)
        if tick_index + 1 < tick_count:
            incoming = from_behind(passed, "pipe", -1)
    row_count = micro_count * tok_rows
    term = weight_terms(hiddens.reshape(row_count, -1), arrived.reshape(row_count, -1))
    summed = lax.psum_scatter(term, "dp", scatter_dimension=0, tiled=True)
    grad_scale = float(row_count * lax.axis_size("dp")) ** (-0.5)
    gradient = summed * grad_scale
    new_moment = 0.9 * moment[0] + 0.1 * gradient
    new_second = 0.999 * second[0] + 0.001 * gradient * gradient
    update = new_moment / (1.0 - 0.9**10) / (jnp.sqrt(new_second / (1.0 - 0.999**10)) + 1e-08)
    return (in_grads[None], new_moment[None], new_second[None], update[None])


def solution(mesh):
    placed = (
        P("pipe", None, "dp", None),
        P(None, "dp", None),
        P("pipe", None, None),
        P("pipe", "dp"),
        P("pipe", "dp"),
    )
    return jax.shard_map(
        local,
        mesh=mesh,
        in_specs=placed,
        out_specs=(P("pipe", None, "dp", None), P("pipe", "dp"), P("pipe", "dp"), P("pipe", "dp")),
        check_vma=False,
    )
```

profile of v0, /device:TPU:1, one launch (start us, length us, event | category | flops | bytes accessed | tf_op | source)
XLA Modules:
  0.0 1797.7 jit_solution(3982633755356680525)
XLA Ops:
  7.2 1.8 slice_bitcast_fusion.1
  9.0 4.5 slice_bitcast_fusion
  13.6 1.3 select_dynamic-update-slice_fusion
  16.7 1.3 collective-permute-start
  19.0 1.3 dynamic-slice.20
  20.9 2.1 constant_dynamic-slice_fusion.3
  23.0 21.0 %collective-permute-done = bf16[64,4224]{1,0:T(8,128)(2,1)} collective-permute-done((bf16[64,4224]{1,0:T(8,128)(2,1)}, bf16[64,4224]{1,0:T(8,128)(2,1)}, u32[]{:S(2)}, u32[]{:S(2)}) %collective-permute-start) | collective-permute-done | bytes 540704 | tf_op jit(solution)/shard_map/ppermute | solution.py:10
  44.1 2.2 bitcast_dynamic-update-slice_fusion.3
  47.2 1.4 collective-permute-start.1
  48.6 1.3 bitcast_dynamic-update-slice_fusion.7
  50.0 22.7 %collective-permute-done.1 = bf16[64,4224]{1,0:T(8,128)(2,1)S(1)} collective-permute-done((bf16[64,4224]{1,0:T(8,128)(2,1)}, bf16[64,4224]{1,0:T(8,128)(2,1)S(1)}, u32[]{:S(2)}, u32[]{:S(2)}) %collective-permute-start.1) | collective-permute-done | bytes 540704 | tf_op jit(solution)/shard_map/ppermute | solution.py:10
  73.0 1.0 copy-done.6
  74.1 1.4 collective-permute-start.2
  75.5 1.1 constant_dynamic-slice_fusion.1
  76.6 24.3 %collective-permute-done.2 = bf16[64,4224]{1,0:T(8,128)(2,1)S(1)} collective-permute-done((bf16[64,4224]{1,0:T(8,128)(2,1)S(1)}, bf16[64,4224]{1,0:T(8,128)(2,1)S(1)}, u32[]{:S(2)}, u32[]{:S(2)}) %collective-permute-start.2) | collective-permute-done | bytes 540704 | tf_op jit(solution)/shard_map/ppermute | solution.py:10
  101.0 1.3 bitcast_dynamic-update-slice_fusion.1
  102.3 1.0 copy-done.8
  103.3 5.5 conditional.8
  103.3 3.8 fusion.32
  108.8 1.4 collective-permute-start.3
  110.3 1.1 constant_dynamic-slice_fusion
  111.4 22.8 %collective-permute-done.3 = bf16[64,4224]{1,0:T(8,128)(2,1)S(1)} collective-permute-done((bf16[64,4224]{1,0:T(8,128)(2,1)S(1)}, bf16[64,4224]{1,0:T(8,128)(2,1)S(1)}, u32[]{:S(2)}, u32[]{:S(2)}) %collective-permute-start.3) | collective-permute-done | bytes 540704 | tf_op jit(solution)/shard_map/ppermute | solution.py:10
  134.2 1.3 bitcast_dynamic-update-slice_fusion
  135.5 1.0 copy-done.10
  136.5 6.3 conditional.9
  136.5 3.8 fusion.42
  141.1 1.7 fusion.41
  142.8 4.0 convolution_bitcast_fusion
  146.9 4.9 reshape.32
  151.9 1.0 copy-done.17
  154.1 1.2 bitcast_dynamic-update-slice_fusion.4
  155.4 1632.7 %all-reduce.3.cloned.1.call-done = f32[1081344]{0:T(1024)} async-done(((f32[1081344]{0:T(1024)}), f32[1081344]{0:T(1024)}) %all-reduce.3.cloned.1.call-update) | async-done | bytes 4325392
  (81 shorter events, 12.4 us)
Async XLA Ops:
  7.2 1780.9 %all-reduce.3.cloned.1.call-start = ((), (), s32[]{:S(2)}) async-start(), calls=%async_computation | async-start | bytes 8650752
  13.6 1.5 copy-start.11
  14.9 1.0 copy-start.4
  16.7 27.3 %collective-permute-start = (bf16[64,4224]{1,0:T(8,128)(2,1)}, bf16[64,4224]{1,0:T(8,128)(2,1)}, u32[]{:S(2)}, u32[]{:S(2)}) collective-permute-start(bf16[64,4224]{1,0:T(8,128)(2,1)} %get-tuple-element.166), channel_id=1, source_target_pairs={{1,0},{2,1},{3,2},{5,4},{6,5},{7,6},{9,8},{10,9},{11,10},{13,12},{... | collective-permute-start | bytes 1622024 | tf_op jit(solution)/shard_map/ppermute | solution.py:10
  18.1 0.7 copy-start.21
  18.1 0.7 copy-start.22
  20.9 25.4 %copy-start = (bf16[512,4224]{1,0:T(8,128)(2,1)S(1)}, bf16[512,4224]{1,0:T(8,128)(2,1)}, u32[]{:S(2)}) copy-start(bf16[512,4224]{1,0:T(8,128)(2,1)} %slice_bitcast_fusion) | copy-start | bytes 12976132
  47.2 2.8 copy-start.5
  47.2 25.6 %collective-permute-start.1 = (bf16[64,4224]{1,0:T(8,128)(2,1)}, bf16[64,4224]{1,0:T(8,128)(2,1)S(1)}, u32[]{:S(2)}, u32[]{:S(2)}) collective-permute-start(bf16[64,4224]{1,0:T(8,128)(2,1)} %get-tuple-element.167), channel_id=1, source_target_pairs={{1,0},{2,1},{3,2},{5,4},{6,5},{7,6},{9,8},{10,9},{11,10},{13,12},{... | collective-permute-start | bytes 1622024 | tf_op jit(solution)/shard_map/ppermute | solution.py:10
  48.6 24.2 %copy-start.15 = (bf16[2,64,4224]{2,1,0:T(8,128)(2,1)S(1)}, bf16[2,64,4224]{2,1,0:T(8,128)(2,1)}, u32[]{:S(2)}) copy-start(bf16[2,64,4224]{2,1,0:T(8,128)(2,1)} %param.16) | copy-start | bytes 3244036
  50.0 23.0 %copy-start.12 = (bf16[1,2,64,4224]{3,2,1,0:T(8,128)(2,1)S(1)}, bf16[1,2,64,4224]{3,2,1,0:T(8,128)(2,1)}, u32[]{:S(2)}) copy-start(bf16[1,2,64,4224]{3,2,1,0:T(8,128)(2,1)} %param.15) | copy-start | bytes 3244036
  73.0 1.0 copy-start.6
  74.0 28.2 %copy-start.16 = (bf16[64,4224]{1,0:T(8,128)(2,1)}, bf16[64,4224]{1,0:T(8,128)(2,1)S(1)}, u32[]{:S(2)}) copy-start(bf16[64,4224]{1,0:T(8,128)(2,1)S(1)} %get-tuple-element.168) | copy-start | bytes 1622020
  74.0 26.9 %copy-start.7 = (bf16[2,64,4224]{2,1,0:T(8,128)(2,1)S(1)}, bf16[2,64,4224]{2,1,0:T(8,128)(2,1)}, u32[]{:S(2)}) copy-start(bf16[2,64,4224]{2,1,0:T(8,128)(2,1)} %copy-done.6) | copy-start | bytes 3244036
  74.1 26.9 %collective-permute-start.2 = (bf16[64,4224]{1,0:T(8,128)(2,1)S(1)}, bf16[64,4224]{1,0:T(8,128)(2,1)S(1)}, u32[]{:S(2)}, u32[]{:S(2)}) collective-permute-start(bf16[64,4224]{1,0:T(8,128)(2,1)S(1)} %get-tuple-element.168), channel_id=1, source_target_pairs={{1,0},{2,1},{3,2},{5,4},{6,5},{7,6},{9,8},{10,9},{11,10},{13,12},{... | collective-permute-start | bytes 1622024 | tf_op jit(solution)/shard_map/ppermute | solution.py:10
  76.6 25.7 %copy-start.13 = (bf16[1,2,64,4224]{3,2,1,0:T(8,128)(2,1)S(1)}, bf16[1,2,64,4224]{3,2,1,0:T(8,128)(2,1)}, u32[]{:S(2)}) copy-start(bf16[1,2,64,4224]{3,2,1,0:T(8,128)(2,1)} %param.15) | copy-start | bytes 3244036
  102.3 1.0 copy-start.8
  103.3 4.6 copy-start.2
  108.8 26.7 %copy-start.18 = (bf16[64,4224]{1,0:T(8,128)(2,1)}, bf16[64,4224]{1,0:T(8,128)(2,1)S(1)}, u32[]{:S(2)}) copy-start(bf16[64,4224]{1,0:T(8,128)(2,1)S(1)} %get-tuple-element.169) | copy-start | bytes 1622020
  108.8 25.4 %copy-start.9 = (bf16[2,64,4224]{2,1,0:T(8,128)(2,1)S(1)}, bf16[2,64,4224]{2,1,0:T(8,128)(2,1)}, u32[]{:S(2)}) copy-start(bf16[2,64,4224]{2,1,0:T(8,128)(2,1)} %copy-done.8) | copy-start | bytes 3244036
  108.8 25.4 %collective-permute-start.3 = (bf16[64,4224]{1,0:T(8,128)(2,1)S(1)}, bf16[64,4224]{1,0:T(8,128)(2,1)S(1)}, u32[]{:S(2)}, u32[]{:S(2)}) collective-permute-start(bf16[64,4224]{1,0:T(8,128)(2,1)S(1)} %get-tuple-element.169), channel_id=1, source_target_pairs={{1,0},{2,1},{3,2},{5,4},{6,5},{7,6},{9,8},{10,9},{11,10},{13,12},{... | collective-permute-start | bytes 1622024 | tf_op jit(solution)/shard_map/ppermute | solution.py:10
  111.4 24.1 %copy-start.14 = (bf16[1,2,64,4224]{3,2,1,0:T(8,128)(2,1)S(1)}, bf16[1,2,64,4224]{3,2,1,0:T(8,128)(2,1)}, u32[]{:S(2)}) copy-start(bf16[1,2,64,4224]{3,2,1,0:T(8,128)(2,1)} %param.15) | copy-start | bytes 3244036
  135.5 1.0 copy-start.10
  136.5 4.6 copy-start.3
  151.8 1.0 copy-start.17
  152.9 1.0 copy-start.19
  155.3 1635.5 %copy-start.20 = (bf16[1,2,64,4224]{3,2,1,0:T(8,128)(2,1)}, bf16[1,2,64,4224]{3,2,1,0:T(8,128)(2,1)S(1)}, u32[]{:S(2)}) copy-start(bf16[1,2,64,4224]{3,2,1,0:T(8,128)(2,1)S(1)} %bitcast_dynamic-update-slice_fusion.4) | copy-start | bytes 3244036
Sparse Core Ops, SparseCore 0:
  151.9 1636.1 all-reduce.2
where the time goes:
time: 1800 us
  waiting for transfers between devices  1720 us (96%)
  local copies, waits for them, and re-layouts  27 us (2%)
    unnamed x2, waiting for transfers between devices  1630 us
    ppermute x4, waiting for transfers between devices, from_behind(): lax.ppermute(value, axis, [(source, source + steps) for source in range(l...  90.9 us
  transfers between devices with their start and end apart: 5, of which 5 were waited for; matrix products, arithmetic and copies ran while one was open for 1% of the time, Pallas kernels for 0%

commit v1 on v0

v1 whole, which is shorter than its diff:
```python
import jax
import jax.numpy as jnp
from jax import lax
from jax.sharding import Mesh, PartitionSpec as P

CHUNKS = 4
DP = ("x", "yl", "z", "core")


def shifted(value, rows, steps, lead, total):
    width = value.shape[1]
    pad = jnp.zeros((lead * rows, width), value.dtype)
    padded = jnp.concatenate([pad, value, pad], axis=0)
    return lax.dynamic_slice(padded, (steps * rows, 0), (total * rows, width))


def reduce_rows(term):
    core = lax.axis_index("core")
    shares = term.reshape(96, 2, -1, 128)
    mine = jnp.where(core == 0, shares[:, 0], shares[:, 1])
    other = jnp.where(core == 0, shares[:, 1], shares[:, 0]).astype(jnp.bfloat16)
    got = lax.ppermute(other, "core", [(0, 1), (1, 0)])
    half = (mine + got.astype(jnp.float32)).astype(jnp.bfloat16)
    got = lax.all_to_all(half, ("x", "yl", "z"), 0, 0, tiled=True)
    return jnp.sum(got.astype(jnp.float32), axis=0).reshape(-1)


def local(acts, out_grad, params, moment, second):
    sections = lax.axis_size("pipe")
    section = lax.axis_index("pipe")
    width = acts.shape[-1]
    inputs = acts.reshape(-1, width)
    top = out_grad.reshape(-1, width)
    tokens = inputs.shape[0]
    rows = tokens // CHUNKS
    lead = sections - 1
    ticks = CHUNKS + lead
    block = params.shape[1] // 3
    weights_in = params[0, : 2 * block]
    weights_down = params[0, 2 * block :]
    gate_up = lax.dot_general(
        inputs, weights_in, (((1,), (1,)), ((), ())), preferred_element_type=jnp.float32
    )
    gate = gate_up[:, :block]
    up = gate_up[:, block:]
    sg = jax.nn.sigmoid(gate)
    activated = gate * sg
    factors = jnp.concatenate([up * sg * (1.0 + gate * (1.0 - sg)), activated], axis=1)
    hidden = (activated * up).astype(jnp.bfloat16)
    factors = shifted(factors, rows, section, lead, ticks)

    incoming = jnp.zeros((rows, width), jnp.bfloat16)
    grads = []
    passes = []
    for tick in range(ticks):
        grad = incoming
        if tick < CHUNKS:
            grad = jnp.where(section == lead, top[tick * rows : (tick + 1) * rows], incoming)
        d_hidden = lax.dot_general(
            grad, weights_down, (((1,), (1,)), ((), ())), preferred_element_type=jnp.float32
        )
        part = factors[tick * rows : (tick + 1) * rows]
        d_gate_up = (jnp.concatenate([d_hidden, d_hidden], axis=1) * part).astype(jnp.bfloat16)
        passed = grad.astype(jnp.float32) + jnp.dot(
            d_gate_up, weights_in, preferred_element_type=jnp.float32
        )
        passed = passed.astype(jnp.bfloat16)
        grads.append(grad)
        passes.append(passed)
        if tick + 1 < ticks:
            incoming = lax.ppermute(passed, "pipe", [(s, s - 1) for s in range(1, sections)])
    first = (lead - section) * rows
    arrived = lax.dynamic_slice(jnp.concatenate(grads, axis=0), (first, 0), (tokens, width))
    in_grads = lax.dynamic_slice(jnp.concatenate(passes, axis=0), (first, 0), (tokens, width))
    term = lax.dot_general(
        hidden, arrived, (((0,), (0,)), ((), ())), preferred_element_type=jnp.float32
    )
    total = tokens * lax.axis_size(DP)
    gradient = reduce_rows(term) * float(total) ** (-0.5)
    new_moment = 0.9 * moment[0] + 0.1 * gradient
    new_second = 0.999 * second[0] + 0.001 * gradient * gradient
    update = new_moment / (1.0 - 0.9**10) / (jnp.sqrt(new_second / (1.0 - 0.999**10)) + 1e-08)
    return (in_grads.reshape(acts.shape), new_moment[None], new_second[None], update[None])


def solution(mesh):
    fine = Mesh(mesh.devices.reshape(4, 2, 12, 2, 4), DP + ("pipe",))
    placed = (
        P("pipe", None, DP, None),
        P(None, DP, None),
        P("pipe", None, None),
        P("pipe", DP),
        P("pipe", DP),
    )
    return jax.shard_map(
        local,
        mesh=fine,
        in_specs=placed,
        out_specs=(P("pipe", None, DP, None), P("pipe", DP), P("pipe", DP), P("pipe", DP)),
        check_vma=False,
    )
```

time: 1800 us -> 210 us (0.12)
  the two profiles are of different devices: /device:TPU:1 before, /device:TPU:24 now
where the time goes in v1:
time: 210 us
  waiting for transfers between devices  107 us (51%)
  starting transfers between devices  48.9 us (23%)
  matrix products  36.3 us (17%)
  local copies, waits for them, and re-layouts  9.87 us (5%)
  other arithmetic  6.52 us (3%)
    ppermute x6, waiting for transfers between devices, local(): lax.ppermute(passed, 'pipe', [(s, s - 1) for s in range(1, sections)])  65.2 us
    all_to_all x1, waiting for transfers between devices, reduce_rows(): got = lax.all_to_all(half, ('x', 'yl', 'z'), 0, 0, tiled=True)  39.4 us
    all_to_all x1, starting transfers between devices, reduce_rows(): got = lax.all_to_all(half, ('x', 'yl', 'z'), 0, 0, tiled=True)  34.5 us
    dot_general x7, matrix products, local(): jnp.dot(d_gate_up, weights_in, preferred_element_type=jnp.float32)  17.8 us
    ppermute x6, starting transfers between devices, local(): lax.ppermute(passed, 'pipe', [(s, s - 1) for s in range(1, sections)])  12.5 us
    dot_general x7, matrix products, local(): lax.dot_general(grad, weights_down, (((1,), (1,)), ((), ())), preferred_e...  11.7 us
    reshape x1, local copies, waits for them, and re-layouts, reduce_rows(): shares = term.reshape(96, 2, -1, 128)  5.17 us
  transfers between devices with their start and end apart: 8, of which 8 were waited for; matrix products, arithmetic and copies ran while one was open for 3% of the time, Pallas kernels for 0%

profile of v1, /device:TPU:24, one launch (start us, length us, event | category | flops | bytes accessed | tf_op | source)
XLA Modules:
  0.0 209.9 jit_solution(13986824650981207221)
XLA Ops:
  0.7 1.2 copy-done
  1.9 3.9 %fusion.14 = f32[128,512]{1,0:T(8,128)S(1)} fusion(bf16[128,4224]{1,0:T(8,128)(2,1)S(1)} %bitcast.84, bf16[1,768,4224]{2,1,0:T(8,128)(2,1)} %param.7), kind=kOutput, calls=%fused_computation.15 | convolution fusion | flops 553648128 | bytes 5668864 | tf_op jit(solution)/shard_map/dot_general | solution.py:41
  7.2 2.6 %fusion.29 = f32[32,256]{1,0:T(8,128)S(1)} fusion(bf16[1,768,4224]{2,1,0:T(8,128)(2,1)} %param.7, bf16[128,4224]{1,0:T(8,128)(2,1)} %bitcast.88, pred[]{:T(512)S(6)} %eq.4), kind=kOutput, calls=%fused_computation.33 | convolution fusion | flops 69341184 | bytes 2465793 | tf_op jit(solution)/shard_map/dot_general | solution.py:59
  10.1 3.3 %constant_dynamic-update-slice_fusion.5 = (bf16[224,4224]{1,0:T(8,128)(2,1)S(1)}, bf16[32,4224]{1,0:T(8,128)(2,1)S(1)}) fusion(bf16[1,768,4224]{2,1,0:T(8,128)(2,1)} %param.7, f32[224,512]{1,0:T(8,128)S(1)} %fusion.50, f32[32,256]{1,0:T(8,128)S(1)} %fusion.29, bf16[128,4224]{1,0:T(8,128)(2,1)} %bitcast.89, pred[]{:T(512)S(6)} %eq.4), kind=kOutput, calls=%fused_computation.96 | convolution fusion | flops 139001856 | bytes 5234689 | tf_op jit(solution)/shard_map/dot_general | solution.py:64
  13.4 2.2 %collective-permute-start = (bf16[32,4224]{1,0:T(8,128)(2,1)S(1)}, bf16[32,4224]{1,0:T(8,128)(2,1)S(1)}, u32[]{:S(2)}, u32[]{:S(2)}) collective-permute-start(bf16[32,4224]{1,0:T(8,128)(2,1)S(1)} %get-tuple-element.18), channel_id=1, source_target_pairs={{1,0},{2,1},{3,2},{5,4},{6,5},{7,6},{9,8},{10,9},{11,10},{13,12},{... | collective-permute-start | bytes 811016 | tf_op jit(solution)/shard_map/ppermute | solution.py:71
  15.7 10.2 %collective-permute-done = bf16[32,4224]{1,0:T(8,128)(2,1)S(1)} collective-permute-done((bf16[32,4224]{1,0:T(8,128)(2,1)S(1)}, bf16[32,4224]{1,0:T(8,128)(2,1)S(1)}, u32[]{:S(2)}, u32[]{:S(2)}) %collective-permute-start) | collective-permute-done | bytes 270368 | tf_op jit(solution)/shard_map/ppermute | solution.py:71
  27.6 2.1 collective-permute-start.1
  29.7 9.4 %collective-permute-done.1 = bf16[32,4224]{1,0:T(8,128)(2,1)S(1)} collective-permute-done((bf16[32,4224]{1,0:T(8,128)(2,1)S(1)}, bf16[32,4224]{1,0:T(8,128)(2,1)S(1)}, u32[]{:S(2)}, u32[]{:S(2)}) %collective-permute-start.1) | collective-permute-done | bytes 270368 | tf_op jit(solution)/shard_map/ppermute | solution.py:71
  40.8 1.9 collective-permute-start.2
  42.8 9.7 %collective-permute-done.2 = bf16[32,4224]{1,0:T(8,128)(2,1)S(1)} collective-permute-done((bf16[32,4224]{1,0:T(8,128)(2,1)S(1)}, bf16[32,4224]{1,0:T(8,128)(2,1)S(1)}, u32[]{:S(2)}, u32[]{:S(2)}) %collective-permute-start.2) | collective-permute-done | bytes 270368 | tf_op jit(solution)/shard_map/ppermute | solution.py:71
  53.3 1.6 constant_dynamic-update-slice_fusion.2
  54.9 1.2 copy-done.6
  56.2 2.5 %collective-permute-start.3 = (bf16[32,4224]{1,0:T(8,128)(2,1)}, bf16[32,4224]{1,0:T(8,128)(2,1)S(1)}, u32[]{:S(2)}, u32[]{:S(2)}) collective-permute-start(bf16[32,4224]{1,0:T(8,128)(2,1)} %get-tuple-element.24), channel_id=1, source_target_pairs={{1,0},{2,1},{3,2},{5,4},{6,5},{7,6},{9,8},{10,9},{11,10},{13,12},{... | collective-permute-start | bytes 811016 | tf_op jit(solution)/shard_map/ppermute | solution.py:71
  58.7 12.6 %collective-permute-done.3 = bf16[32,4224]{1,0:T(8,128)(2,1)S(1)} collective-permute-done((bf16[32,4224]{1,0:T(8,128)(2,1)}, bf16[32,4224]{1,0:T(8,128)(2,1)S(1)}, u32[]{:S(2)}, u32[]{:S(2)}) %collective-permute-start.3) | collective-permute-done | bytes 270368 | tf_op jit(solution)/shard_map/ppermute | solution.py:71
  71.3 2.3 %fusion.21 = f32[32,256]{1,0:T(8,128)S(1)} fusion(bf16[32,4224]{1,0:T(8,128)(2,1)S(1)} %collective-permute-done.3, bf16[1,768,4224]{2,1,0:T(8,128)(2,1)} %param.7), kind=kOutput, calls=%fused_computation.25 | convolution fusion | flops 69206016 | bytes 2465792 | tf_op jit(solution)/shard_map/dot_general | solution.py:59
  73.6 4.0 %constant_dynamic-update-slice_fusion.1 = (bf16[224,4224]{1,0:T(8,128)(2,1)}, bf16[32,4224]{1,0:T(8,128)(2,1)S(1)}) fusion(bf16[224,4224]{1,0:T(8,128)(2,1)} %copy-done.6, bf16[1,768,4224]{2,1,0:T(8,128)(2,1)} %param.7, f32[224,512]{1,0:T(8,128)} %copy-done.2, f32[32,256]{1,0:T(8,128)S(1)} %fusion.21, bf16[32,4224]{1,0:T(8,128)(2,1)S(1)} %collective-permute-done.3), kind=kOutput, calls=%fused_computation.92 | convolution fusion | flops 138866688 | bytes 5234688 | tf_op jit(solution)/shard_map/dot_general | solution.py:64
  77.6 1.9 collective-permute-start.4
  79.6 11.9 %collective-permute-done.4 = bf16[32,4224]{1,0:T(8,128)(2,1)S(1)} collective-permute-done((bf16[32,4224]{1,0:T(8,128)(2,1)S(1)}, bf16[32,4224]{1,0:T(8,128)(2,1)S(1)}, u32[]{:S(2)}, u32[]{:S(2)}) %collective-permute-start.4) | collective-permute-done | bytes 270368 | tf_op jit(solution)/shard_map/ppermute | solution.py:71
  91.5 2.3 %fusion.19 = f32[32,256]{1,0:T(8,128)S(1)} fusion(bf16[32,4224]{1,0:T(8,128)(2,1)S(1)} %collective-permute-done.4, bf16[1,768,4224]{2,1,0:T(8,128)(2,1)} %param.7), kind=kOutput, calls=%fused_computation.23 | convolution fusion | flops 69206016 | bytes 2465792 | tf_op jit(solution)/shard_map/dot_general | solution.py:59
  93.8 3.9 %constant_dynamic-update-slice_fusion = (bf16[224,4224]{1,0:T(8,128)(2,1)}, bf16[32,4224]{1,0:T(8,128)(2,1)S(1)}) fusion(bf16[224,4224]{1,0:T(8,128)(2,1)} %get-tuple-element.25, bf16[1,768,4224]{2,1,0:T(8,128)(2,1)} %param.7, f32[224,512]{1,0:T(8,128)} %copy-done.2, f32[32,256]{1,0:T(8,128)S(1)} %fusion.19, bf16[32,4224]{1,0:T(8,128)(2,1)S(1)} %collective-permute-done.4), kind=kOutput, calls=%fused_computation.91 | convolution fusion | flops 138866688 | bytes 5234688 | tf_op jit(solution)/shard_map/dot_general | solution.py:64
  97.7 1.9 collective-permute-start.5
  99.7 11.4 %collective-permute-done.5 = bf16[32,4224]{1,0:T(8,128)(2,1)S(1)} collective-permute-done((bf16[32,4224]{1,0:T(8,128)(2,1)S(1)}, bf16[32,4224]{1,0:T(8,128)(2,1)S(1)}, u32[]{:S(2)}, u32[]{:S(2)}) %collective-permute-start.5) | collective-permute-done | bytes 270368 | tf_op jit(solution)/shard_map/ppermute | solution.py:71
  111.1 2.9 %fusion.32 = f32[256,4224]{1,0:T(8,128)} fusion(bf16[224,4224]{1,0:T(8,128)(2,1)S(1)} %constant_dynamic-update-slice_fusion.6, s32[]{:T(128)S(6)} %select_n.49, f32[128,512]{1,0:T(8,128)S(1)} %copy-done.9), kind=kOutput, calls=%fused_computation.36 | convolution fusion | flops 277020672 | bytes 5668868 | tf_op jit(solution)/shard_map/dot_general | solution.py:75
  113.9 5.2 %reshape.69 = f32[96,2,44,128]{3,2,1,0:T(8,128)} reshape(f32[256,4224]{1,0:T(8,128)} %fusion.32) | data formatting | bytes 8650752 | tf_op jit(solution)/shard_map/reshape | solution.py:19
  119.1 2.8 %fusion.31 = bf16[96,44,128]{2,1,0:T(8,128)(2,1)S(1)} fusion(f32[96,2,44,128]{3,2,1,0:T(8,128)} %reshape.69, pred[]{:T(512)S(6)} %eq.5), kind=kLoop, calls=%fused_computation.35 | loop fusion | flops 540672 | bytes 3244033 | tf_op jit(solution)/shard_map/convert_element_type | solution.py:21
  122.1 1.9 collective-permute-start.6
  124.1 2.7 %collective-permute-done.6 = bf16[96,44,128]{2,0,1:T(8,128)(2,1)S(1)} collective-permute-done((bf16[96,44,128]{2,0,1:T(8,128)(2,1)S(1)}, bf16[96,44,128]{2,0,1:T(8,128)(2,1)S(1)}, u32[]{:S(2)}, u32[]{:S(2)}) %collective-permute-start.6) | collective-permute-done | bytes 1081376 | tf_op jit(solution)/shard_map/ppermute | solution.py:22
  126.7 1.6 fusion.16
  128.3 34.5 %all-to-all-start = ((bf16[96,44,128]{2,1,0:T(8,128)(2,1)}), bf16[96,44,128]{2,1,0:T(8,128)(2,1)S(1)}, u32[]{:S(2)}, u32[]{:S(2)}) async-start(bf16[96,44,128]{2,1,0:T(8,128)(2,1)} %fusion.16), calls=%async_computation | async-start | bytes 2359296 | tf_op jit(solution)/shard_map/all_to_all | solution.py:24
  162.8 2.5 %fusion.17 = f32[32,256]{1,0:T(8,128)S(1)} fusion(bf16[32,4224]{1,0:T(8,128)(2,1)S(1)} %collective-permute-done.5, bf16[1,768,4224]{2,1,0:T(8,128)(2,1)} %param.7), kind=kOutput, calls=%fused_computation.21 | convolution fusion | flops 69206016 | bytes 2465792 | tf_op jit(solution)/shard_map/dot_general | solution.py:59
  165.3 3.1 %fusion.52 = bf16[224,4224]{1,0:T(8,128)(2,1)S(1)} fusion(bf16[224,4224]{1,0:T(8,128)(2,1)S(1)} %copy-done.7, bf16[32,4224]{1,0:T(8,128)(2,1)S(1)} %collective-permute-done.5, bf16[1,768,4224]{2,1,0:T(8,128)(2,1)} %param.7, f32[224,512]{1,0:T(8,128)} %copy-done.2, f32[32,256]{1,0:T(8,128)S(1)} %fusion.17), kind=kOutput, calls=%fused_computation.66 | convolution fusion | flops 138866688 | bytes 4964352 | tf_op jit(solution)/shard_map/dot_general | solution.py:64
  169.5 39.4 %all-to-all-done = bf16[96,44,128]{2,1,0:T(8,128)(2,1)S(1)} async-done(((bf16[96,44,128]{2,1,0:T(8,128)(2,1)}), bf16[96,44,128]{2,1,0:T(8,128)(2,1)S(1)}, u32[]{:S(2)}, u32[]{:S(2)}) %all-to-all-start) | async-done | bytes 1081376 | tf_op jit(solution)/shard_map/all_to_all | solution.py:24
  (49 shorter events, 8.3 us)
Async XLA Ops:
  0.6 1.2 copy-start
  1.9 24.1 %slice-start = ((s8[6488064]{0:T(1024)(128)(4,1)}), s8[2293760]{0:T(1024)(128)(4,1)S(1)}, s32[]{:S(2)}) async-start(s8[6488064]{0:T(1024)(128)(4,1)} %bitcast.85), calls=%async_computation.1 | async-start | bytes 4587520
  5.8 0.7 copy-start.8
  7.2 2.6 %copy-start.10 = (f32[128,256]{1,0:T(8,128)S(1)}, f32[128,256]{1,0:T(8,128)}, u32[]{:S(2)}) copy-start(f32[128,256]{1,0:T(8,128)} %get-tuple-element.14) | copy-start | bytes 393220
  7.2 18.7 %slice-start.1 = ((s8[6488064]{0:T(1024)(128)(4,1)}), s8[4194304]{0:T(1024)(128)(4,1)S(1)}, s32[]{:S(2)}) async-start(s8[6488064]{0:T(1024)(128)(4,1)} %bitcast.85), calls=%async_computation.2 | async-start | bytes 8388608
  10.0 43.3 %copy-start.2 = (f32[224,512]{1,0:T(8,128)}, f32[224,512]{1,0:T(8,128)S(1)}, u32[]{:S(2)}) copy-start(f32[224,512]{1,0:T(8,128)S(1)} %fusion.50) | copy-start | bytes 1376260
  10.1 5.6 %copy-start.3 = (bf16[2,64,4224]{2,1,0:T(8,128)(2,1)S(1)}, bf16[2,64,4224]{2,1,0:T(8,128)(2,1)}, u32[]{:S(2)}) copy-start(bf16[2,64,4224]{2,1,0:T(8,128)(2,1)} %param.6) | copy-start | bytes 3244036
  13.4 12.5 %collective-permute-start = (bf16[32,4224]{1,0:T(8,128)(2,1)S(1)}, bf16[32,4224]{1,0:T(8,128)(2,1)S(1)}, u32[]{:S(2)}, u32[]{:S(2)}) collective-permute-start(bf16[32,4224]{1,0:T(8,128)(2,1)S(1)} %get-tuple-element.18), channel_id=1, source_target_pairs={{1,0},{2,1},{3,2},{5,4},{6,5},{7,6},{9,8},{10,9},{11,10},{13,12},{... | collective-permute-start | bytes 811016 | tf_op jit(solution)/shard_map/ppermute | solution.py:71
  27.6 11.5 %collective-permute-start.1 = (bf16[32,4224]{1,0:T(8,128)(2,1)S(1)}, bf16[32,4224]{1,0:T(8,128)(2,1)S(1)}, u32[]{:S(2)}, u32[]{:S(2)}) collective-permute-start(bf16[32,4224]{1,0:T(8,128)(2,1)S(1)} %get-tuple-element.20), channel_id=1, source_target_pairs={{1,0},{2,1},{3,2},{5,4},{6,5},{7,6},{9,8},{10,9},{11,10},{13,12},{... | collective-permute-start | bytes 811016 | tf_op jit(solution)/shard_map/ppermute | solution.py:71
  40.8 11.7 %collective-permute-start.2 = (bf16[32,4224]{1,0:T(8,128)(2,1)S(1)}, bf16[32,4224]{1,0:T(8,128)(2,1)S(1)}, u32[]{:S(2)}, u32[]{:S(2)}) collective-permute-start(bf16[32,4224]{1,0:T(8,128)(2,1)S(1)} %get-tuple-element.22), channel_id=1, source_target_pairs={{1,0},{2,1},{3,2},{5,4},{6,5},{7,6},{9,8},{10,9},{11,10},{13,12},{... | collective-permute-start | bytes 811016 | tf_op jit(solution)/shard_map/ppermute | solution.py:71
  52.6 2.3 %copy-start.4 = (bf16[224,4224]{1,0:T(8,128)(2,1)}, bf16[224,4224]{1,0:T(8,128)(2,1)S(1)}, u32[]{:S(2)}) copy-start(bf16[224,4224]{1,0:T(8,128)(2,1)S(1)} %get-tuple-element.7) | copy-start | bytes 5677060
  54.9 1.2 copy-start.6
  56.2 15.1 %collective-permute-start.3 = (bf16[32,4224]{1,0:T(8,128)(2,1)}, bf16[32,4224]{1,0:T(8,128)(2,1)S(1)}, u32[]{:S(2)}, u32[]{:S(2)}) collective-permute-start(bf16[32,4224]{1,0:T(8,128)(2,1)} %get-tuple-element.24), channel_id=1, source_target_pairs={{1,0},{2,1},{3,2},{5,4},{6,5},{7,6},{9,8},{10,9},{11,10},{13,12},{... | collective-permute-start | bytes 811016 | tf_op jit(solution)/shard_map/ppermute | solution.py:71
  73.6 5.9 %copy-start.5 = (bf16[224,4224]{1,0:T(8,128)(2,1)S(1)}, bf16[224,4224]{1,0:T(8,128)(2,1)}, u32[]{:S(2)}) copy-start(bf16[224,4224]{1,0:T(8,128)(2,1)} %copy-done.4) | copy-start | bytes 5677060
  77.6 13.8 %collective-permute-start.4 = (bf16[32,4224]{1,0:T(8,128)(2,1)S(1)}, bf16[32,4224]{1,0:T(8,128)(2,1)S(1)}, u32[]{:S(2)}, u32[]{:S(2)}) collective-permute-start(bf16[32,4224]{1,0:T(8,128)(2,1)S(1)} %get-tuple-element.26), channel_id=1, source_target_pairs={{1,0},{2,1},{3,2},{5,4},{6,5},{7,6},{9,8},{10,9},{11,10},{13,12},{... | collective-permute-start | bytes 811016 | tf_op jit(solution)/shard_map/ppermute | solution.py:71
  93.8 17.3 %copy-start.9 = (f32[128,512]{1,0:T(8,128)S(1)}, f32[128,512]{1,0:T(8,128)}, u32[]{:S(2)}) copy-start(f32[128,512]{1,0:T(8,128)} %copy-done.8) | copy-start | bytes 786436
  97.7 13.3 %collective-permute-start.5 = (bf16[32,4224]{1,0:T(8,128)(2,1)S(1)}, bf16[32,4224]{1,0:T(8,128)(2,1)S(1)}, u32[]{:S(2)}, u32[]{:S(2)}) collective-permute-start(bf16[32,4224]{1,0:T(8,128)(2,1)S(1)} %get-tuple-element.28), channel_id=1, source_target_pairs={{1,0},{2,1},{3,2},{5,4},{6,5},{7,6},{9,8},{10,9},{11,10},{13,12},{... | collective-permute-start | bytes 811016 | tf_op jit(solution)/shard_map/ppermute | solution.py:71
  119.1 7.6 %copy-start.1 = (f32[96,2,44,128]{3,2,1,0:T(8,128)S(1)}, f32[96,2,44,128]{3,2,1,0:T(8,128)}, u32[]{:S(2)}) copy-start(f32[96,2,44,128]{3,2,1,0:T(8,128)} %reshape.69) | copy-start | bytes 12976132
  122.1 4.6 %collective-permute-start.6 = (bf16[96,44,128]{2,0,1:T(8,128)(2,1)S(1)}, bf16[96,44,128]{2,0,1:T(8,128)(2,1)S(1)}, u32[]{:S(2)}, u32[]{:S(2)}) collective-permute-start(bf16[96,44,128]{2,0,1:T(8,128)(2,1)S(1)} %copy.17), channel_id=1, source_target_pairs={{0,4},{4,0},{1,5},{5,1},{2,6},{6,2},{3,7},{7,3},{8,12},{12,8},{9,1... | collective-permute-start | bytes 3244040 | tf_op jit(solution)/shard_map/ppermute | solution.py:22
  128.3 80.6 %all-to-all-start = ((bf16[96,44,128]{2,1,0:T(8,128)(2,1)}), bf16[96,44,128]{2,1,0:T(8,128)(2,1)S(1)}, u32[]{:S(2)}, u32[]{:S(2)}) async-start(bf16[96,44,128]{2,1,0:T(8,128)(2,1)} %fusion.16), calls=%async_computation | async-start | bytes 2359296 | tf_op jit(solution)/shard_map/all_to_all | solution.py:24
  162.8 2.5 %copy-start.7 = (bf16[224,4224]{1,0:T(8,128)(2,1)S(1)}, bf16[224,4224]{1,0:T(8,128)(2,1)}, u32[]{:S(2)}) copy-start(bf16[224,4224]{1,0:T(8,128)(2,1)} %get-tuple-element.27) | copy-start | bytes 5677060
  168.4 40.7 %copy-start.11 = (f32[1,5632]{1,0:T(1,128)S(1)}, f32[1,5632]{1,0:T(1,128)}, u32[]{:S(2)}) copy-start(f32[1,5632]{1,0:T(1,128)} %param.9) | copy-start | bytes 67588
  168.4 40.7 %copy-start.12 = (f32[1,5632]{1,0:T(1,128)S(1)}, f32[1,5632]{1,0:T(1,128)}, u32[]{:S(2)}) copy-start(f32[1,5632]{1,0:T(1,128)} %param.8) | copy-start | bytes 67588

commit v2 on v1

v2 whole, which is shorter than its diff:
```python
import jax
import jax.numpy as jnp
from jax import lax
from jax.sharding import Mesh, PartitionSpec as P

CHUNKS = 4
DP = ("x", "yl", "z", "core")
SIDE = ("x", "core")
F32 = jnp.float32
BF16 = jnp.bfloat16


def rows_dot(left, right):
    return lax.dot_general(left, right, (((0,), (0,)), ((), ())), preferred_element_type=F32)


def cols_dot(left, right):
    return lax.dot_general(left, right, (((1,), (1,)), ((), ())), preferred_element_type=F32)


def spread(value, places):
    shape = (value.shape[1], places * 2)
    have = lax.broadcasted_iota(jnp.int32, shape, 0)
    col = lax.broadcasted_iota(jnp.int32, shape, 1)
    place = col // 2
    want = (place // 3) * 4 + place % 3 + col % 2
    return jnp.dot(value, (have == want).astype(BF16), preferred_element_type=F32).astype(BF16)


def to_side(rows):
    count = lax.axis_size(SIDE)
    parts = rows.reshape(rows.shape[0], count, -1).transpose(1, 0, 2)
    parts = lax.all_to_all(parts, SIDE, 0, 0, tiled=True)
    return parts.reshape(-1, parts.shape[2])


def step(acts, out_grad, params, moment, second):
    sections = lax.axis_size("pipe")
    section = lax.axis_index("pipe")
    places = lax.axis_size(DP)
    side = lax.axis_size(SIDE)
    width = acts.shape[-1]
    inputs = acts.reshape(-1, width)
    top = out_grad.reshape(-1, width)
    tokens = inputs.shape[0]
    rows = tokens // CHUNKS
    lead = sections - 1
    ticks = CHUNKS + lead
    block = params.shape[1] // 3
    weights_in = params[0, : 2 * block]
    weights_down = params[0, 2 * block :]
    gate_up = cols_dot(inputs, weights_in)
    gate = gate_up[:, :block]
    up = gate_up[:, block:]
    sg = jax.nn.sigmoid(gate)
    activated = gate * sg
    factors = jnp.concatenate([up * sg * (1.0 + gate * (1.0 - sg)), activated], axis=1)
    hidden = (activated * up).astype(BF16)
    pad = jnp.zeros((lead * rows, 2 * block), F32)
    factors = lax.dynamic_slice(
        jnp.concatenate([pad, factors, pad], axis=0),
        (section * rows, 0),
        (ticks * rows, 2 * block),
    )
    down = [(s, s - 1) for s in range(1, sections)]
    most = tokens - rows

    def own(values, chunk, among=sections):
        value = values[chunk]
        for behind in range(1, among):
            value = jnp.where(section == lead - behind, values[chunk + behind], value)
        return value

    moved = []
    grads = []
    passes = []
    for tick in range(ticks):
        grad = jnp.zeros((rows, width), BF16) if tick == 0 else moved[tick - 1]
        if tick < CHUNKS:
            grad = jnp.where(section == lead, top[tick * rows : (tick + 1) * rows], grad)
        d_hidden = cols_dot(grad, weights_down)
        part = factors[tick * rows : (tick + 1) * rows]
        d_gate_up = (jnp.concatenate([d_hidden, d_hidden], axis=1) * part).astype(BF16)
        passed = grad.astype(F32) + jnp.dot(d_gate_up, weights_in, preferred_element_type=F32)
        passed = passed.astype(BF16)
        grads.append(grad)
        passes.append(passed)
        if tick + 1 < ticks:
            moved.append(lax.ppermute(passed, "pipe", down))
        if tick == 0:
            hidden, _ = lax.optimization_barrier((hidden, passed))
            copies = jnp.broadcast_to(hidden[None], (side,) + hidden.shape)
            hidden = lax.all_to_all(copies, SIDE, 0, 0, tiled=True)
            hidden = spread(hidden.reshape(-1, block), places).reshape(side, tokens, -1)
        if tick + 2 == ticks:
            arrived = jnp.concatenate([own(grads, chunk) for chunk in range(CHUNKS - 1)], axis=0)
            last = own(grads, CHUNKS - 1, lead)
            arrived, last = lax.optimization_barrier((arrived, last))
            terms = rows_dot(hidden[:, :most].reshape(side * most, -1), to_side(arrived))
    arrived = jnp.where(section == 0, grads[-1], last)
    terms = terms + rows_dot(hidden[:, most:].reshape(side * rows, -1), to_side(arrived))
    in_grads = jnp.concatenate([own(passes, chunk) for chunk in range(CHUNKS)], axis=0)

    terms = terms.astype(BF16).reshape(places, 2, -1)
    terms = lax.all_to_all(terms, DP, 0, 0, tiled=True)
    sizes = tuple(lax.axis_size(name) for name in DP)
    summed = jnp.sum(terms.astype(F32).reshape(sizes + terms.shape[1:]), axis=(1, 2))
    summed = summed.transpose(2, 0, 1, 3).reshape(-1)
    start = lax.rem(lax.axis_index(DP), 3) * (width // 3)
    summed = lax.dynamic_slice(summed, (start,), (moment.shape[1],))

    gradient = summed * float(tokens * places) ** (-0.5)
    new_moment = 0.9 * moment[0] + 0.1 * gradient
    new_second = 0.999 * second[0] + 0.001 * gradient * gradient
    update = new_moment / (1.0 - 0.9**10) / (jnp.sqrt(new_second / (1.0 - 0.999**10)) + 1e-08)
    return (in_grads.reshape(acts.shape), new_moment[None], new_second[None], update[None])


def solution(mesh):
    fine = Mesh(mesh.devices.reshape(4, 2, 12, 2, 4), DP + ("pipe",))
    placed = (
        P("pipe", None, DP, None),
        P(None, DP, None),
        P("pipe", None, None),
        P("pipe", DP),
        P("pipe", DP),
    )
    return jax.shard_map(
        step,
        mesh=fine,
        in_specs=placed,
        out_specs=(P("pipe", None, DP, None), P("pipe", DP), P("pipe", DP), P("pipe", DP)),
        check_vma=False,
    )
```

time: 210 us -> 191 us (0.910)
  the two profiles are of different devices: /device:TPU:24 before, /device:TPU:45 now
where the time goes in v2:
time: 191 us; the launch traced here: 190 us
  starting transfers between devices  80.9 us (42%)
  waiting for transfers between devices  52.9 us (28%)
  matrix products  40.2 us (21%)
  local copies, waits for them, and re-layouts  9.73 us (5%)
  other arithmetic  5.09 us (3%)
    all_to_all x2, starting transfers between devices, to_side(): parts = lax.all_to_all(parts, SIDE, 0, 0, tiled=True)  23.8 us
    ppermute x6, waiting for transfers between devices, step(): moved.append(lax.ppermute(passed, 'pipe', down))  23.3 us
    all_to_all x1, starting transfers between devices, step(): terms = lax.all_to_all(terms, DP, 0, 0, tiled=True)  22.8 us
    ppermute x6, starting transfers between devices, step(): moved.append(lax.ppermute(passed, 'pipe', down))  22.8 us
    dot_general x7, matrix products, step(): jnp.dot(d_gate_up, weights_in, preferred_element_type=F32)  19.5 us
    dot_general x8, matrix products, cols_dot(): lax.dot_general(left, right, (((1,), (1,)), ((), ())), preferred_element_...  17.3 us
    all_to_all x1, waiting for transfers between devices, step(): terms = lax.all_to_all(terms, DP, 0, 0, tiled=True)  17.1 us
    all_to_all x2, waiting for transfers between devices, to_side(): parts = lax.all_to_all(parts, SIDE, 0, 0, tiled=True)  12.4 us
  transfers between devices with their start and end apart: 10, of which 7 were waited for; matrix products, arithmetic and copies ran while one was open for 13% of the time, Pallas kernels for 0%

profile of v2, /device:TPU:45, one launch (start us, length us, event | category | flops | bytes accessed | tf_op | source)
XLA Modules:
  0.0 190.0 jit_solution(4321307975252918263)
XLA Ops:
  0.7 1.2 copy-done
  1.9 3.9 %fusion.14 = f32[128,512]{1,0:T(8,128)S(1)} fusion(bf16[128,4224]{1,0:T(8,128)(2,1)S(1)} %bitcast.78, bf16[1,768,4224]{2,1,0:T(8,128)(2,1)} %param.7), kind=kOutput, calls=%fused_computation.15 | convolution fusion | flops 553648128 | bytes 5668864 | tf_op jit(solution)/shard_map/dot_general | solution.py:18
  6.5 2.6 %fusion.28 = f32[32,256]{1,0:T(8,128)S(1)} fusion(bf16[1,768,4224]{2,1,0:T(8,128)(2,1)} %param.7, bf16[128,4224]{1,0:T(8,128)(2,1)} %bitcast.82, pred[]{:T(512)S(6)} %eq.14), kind=kOutput, calls=%fused_computation.29 | convolution fusion | flops 69341184 | bytes 2465793 | tf_op jit(solution)/shard_map/dot_general | solution.py:18
  10.2 3.3 %fusion = bf16[32,4224]{1,0:T(8,128)(2,1)S(1)} fusion(bf16[1,768,4224]{2,1,0:T(8,128)(2,1)} %param.7, bf16[128,4224]{1,0:T(8,128)(2,1)} %bitcast.83, pred[]{:T(512)S(6)} %eq.14, f32[224,512]{1,0:T(8,128)S(1)} %fusion.53, f32[32,256]{1,0:T(8,128)S(1)} %fusion.28), kind=kOutput, calls=%fused_computation.1 | convolution fusion | flops 139001856 | bytes 4964353 | tf_op jit(solution)/shard_map/dot_general | solution.py:84
  13.5 2.9 %collective-permute-start = (bf16[32,4224]{1,0:T(8,128)(2,1)S(1)}, bf16[32,4224]{1,0:T(8,128)(2,1)S(1)}, u32[]{:S(2)}, u32[]{:S(2)}) collective-permute-start(bf16[32,4224]{1,0:T(8,128)(2,1)S(1)} %fusion), channel_id=1, source_target_pairs={{1,0},{2,1},{3,2},{5,4},{6,5},{7,6},{9,8},{10,9},{11,10},{13,12},{... | collective-permute-start | bytes 811016 | tf_op jit(solution)/shard_map/ppermute | solution.py:89
  16.4 7.4 %collective-permute-done = bf16[32,4224]{1,0:T(8,128)(2,1)S(1)} collective-permute-done((bf16[32,4224]{1,0:T(8,128)(2,1)S(1)}, bf16[32,4224]{1,0:T(8,128)(2,1)S(1)}, u32[]{:S(2)}, u32[]{:S(2)}) %collective-permute-start) | collective-permute-done | bytes 270368 | tf_op jit(solution)/shard_map/ppermute | solution.py:89
  25.5 4.3 %collective-permute-start.1 = (bf16[32,4224]{1,0:T(8,128)(2,1)S(1)}, bf16[32,4224]{1,0:T(8,128)(2,1)S(1)}, u32[]{:S(2)}, u32[]{:S(2)}) collective-permute-start(bf16[32,4224]{1,0:T(8,128)(2,1)S(1)} %add_convert_fusion.5), channel_id=1, source_target_pairs={{1,0},{2,1},{3,2},{5,4},{6,5},{7,6},{9,8},{10,9},{11,10},{13,12},{... | collective-permute-start | bytes 811016 | tf_op jit(solution)/shard_map/ppermute | solution.py:89
  29.8 4.9 %collective-permute-done.1 = bf16[32,4224]{1,0:T(8,128)(2,1)S(1)} collective-permute-done((bf16[32,4224]{1,0:T(8,128)(2,1)S(1)}, bf16[32,4224]{1,0:T(8,128)(2,1)S(1)}, u32[]{:S(2)}, u32[]{:S(2)}) %collective-permute-start.1) | collective-permute-done | bytes 270368 | tf_op jit(solution)/shard_map/ppermute | solution.py:89
  35.6 1.6 add_convert_fusion.4
  37.1 5.6 %collective-permute-start.2 = (bf16[32,4224]{1,0:T(8,128)(2,1)}, bf16[32,4224]{1,0:T(8,128)(2,1)S(1)}, u32[]{:S(2)}, u32[]{:S(2)}) collective-permute-start(bf16[32,4224]{1,0:T(8,128)(2,1)} %add_convert_fusion.4), channel_id=1, source_target_pairs={{1,0},{2,1},{3,2},{5,4},{6,5},{7,6},{9,8},{10,9},{11,10},{13,12},{... | collective-permute-start | bytes 811016 | tf_op jit(solution)/shard_map/ppermute | solution.py:89
  42.8 3.7 %collective-permute-done.2 = bf16[32,4224]{1,0:T(8,128)(2,1)S(1)} collective-permute-done((bf16[32,4224]{1,0:T(8,128)(2,1)}, bf16[32,4224]{1,0:T(8,128)(2,1)S(1)}, u32[]{:S(2)}, u32[]{:S(2)}) %collective-permute-start.2) | collective-permute-done | bytes 270368 | tf_op jit(solution)/shard_map/ppermute | solution.py:89
  47.7 2.3 %fusion.22 = f32[32,256]{1,0:T(8,128)S(1)} fusion(bf16[32,4224]{1,0:T(8,128)(2,1)S(1)} %get-tuple-element.14, bf16[1,768,4224]{2,1,0:T(8,128)(2,1)} %param.7), kind=kOutput, calls=%fused_computation.23 | convolution fusion | flops 69206016 | bytes 2465792 | tf_op jit(solution)/shard_map/dot_general | solution.py:18
  50.0 3.1 %add_convert_fusion.3 = bf16[32,4224]{1,0:T(8,128)(2,1)S(1)} fusion(bf16[32,4224]{1,0:T(8,128)(2,1)S(1)} %get-tuple-element.14, bf16[1,768,4224]{2,1,0:T(8,128)(2,1)} %param.7, f32[224,512]{1,0:T(8,128)} %copy-done.5, f32[32,256]{1,0:T(8,128)S(1)} %fusion.22), kind=kOutput, calls=%fused_computation.71 | convolution fusion | flops 138866688 | bytes 4964352 | tf_op jit(solution)/shard_map/dot_general | solution.py:84
  53.1 6.1 %collective-permute-start.3 = (bf16[32,4224]{1,0:T(8,128)(2,1)S(1)}, bf16[32,4224]{1,0:T(8,128)(2,1)S(1)}, u32[]{:S(2)}, u32[]{:S(2)}) collective-permute-start(bf16[32,4224]{1,0:T(8,128)(2,1)S(1)} %add_convert_fusion.3), channel_id=1, source_target_pairs={{1,0},{2,1},{3,2},{5,4},{6,5},{7,6},{9,8},{10,9},{11,10},{13,12},{... | collective-permute-start | bytes 811016 | tf_op jit(solution)/shard_map/ppermute | solution.py:89
  60.1 11.4 %all-to-all-start = ((bf16[8,128,256]{2,1,0:T(8,128)(2,1)}), bf16[8,128,256]{2,1,0:T(8,128)(2,1)}, u32[]{:S(2)}, u32[]{:S(2)}) async-start(bf16[8,128,256]{2,1,0:T(8,128)(2,1)} %broadcast_in_dim.23), calls=%async_computation | async-start | bytes 1048576 | tf_op jit(solution)/shard_map/all_to_all | solution.py:93
  71.6 2.3 %fusion.20 = f32[32,256]{1,0:T(8,128)S(1)} fusion(bf16[32,4224]{1,0:T(8,128)(2,1)S(1)} %collective-permute-done.3, bf16[1,768,4224]{2,1,0:T(8,128)(2,1)} %param.7), kind=kOutput, calls=%fused_computation.21 | convolution fusion | flops 69206016 | bytes 2465792 | tf_op jit(solution)/shard_map/dot_general | solution.py:18
  74.0 3.2 %add_convert_fusion.2 = bf16[32,4224]{1,0:T(8,128)(2,1)S(1)} fusion(bf16[32,4224]{1,0:T(8,128)(2,1)S(1)} %collective-permute-done.3, bf16[1,768,4224]{2,1,0:T(8,128)(2,1)} %param.7, f32[224,512]{1,0:T(8,128)} %copy-done.5, f32[32,256]{1,0:T(8,128)S(1)} %fusion.20), kind=kOutput, calls=%fused_computation.70 | convolution fusion | flops 138866688 | bytes 4964352 | tf_op jit(solution)/shard_map/dot_general | solution.py:84
  77.2 1.9 %collective-permute-start.4 = (bf16[32,4224]{1,0:T(8,128)(2,1)S(1)}, bf16[32,4224]{1,0:T(8,128)(2,1)S(1)}, u32[]{:S(2)}, u32[]{:S(2)}) collective-permute-start(bf16[32,4224]{1,0:T(8,128)(2,1)S(1)} %add_convert_fusion.2), channel_id=1, source_target_pairs={{1,0},{2,1},{3,2},{5,4},{6,5},{7,6},{9,8},{10,9},{11,10},{13,12},{... | collective-permute-start | bytes 811016 | tf_op jit(solution)/shard_map/ppermute | solution.py:89
  79.3 7.4 %collective-permute-done.4 = bf16[32,4224]{1,0:T(8,128)(2,1)S(1)} collective-permute-done((bf16[32,4224]{1,0:T(8,128)(2,1)S(1)}, bf16[32,4224]{1,0:T(8,128)(2,1)S(1)}, u32[]{:S(2)}, u32[]{:S(2)}) %collective-permute-start.4) | collective-permute-done | bytes 270368 | tf_op jit(solution)/shard_map/ppermute | solution.py:89
  86.6 2.3 %fusion.18 = f32[32,256]{1,0:T(8,128)S(1)} fusion(bf16[32,4224]{1,0:T(8,128)(2,1)S(1)} %collective-permute-done.4, bf16[1,768,4224]{2,1,0:T(8,128)(2,1)} %param.7), kind=kOutput, calls=%fused_computation.19 | convolution fusion | flops 69206016 | bytes 2465792 | tf_op jit(solution)/shard_map/dot_general | solution.py:18
  89.0 4.1 %select_select_fusion.6 = (bf16[32,4224]{1,0:T(8,128)(2,1)}, bf16[32,4224]{1,0:T(8,128)(2,1)}, bf16[32,4224]{1,0:T(8,128)(2,1)}, bf16[32,4224]{1,0:T(8,128)(2,1)}) fusion(bf16[32,4224]{1,0:T(8,128)(2,1)S(1)} %add_convert_fusion.3, bf16[32,4224]{1,0:T(8,128)(2,1)} %add_convert_fusion.4, bf16[32,4224]{1,0:T(8,128)(2,1)S(1)} %copy-done.10, ...), kind=kOutput, calls=%fused_computation.96 | convolution fusion | flops 140083200 | bytes 7127043 | tf_op jit(solution)/shard_map/dot_general | solution.py:84
  93.2 1.9 %collective-permute-start.5 = (bf16[32,4224]{1,0:T(8,128)(2,1)}, bf16[32,4224]{1,0:T(8,128)(2,1)}, u32[]{:S(2)}, u32[]{:S(2)}) collective-permute-start(bf16[32,4224]{1,0:T(8,128)(2,1)} %get-tuple-element.24), channel_id=1, source_target_pairs={{1,0},{2,1},{3,2},{5,4},{6,5},{7,6},{9,8},{10,9},{11,10},{13,12},{... | collective-permute-start | bytes 811016 | tf_op jit(solution)/shard_map/ppermute | solution.py:89
  97.6 17.2 %all-to-all-start.1 = ((bf16[8,96,528]{2,1,0:T(8,128)(2,1)}), bf16[8,96,528]{2,1,0:T(8,128)(2,1)S(1)}, u32[]{:S(2)}, u32[]{:S(2)}) async-start(bf16[8,96,528]{2,1,0:T(8,128)(2,1)} %bitcast.76), calls=%async_computation.1 | async-start | bytes 1966080 | tf_op jit(solution)/shard_map/all_to_all | solution.py:33
  115.9 10.7 %all-to-all-done.1 = bf16[8,96,528]{2,1,0:T(8,128)(2,1)S(1)} async-done(((bf16[8,96,528]{2,1,0:T(8,128)(2,1)}), bf16[8,96,528]{2,1,0:T(8,128)(2,1)S(1)}, u32[]{:S(2)}, u32[]{:S(2)}) %all-to-all-start.1) | async-done | bytes 811040 | tf_op jit(solution)/shard_map/all_to_all | solution.py:33
  126.6 6.7 %all-to-all-start.2 = ((bf16[8,32,528]{2,1,0:T(8,128)(2,1)}), bf16[8,32,528]{2,1,0:T(8,128)(2,1)S(1)}, u32[]{:S(2)}, u32[]{:S(2)}) async-start(bf16[8,32,528]{2,1,0:T(8,128)(2,1)} %bitcast.77), calls=%async_computation.2 | async-start | bytes 655360 | tf_op jit(solution)/shard_map/all_to_all | solution.py:33
  133.3 1.5 convolution_convert_fusion
  136.4 1.8 all-to-all-done.2
  138.1 1.3 fusion.31
  140.6 22.8 %all-to-all-start.3 = ((bf16[192,2,528]{2,1,0:T(2,128)(2,1)}), bf16[192,2,528]{2,1,0:T(2,128)(2,1)S(1)}, u32[]{:S(2)}, u32[]{:S(2)}) async-start(bf16[192,2,528]{2,1,0:T(2,128)(2,1)} %reshape.57), calls=%async_computation.3 | async-start | bytes 983040 | tf_op jit(solution)/shard_map/all_to_all | solution.py:105
  163.5 2.5 %fusion.16 = f32[32,256]{1,0:T(8,128)S(1)} fusion(bf16[32,4224]{1,0:T(8,128)(2,1)} %collective-permute-done.5, bf16[1,768,4224]{2,1,0:T(8,128)(2,1)} %param.7), kind=kOutput, calls=%fused_computation.17 | convolution fusion | flops 69206016 | bytes 2465792 | tf_op jit(solution)/shard_map/dot_general | solution.py:18
  166.0 3.3 %fusion.66 = bf16[32,4224]{1,0:T(8,128)(2,1)S(1)} fusion(bf16[32,4224]{1,0:T(8,128)(2,1)} %collective-permute-done.5, bf16[32,4224]{1,0:T(8,128)(2,1)} %get-tuple-element.24, bf16[32,4224]{1,0:T(8,128)(2,1)} %copy-done.8, bf16[32,4224]{1,0:T(8,128)(2,1)S(1)} %add_convert_fusion.3, pred[]{:T(512)S(6)} %eq.16, pred[]{:T(512)S(6)} %eq.15, pred[]{:T(512)S(6)} %eq.13, ...), kind=kOutput, calls=%fused_computation.85 | convolution fusion | flops 139272192 | bytes 5775363 | tf_op jit(solution)/shard_map/dot_general | solution.py:84
  170.4 17.1 %all-to-all-done.3 = bf16[192,2,528]{2,1,0:T(2,128)(2,1)S(1)} async-done(((bf16[192,2,528]{2,1,0:T(2,128)(2,1)}), bf16[192,2,528]{2,1,0:T(2,128)(2,1)S(1)}, u32[]{:S(2)}, u32[]{:S(2)}) %all-to-all-start.3) | async-done | bytes 405536 | tf_op jit(solution)/shard_map/all_to_all | solution.py:105
  (77 shorter events, 16.5 us)
Async XLA Ops:
  0.6 1.2 copy-start
  1.9 21.9 %slice-start = ((s8[6488064]{0:T(1024)(128)(4,1)}), s8[2293760]{0:T(1024)(128)(4,1)S(1)}, s32[]{:S(2)}) async-start(s8[6488064]{0:T(1024)(128)(4,1)} %bitcast.79), calls=%async_computation.4 | async-start | bytes 4587520
  6.5 17.2 %copy-start.6 = (bf16[2,64,4224]{2,1,0:T(8,128)(2,1)S(1)}, bf16[2,64,4224]{2,1,0:T(8,128)(2,1)}, u32[]{:S(2)}) copy-start(bf16[2,64,4224]{2,1,0:T(8,128)(2,1)} %param.6) | copy-start | bytes 3244036
  6.5 17.3 %slice-start.1 = ((s8[6488064]{0:T(1024)(128)(4,1)}), s8[4194304]{0:T(1024)(128)(4,1)S(1)}, s32[]{:S(2)}) async-start(s8[6488064]{0:T(1024)(128)(4,1)} %bitcast.79), calls=%async_computation.5 | async-start | bytes 8388608
  10.2 25.3 %copy-start.5 = (f32[224,512]{1,0:T(8,128)}, f32[224,512]{1,0:T(8,128)S(1)}, u32[]{:S(2)}) copy-start(f32[224,512]{1,0:T(8,128)S(1)} %fusion.53) | copy-start | bytes 1376260
  13.5 2.9 %copy-start.17 = (bf16[32,4224]{1,0:T(8,128)(2,1)}, bf16[32,4224]{1,0:T(8,128)(2,1)S(1)}, u32[]{:S(2)}) copy-start(bf16[32,4224]{1,0:T(8,128)(2,1)S(1)} %fusion) | copy-start | bytes 811012
  13.5 10.2 %collective-permute-start = (bf16[32,4224]{1,0:T(8,128)(2,1)S(1)}, bf16[32,4224]{1,0:T(8,128)(2,1)S(1)}, u32[]{:S(2)}, u32[]{:S(2)}) collective-permute-start(bf16[32,4224]{1,0:T(8,128)(2,1)S(1)} %fusion), channel_id=1, source_target_pairs={{1,0},{2,1},{3,2},{5,4},{6,5},{7,6},{9,8},{10,9},{11,10},{13,12},{... | collective-permute-start | bytes 811016 | tf_op jit(solution)/shard_map/ppermute | solution.py:89
  23.8 11.7 %copy-start.1 = (bf16[32,4224]{1,0:T(8,128)(2,1)}, bf16[32,4224]{1,0:T(8,128)(2,1)S(1)}, u32[]{:S(2)}) copy-start(bf16[32,4224]{1,0:T(8,128)(2,1)S(1)} %slice_select_fusion.1) | copy-start | bytes 811012
  25.5 4.3 %copy-start.9 = (bf16[32,4224]{1,0:T(8,128)(2,1)}, bf16[32,4224]{1,0:T(8,128)(2,1)S(1)}, u32[]{:S(2)}) copy-start(bf16[32,4224]{1,0:T(8,128)(2,1)S(1)} %add_convert_fusion.5) | copy-start | bytes 811012
  25.5 9.3 %collective-permute-start.1 = (bf16[32,4224]{1,0:T(8,128)(2,1)S(1)}, bf16[32,4224]{1,0:T(8,128)(2,1)S(1)}, u32[]{:S(2)}, u32[]{:S(2)}) collective-permute-start(bf16[32,4224]{1,0:T(8,128)(2,1)S(1)} %add_convert_fusion.5), channel_id=1, source_target_pairs={{1,0},{2,1},{3,2},{5,4},{6,5},{7,6},{9,8},{10,9},{11,10},{13,12},{... | collective-permute-start | bytes 811016 | tf_op jit(solution)/shard_map/ppermute | solution.py:89
  34.8 2.3 %copy-start.3 = (bf16[32,4224]{1,0:T(8,128)(2,1)}, bf16[32,4224]{1,0:T(8,128)(2,1)S(1)}, u32[]{:S(2)}) copy-start(bf16[32,4224]{1,0:T(8,128)(2,1)S(1)} %slice_select_fusion.2) | copy-start | bytes 811012
  37.1 9.3 %collective-permute-start.2 = (bf16[32,4224]{1,0:T(8,128)(2,1)}, bf16[32,4224]{1,0:T(8,128)(2,1)S(1)}, u32[]{:S(2)}, u32[]{:S(2)}) collective-permute-start(bf16[32,4224]{1,0:T(8,128)(2,1)} %add_convert_fusion.4), channel_id=1, source_target_pairs={{1,0},{2,1},{3,2},{5,4},{6,5},{7,6},{9,8},{10,9},{11,10},{13,12},{... | collective-permute-start | bytes 811016 | tf_op jit(solution)/shard_map/ppermute | solution.py:89
  42.8 16.5 %copy-start.14 = (bf16[128,256]{1,0:T(8,128)(2,1)S(1)}, bf16[128,256]{1,0:T(8,128)(2,1)}, u32[]{:S(2)}) copy-start(bf16[128,256]{1,0:T(8,128)(2,1)} %get-tuple-element.7) | copy-start | bytes 196612
  53.1 18.5 %collective-permute-start.3 = (bf16[32,4224]{1,0:T(8,128)(2,1)S(1)}, bf16[32,4224]{1,0:T(8,128)(2,1)S(1)}, u32[]{:S(2)}, u32[]{:S(2)}) collective-permute-start(bf16[32,4224]{1,0:T(8,128)(2,1)S(1)} %add_convert_fusion.3), channel_id=1, source_target_pairs={{1,0},{2,1},{3,2},{5,4},{6,5},{7,6},{9,8},{10,9},{11,10},{13,12},{... | collective-permute-start | bytes 811016 | tf_op jit(solution)/shard_map/ppermute | solution.py:89
  60.1 19.0 %copy-start.15 = (f32[1,5632]{1,0:T(1,128)S(1)}, f32[1,5632]{1,0:T(1,128)}, u32[]{:S(2)}) copy-start(f32[1,5632]{1,0:T(1,128)} %param.9) | copy-start | bytes 67588
  60.1 19.0 %copy-start.16 = (f32[1,5632]{1,0:T(1,128)S(1)}, f32[1,5632]{1,0:T(1,128)}, u32[]{:S(2)}) copy-start(f32[1,5632]{1,0:T(1,128)} %param.8) | copy-start | bytes 67588
  60.1 37.4 %all-to-all-start = ((bf16[8,128,256]{2,1,0:T(8,128)(2,1)}), bf16[8,128,256]{2,1,0:T(8,128)(2,1)}, u32[]{:S(2)}, u32[]{:S(2)}) async-start(bf16[8,128,256]{2,1,0:T(8,128)(2,1)} %broadcast_in_dim.23), calls=%async_computation | async-start | bytes 1048576 | tf_op jit(solution)/shard_map/all_to_all | solution.py:93
  73.9 15.0 %copy-start.10 = (bf16[32,4224]{1,0:T(8,128)(2,1)S(1)}, bf16[32,4224]{1,0:T(8,128)(2,1)}, u32[]{:S(2)}) copy-start(bf16[32,4224]{1,0:T(8,128)(2,1)} %copy-done.9) | copy-start | bytes 811012
  73.9 15.1 %copy-start.18 = (bf16[32,4224]{1,0:T(8,128)(2,1)S(1)}, bf16[32,4224]{1,0:T(8,128)(2,1)}, u32[]{:S(2)}) copy-start(bf16[32,4224]{1,0:T(8,128)(2,1)} %copy-done.17) | copy-start | bytes 811012
  77.1 16.0 %copy-start.8 = (bf16[32,4224]{1,0:T(8,128)(2,1)}, bf16[32,4224]{1,0:T(8,128)(2,1)S(1)}, u32[]{:S(2)}) copy-start(bf16[32,4224]{1,0:T(8,128)(2,1)S(1)} %add_convert_fusion.2) | copy-start | bytes 811012
  77.2 9.5 %collective-permute-start.4 = (bf16[32,4224]{1,0:T(8,128)(2,1)S(1)}, bf16[32,4224]{1,0:T(8,128)(2,1)S(1)}, u32[]{:S(2)}, u32[]{:S(2)}) collective-permute-start(bf16[32,4224]{1,0:T(8,128)(2,1)S(1)} %add_convert_fusion.2), channel_id=1, source_target_pairs={{1,0},{2,1},{3,2},{5,4},{6,5},{7,6},{9,8},{10,9},{11,10},{13,12},{... | collective-permute-start | bytes 811016 | tf_op jit(solution)/shard_map/ppermute | solution.py:89
  89.0 6.1 %copy-start.2 = (bf16[32,4224]{1,0:T(8,128)(2,1)S(1)}, bf16[32,4224]{1,0:T(8,128)(2,1)}, u32[]{:S(2)}) copy-start(bf16[32,4224]{1,0:T(8,128)(2,1)} %copy-done.1) | copy-start | bytes 811012
  89.0 6.1 %copy-start.4 = (bf16[32,4224]{1,0:T(8,128)(2,1)S(1)}, bf16[32,4224]{1,0:T(8,128)(2,1)}, u32[]{:S(2)}) copy-start(bf16[32,4224]{1,0:T(8,128)(2,1)} %copy-done.3) | copy-start | bytes 811012
  93.2 21.5 %collective-permute-start.5 = (bf16[32,4224]{1,0:T(8,128)(2,1)}, bf16[32,4224]{1,0:T(8,128)(2,1)}, u32[]{:S(2)}, u32[]{:S(2)}) collective-permute-start(bf16[32,4224]{1,0:T(8,128)(2,1)} %get-tuple-element.24), channel_id=1, source_target_pairs={{1,0},{2,1},{3,2},{5,4},{6,5},{7,6},{9,8},{10,9},{11,10},{13,12},{... | collective-permute-start | bytes 811016 | tf_op jit(solution)/shard_map/ppermute | solution.py:89
  97.6 29.1 %all-to-all-start.1 = ((bf16[8,96,528]{2,1,0:T(8,128)(2,1)}), bf16[8,96,528]{2,1,0:T(8,128)(2,1)S(1)}, u32[]{:S(2)}, u32[]{:S(2)}) async-start(bf16[8,96,528]{2,1,0:T(8,128)(2,1)} %bitcast.76), calls=%async_computation.1 | async-start | bytes 1966080 | tf_op jit(solution)/shard_map/all_to_all | solution.py:33
  126.6 11.5 %all-to-all-start.2 = ((bf16[8,32,528]{2,1,0:T(8,128)(2,1)}), bf16[8,32,528]{2,1,0:T(8,128)(2,1)S(1)}, u32[]{:S(2)}, u32[]{:S(2)}) async-start(bf16[8,32,528]{2,1,0:T(8,128)(2,1)} %bitcast.77), calls=%async_computation.2 | async-start | bytes 655360 | tf_op jit(solution)/shard_map/all_to_all | solution.py:33
  134.8 0.9 copy-start.7
  140.6 46.8 %all-to-all-start.3 = ((bf16[192,2,528]{2,1,0:T(2,128)(2,1)}), bf16[192,2,528]{2,1,0:T(2,128)(2,1)S(1)}, u32[]{:S(2)}, u32[]{:S(2)}) async-start(bf16[192,2,528]{2,1,0:T(2,128)(2,1)} %reshape.57), calls=%async_computation.3 | async-start | bytes 983040 | tf_op jit(solution)/shard_map/all_to_all | solution.py:105
  163.5 5.8 %copy-start.11 = (bf16[32,4224]{1,0:T(8,128)(2,1)S(1)}, bf16[32,4224]{1,0:T(8,128)(2,1)}, u32[]{:S(2)}) copy-start(bf16[32,4224]{1,0:T(8,128)(2,1)} %get-tuple-element.18) | copy-start | bytes 811012
  163.5 5.8 %copy-start.12 = (bf16[32,4224]{1,0:T(8,128)(2,1)S(1)}, bf16[32,4224]{1,0:T(8,128)(2,1)}, u32[]{:S(2)}) copy-start(bf16[32,4224]{1,0:T(8,128)(2,1)} %get-tuple-element.19) | copy-start | bytes 811012
  163.5 5.8 %copy-start.13 = (bf16[32,4224]{1,0:T(8,128)(2,1)S(1)}, bf16[32,4224]{1,0:T(8,128)(2,1)}, u32[]{:S(2)}) copy-start(bf16[32,4224]{1,0:T(8,128)(2,1)} %get-tuple-element.20) | copy-start | bytes 811012

commit v3 on v2

--- a/solution.py
+++ b/solution.py
@@ -40,6 +40,12 @@
     places = lax.axis_size(DP)
     side = lax.axis_size(SIDE)
     width = acts.shape[-1]
+    first_chunk = (section * (acts.shape[1] * acts.shape[2] // CHUNKS)).astype(jnp.uint32)
+    third = (lax.rem(lax.axis_index(DP), 3) * (width // 3)).astype(jnp.uint32)
+    is_section = [section == at for at in range(sections)]
+    acts, first_chunk, third, is_section = lax.optimization_barrier(
+        (acts, first_chunk, third, is_section)
+    )
     inputs = acts.reshape(-1, width)
     top = out_grad.reshape(-1, width)
     tokens = inputs.shape[0]
@@ -59,16 +65,20 @@
     pad = jnp.zeros((lead * rows, 2 * block), F32)
     factors = lax.dynamic_slice(
         jnp.concatenate([pad, factors, pad], axis=0),
-        (section * rows, 0),
+        (first_chunk, jnp.uint32(0)),
         (ticks * rows, 2 * block),
     )
+    copies = jnp.broadcast_to(hidden[None], (side,) + hidden.shape)
+    hidden = lax.all_to_all(copies, SIDE, 0, 0, tiled=True)
+    hidden = spread(hidden.reshape(-1, block), places).reshape(side, tokens, -1)
     down = [(s, s - 1) for s in range(1, sections)]
-    most = tokens - rows
+    early = CHUNKS - 2
+    cuts = (0, early * rows, (early + 1) * rows, tokens)
 
     def own(values, chunk, among=sections):
         value = values[chunk]
         for behind in range(1, among):
-            value = jnp.where(section == lead - behind, values[chunk + behind], value)
+            value = jnp.where(is_section[lead - behind], values[chunk + behind], value)
         return value
 
     moved = []
@@ -77,7 +87,7 @@
     for tick in range(ticks):
         grad = jnp.zeros((rows, width), BF16) if tick == 0 else moved[tick - 1]
         if tick < CHUNKS:
-            grad = jnp.where(section == lead, top[tick * rows : (tick + 1) * rows], grad)
+            grad = jnp.where(is_section[lead], top[tick * rows : (tick + 1) * rows], grad)
         d_hidden = cols_dot(grad, weights_down)
         part = factors[tick * rows : (tick + 1) * rows]
         d_gate_up = (jnp.concatenate([d_hidden, d_hidden], axis=1) * part).astype(BF16)
@@ -87,18 +97,24 @@
         passes.append(passed)
         if tick + 1 < ticks:
             moved.append(lax.ppermute(passed, "pipe", down))
-        if tick == 0:
-            hidden, _ = lax.optimization_barrier((hidden, passed))
-            copies = jnp.broadcast_to(hidden[None], (side,) + hidden.shape)
-            hidden = lax.all_to_all(copies, SIDE, 0, 0, tiled=True)
-            hidden = spread(hidden.reshape(-1, block), places).reshape(side, tokens, -1)
-        if tick + 2 == ticks:
-            arrived = jnp.concatenate([own(grads, chunk) for chunk in range(CHUNKS - 1)], axis=0)
-            last = own(grads, CHUNKS - 1, lead)
-            arrived, last = lax.optimization_barrier((arrived, last))
-            terms = rows_dot(hidden[:, :most].reshape(side * most, -1), to_side(arrived))
-    arrived = jnp.where(section == 0, grads[-1], last)
-    terms = terms + rows_dot(hidden[:, most:].reshape(side * rows, -1), to_side(arrived))
+        if tick == ticks - 3:
+            arrived = jnp.concatenate([own(grads, chunk) for chunk in range(early)], axis=0)
+            after = (own(grads, early, lead), own(grads, early + 1, lead - 1))
+            arrived, after = lax.optimization_barrier((arrived, after))
+            sides = [to_side(arrived)]
+        if tick == ticks - 2:
+            arrived = jnp.where(is_section[0], grads[-1], after[0])
+            after = jnp.where(is_section[1], grads[-1], after[1])
+            arrived, after = lax.optimization_barrier((arrived, after))
+            sides.append(to_side(arrived))
+    arrived = jnp.where(is_section[0], grads[-1], after)
+    sides.append(to_side(arrived))
+    passes, sides = lax.optimization_barrier((passes, sides))
+    terms = 0.0
+    for begin, end, rows_of_side in zip(cuts[:-1], cuts[1:], sides):
+        terms = terms + rows_dot(
+            hidden[:, begin:end].reshape(side * (end - begin), -1), rows_of_side
+        )
     in_grads = jnp.concatenate([own(passes, chunk) for chunk in range(CHUNKS)], axis=0)
 
     terms = terms.astype(BF16).reshape(places, 2, -1)
@@ -106,8 +122,7 @@
     sizes = tuple(lax.axis_size(name) for name in DP)
     summed = jnp.sum(terms.astype(F32).reshape(sizes + terms.shape[1:]), axis=(1, 2))
     summed = summed.transpose(2, 0, 1, 3).reshape(-1)
-    start = lax.rem(lax.axis_index(DP), 3) * (width // 3)
-    summed = lax.dynamic_slice(summed, (start,), (moment.shape[1],))
+    summed = lax.dynamic_slice(summed, (third,), (moment.shape[1],))
 
     gradient = summed * float(tokens * places) ** (-0.5)
     new_moment = 0.9 * moment[0] + 0.1 * gradient

time: 191 us -> 193 us (1.010)
  the two profiles are of different devices: /device:TPU:45 before, /device:TPU:1 now
where the time goes in v3:
time: 193 us; the launch traced here: 189 us
  waiting for transfers between devices  70.3 us (36%)
  starting transfers between devices  56.5 us (29%)
  matrix products  39.3 us (20%)
  local copies, waits for them, and re-layouts  12.4 us (6%)
  other arithmetic  9.41 us (5%)
    ppermute x6, waiting for transfers between devices, step(): moved.append(lax.ppermute(passed, 'pipe', down))  40.3 us
    all_to_all x1, waiting for transfers between devices, step(): terms = lax.all_to_all(terms, DP, 0, 0, tiled=True)  21.9 us
    all_to_all x3, starting transfers between devices, to_side(): parts = lax.all_to_all(parts, SIDE, 0, 0, tiled=True)  20.5 us
    all_to_all x1, starting transfers between devices, step(): terms = lax.all_to_all(terms, DP, 0, 0, tiled=True)  19.1 us
    dot_general x7, matrix products, step(): jnp.dot(d_gate_up, weights_in, preferred_element_type=F32)  18.2 us
    dot_general x8, matrix products, cols_dot(): lax.dot_general(left, right, (((1,), (1,)), ((), ())), preferred_element_...  16.5 us
    all_to_all x1, starting transfers between devices, step(): hidden = lax.all_to_all(copies, SIDE, 0, 0, tiled=True)  9.09 us
    all_to_all x3, waiting for transfers between devices, to_side(): parts = lax.all_to_all(parts, SIDE, 0, 0, tiled=True)  8.04 us
  transfers between devices with their start and end apart: 11, of which 9 were waited for; matrix products, arithmetic and copies ran while one was open for 20% of the time, Pallas kernels for 0%

profile of v3, /device:TPU:1, one launch (start us, length us, event | category | flops | bytes accessed | tf_op | source)
XLA Modules:
  0.0 189.0 jit_solution(10112465859352541032)
XLA Ops:
  1.9 3.9 %fusion.14 = f32[128,512]{1,0:T(8,128)S(1)} fusion(bf16[128,4224]{1,0:T(8,128)(2,1)S(1)} %bitcast.81, bf16[1,768,4224]{2,1,0:T(8,128)(2,1)} %param.7), kind=kOutput, calls=%fused_computation.15 | convolution fusion | flops 553648128 | bytes 5668864 | tf_op jit(solution)/shard_map/dot_general | solution.py:18
  6.0 1.7 fusion.28
  10.2 13.4 %collective-permute-done = bf16[32,4224]{1,0:T(8,128)(2,1)S(1)} collective-permute-done((bf16[32,4224]{1,0:T(8,128)(2,1)S(1)}, bf16[32,4224]{1,0:T(8,128)(2,1)S(1)}, u32[]{:S(2)}, u32[]{:S(2)}) %collective-permute-start) | collective-permute-done | bytes 270368 | tf_op jit(solution)/shard_map/ppermute | solution.py:99
  24.4 1.6 add_convert_fusion.5
  28.1 9.1 %all-to-all-start.3 = ((bf16[8,128,256]{2,1,0:T(8,128)(2,1)}), bf16[8,128,256]{2,1,0:T(8,128)(2,1)}, u32[]{:S(2)}, u32[]{:S(2)}) async-start(bf16[8,128,256]{2,1,0:T(8,128)(2,1)} %broadcast_in_dim.23), calls=%async_computation.3 | async-start | bytes 1048576 | tf_op jit(solution)/shard_map/all_to_all | solution.py:72
  37.2 4.1 %collective-permute-done.1 = bf16[32,4224]{1,0:T(8,128)(2,1)} collective-permute-done((bf16[32,4224]{1,0:T(8,128)(2,1)}, bf16[32,4224]{1,0:T(8,128)(2,1)}, u32[]{:S(2)}, u32[]{:S(2)}) %collective-permute-start.1) | collective-permute-done | bytes 270368 | tf_op jit(solution)/shard_map/ppermute | solution.py:99
  42.4 2.5 %fusion.24 = f32[32,256]{1,0:T(8,128)S(1)} fusion(bf16[32,4224]{1,0:T(8,128)(2,1)S(1)} %slice_select_fusion.1, bf16[1,768,4224]{2,1,0:T(8,128)(2,1)} %param.7), kind=kOutput, calls=%fused_computation.25 | convolution fusion | flops 69206016 | bytes 2465792 | tf_op jit(solution)/shard_map/dot_general | solution.py:18
  44.8 3.1 %add_convert_fusion.4 = bf16[32,4224]{1,0:T(8,128)(2,1)S(1)} fusion(bf16[32,4224]{1,0:T(8,128)(2,1)S(1)} %slice_select_fusion.1, bf16[1,768,4224]{2,1,0:T(8,128)(2,1)} %param.7, f32[224,512]{1,0:T(8,128)} %copy-done.9, f32[32,256]{1,0:T(8,128)S(1)} %fusion.24), kind=kOutput, calls=%fused_computation.70 | convolution fusion | flops 138866688 | bytes 4964352 | tf_op jit(solution)/shard_map/dot_general | solution.py:94
  50.1 9.5 %collective-permute-done.2 = bf16[32,4224]{1,0:T(8,128)(2,1)S(1)} collective-permute-done((bf16[32,4224]{1,0:T(8,128)(2,1)S(1)}, bf16[32,4224]{1,0:T(8,128)(2,1)S(1)}, u32[]{:S(2)}, u32[]{:S(2)}) %collective-permute-start.2) | collective-permute-done | bytes 270368 | tf_op jit(solution)/shard_map/ppermute | solution.py:99
  61.1 2.5 %add_convert_fusion.3 = bf16[32,4224]{1,0:T(8,128)(2,1)} fusion(bf16[32,4224]{1,0:T(8,128)(2,1)S(1)} %get-tuple-element.52, bf16[1,768,4224]{2,1,0:T(8,128)(2,1)S(1)} %bitcast.83, f32[224,512]{1,0:T(8,128)} %copy-done.9, f32[32,256]{1,0:T(8,128)S(1)} %fusion.22), kind=kOutput, calls=%fused_computation.69 | convolution fusion | flops 138866688 | bytes 4964352 | tf_op jit(solution)/shard_map/dot_general | solution.py:94
  64.9 1.5 convolution_convert_fusion
  67.3 6.5 %collective-permute-done.3 = bf16[32,4224]{1,0:T(8,128)(2,1)S(1)} collective-permute-done((bf16[32,4224]{1,0:T(8,128)(2,1)}, bf16[32,4224]{1,0:T(8,128)(2,1)S(1)}, u32[]{:S(2)}, u32[]{:S(2)}) %collective-permute-start.3) | collective-permute-done | bytes 270368 | tf_op jit(solution)/shard_map/ppermute | solution.py:99
  73.8 2.3 %fusion.20 = f32[32,256]{1,0:T(8,128)S(1)} fusion(bf16[32,4224]{1,0:T(8,128)(2,1)S(1)} %collective-permute-done.3, bf16[1,768,4224]{2,1,0:T(8,128)(2,1)} %param.7), kind=kOutput, calls=%fused_computation.21 | convolution fusion | flops 69206016 | bytes 2465792 | tf_op jit(solution)/shard_map/dot_general | solution.py:18
  76.1 3.1 %add_convert_fusion.2 = bf16[32,4224]{1,0:T(8,128)(2,1)S(1)} fusion(bf16[32,4224]{1,0:T(8,128)(2,1)S(1)} %collective-permute-done.3, bf16[1,768,4224]{2,1,0:T(8,128)(2,1)} %param.7, f32[224,512]{1,0:T(8,128)} %copy-done.9, f32[32,256]{1,0:T(8,128)S(1)} %fusion.20), kind=kOutput, calls=%fused_computation.68 | convolution fusion | flops 138866688 | bytes 4964352 | tf_op jit(solution)/shard_map/dot_general | solution.py:94
  83.3 7.0 %all-to-all-start = ((bf16[8,64,528]{2,1,0:T(8,128)(2,1)}), bf16[8,64,528]{2,1,0:T(8,128)(2,1)S(1)}, u32[]{:S(2)}, u32[]{:S(2)}) async-start(bf16[8,64,528]{2,1,0:T(8,128)(2,1)} %bitcast.78), calls=%async_computation | async-start | bytes 1310720 | tf_op jit(solution)/shard_map/all_to_all | solution.py:33
  90.3 1.8 collective-permute-done.4
  92.1 2.4 %fusion.18 = f32[32,256]{1,0:T(8,128)S(1)} fusion(bf16[32,4224]{1,0:T(8,128)(2,1)S(1)} %collective-permute-done.4, bf16[1,768,4224]{2,1,0:T(8,128)(2,1)} %param.7), kind=kOutput, calls=%fused_computation.19 | convolution fusion | flops 69206016 | bytes 2465792 | tf_op jit(solution)/shard_map/dot_general | solution.py:18
  94.5 3.1 %add_convert_fusion.1 = bf16[32,4224]{1,0:T(8,128)(2,1)S(1)} fusion(bf16[32,4224]{1,0:T(8,128)(2,1)S(1)} %collective-permute-done.4, bf16[1,768,4224]{2,1,0:T(8,128)(2,1)} %param.7, f32[224,512]{1,0:T(8,128)} %copy-done.9, f32[32,256]{1,0:T(8,128)S(1)} %fusion.18), kind=kOutput, calls=%fused_computation.67 | convolution fusion | flops 138866688 | bytes 4964352 | tf_op jit(solution)/shard_map/dot_general | solution.py:94
  99.0 1.8 broadcast_select_fusion.1
  100.8 1.3 reshape.71
  102.9 5.1 %collective-permute-done.5 = bf16[32,4224]{1,0:T(8,128)(2,1)S(1)} collective-permute-done((bf16[32,4224]{1,0:T(8,128)(2,1)S(1)}, bf16[32,4224]{1,0:T(8,128)(2,1)S(1)}, u32[]{:S(2)}, u32[]{:S(2)}) %collective-permute-start.5) | collective-permute-done | bytes 270368 | tf_op jit(solution)/shard_map/ppermute | solution.py:99
  108.8 1.3 reshape.73
  110.9 9.1 %all-to-all-start.1 = ((bf16[8,32,528]{2,1,0:T(8,128)(2,1)}), bf16[8,32,528]{2,1,0:T(8,128)(2,1)S(1)}, u32[]{:S(2)}, u32[]{:S(2)}) async-start(bf16[8,32,528]{2,1,0:T(8,128)(2,1)} %bitcast.80), calls=%async_computation.1 | async-start | bytes 655360 | tf_op jit(solution)/shard_map/all_to_all | solution.py:33
  120.0 2.3 %fusion.16 = f32[32,256]{1,0:T(8,128)S(1)} fusion(bf16[32,4224]{1,0:T(8,128)(2,1)S(1)} %collective-permute-done.5, bf16[1,768,4224]{2,1,0:T(8,128)(2,1)} %param.7), kind=kOutput, calls=%fused_computation.17 | convolution fusion | flops 69206016 | bytes 2465792 | tf_op jit(solution)/shard_map/dot_general | solution.py:18
  122.3 4.8 %all-to-all-done.1 = bf16[8,32,528]{2,1,0:T(8,128)(2,1)S(1)} async-done(((bf16[8,32,528]{2,1,0:T(8,128)(2,1)}), bf16[8,32,528]{2,1,0:T(8,128)(2,1)S(1)}, u32[]{:S(2)}, u32[]{:S(2)}) %all-to-all-start.1) | async-done | bytes 270368 | tf_op jit(solution)/shard_map/all_to_all | solution.py:33
  127.1 4.5 %all-to-all-start.2 = ((bf16[8,32,528]{2,1,0:T(8,128)(2,1)}), bf16[8,32,528]{2,1,0:T(8,128)(2,1)S(1)}, u32[]{:S(2)}, u32[]{:S(2)}) async-start(bf16[8,32,528]{2,1,0:T(8,128)(2,1)} %bitcast.79), calls=%async_computation.2 | async-start | bytes 655360 | tf_op jit(solution)/shard_map/all_to_all | solution.py:33
  131.5 3.8 %add_convert_fusion = bf16[32,4224]{1,0:T(8,128)(2,1)} fusion(bf16[32,4224]{1,0:T(8,128)(2,1)S(1)} %collective-permute-done.5, bf16[1,768,4224]{2,1,0:T(8,128)(2,1)} %param.7, f32[224,512]{1,0:T(8,128)} %copy-done.9, f32[32,256]{1,0:T(8,128)S(1)} %fusion.16), kind=kOutput, calls=%fused_computation.66 | convolution fusion | flops 138866688 | bytes 4964352 | tf_op jit(solution)/shard_map/dot_general | solution.py:94
  135.3 3.3 %all-to-all-done.2 = bf16[8,32,528]{2,1,0:T(8,128)(2,1)S(1)} async-done(((bf16[8,32,528]{2,1,0:T(8,128)(2,1)}), bf16[8,32,528]{2,1,0:T(8,128)(2,1)S(1)}, u32[]{:S(2)}, u32[]{:S(2)}) %all-to-all-start.2) | async-done | bytes 270368 | tf_op jit(solution)/shard_map/all_to_all | solution.py:33
  139.2 1.3 convolution_add_fusion.2
  143.1 19.1 %all-to-all-start.4 = ((bf16[192,2,528]{2,1,0:T(2,128)(2,1)}), bf16[192,2,528]{2,1,0:T(2,128)(2,1)S(1)}, u32[]{:S(2)}, u32[]{:S(2)}) async-start(bf16[192,2,528]{2,1,0:T(2,128)(2,1)} %reshape.81), calls=%async_computation.4 | async-start | bytes 983040 | tf_op jit(solution)/shard_map/all_to_all | solution.py:121
  162.2 1.3 select_select_fusion.3
  164.6 21.9 %all-to-all-done.4 = bf16[192,2,528]{2,1,0:T(2,128)(2,1)S(1)} async-done(((bf16[192,2,528]{2,1,0:T(2,128)(2,1)}), bf16[192,2,528]{2,1,0:T(2,128)(2,1)S(1)}, u32[]{:S(2)}, u32[]{:S(2)}) %all-to-all-start.4) | async-done | bytes 405536 | tf_op jit(solution)/shard_map/all_to_all | solution.py:121
  (100 shorter events, 27.7 us)
Async XLA Ops:
  1.9 6.2 %copy-start.16 = (bf16[2,64,4224]{2,1,0:T(8,128)(2,1)S(1)}, bf16[2,64,4224]{2,1,0:T(8,128)(2,1)}, u32[]{:S(2)}) copy-start(bf16[2,64,4224]{2,1,0:T(8,128)(2,1)} %param.6) | copy-start | bytes 3244036
  8.0 17.9 %copy-start.9 = (f32[224,512]{1,0:T(8,128)}, f32[224,512]{1,0:T(8,128)S(1)}, u32[]{:S(2)}) copy-start(f32[224,512]{1,0:T(8,128)S(1)} %fusion.51) | copy-start | bytes 1376260
  8.9 14.7 %collective-permute-start = (bf16[32,4224]{1,0:T(8,128)(2,1)S(1)}, bf16[32,4224]{1,0:T(8,128)(2,1)S(1)}, u32[]{:S(2)}, u32[]{:S(2)}) collective-permute-start(bf16[32,4224]{1,0:T(8,128)(2,1)S(1)} %fusion), channel_id=1, source_target_pairs={{1,0},{2,1},{3,2},{5,4},{6,5},{7,6},{9,8},{10,9},{11,10},{13,12},{... | collective-permute-start | bytes 811016 | tf_op jit(solution)/shard_map/ppermute | solution.py:99
  24.4 36.0 %slice-start = ((s8[6488064]{0:T(1024)(128)(4,1)}), s8[2293760]{0:T(1024)(128)(4,1)S(1)}, s32[]{:S(2)}) async-start(s8[6488064]{0:T(1024)(128)(4,1)} %bitcast.82), calls=%async_computation.5 | async-start | bytes 4587520
  26.0 15.3 %collective-permute-start.1 = (bf16[32,4224]{1,0:T(8,128)(2,1)}, bf16[32,4224]{1,0:T(8,128)(2,1)}, u32[]{:S(2)}, u32[]{:S(2)}) collective-permute-start(bf16[32,4224]{1,0:T(8,128)(2,1)} %add_convert_fusion.5), channel_id=1, source_target_pairs={{1,0},{2,1},{3,2},{5,4},{6,5},{7,6},{9,8},{10,9},{11,10},{13,12},{... | collective-permute-start | bytes 811016 | tf_op jit(solution)/shard_map/ppermute | solution.py:99
  28.1 36.8 %all-to-all-start.3 = ((bf16[8,128,256]{2,1,0:T(8,128)(2,1)}), bf16[8,128,256]{2,1,0:T(8,128)(2,1)}, u32[]{:S(2)}, u32[]{:S(2)}) async-start(bf16[8,128,256]{2,1,0:T(8,128)(2,1)} %broadcast_in_dim.23), calls=%async_computation.3 | async-start | bytes 1048576 | tf_op jit(solution)/shard_map/all_to_all | solution.py:72
  37.2 12.1 %copy-start.24 = (f32[1,5632]{1,0:T(1,128)S(1)}, f32[1,5632]{1,0:T(1,128)}, u32[]{:S(2)}) copy-start(f32[1,5632]{1,0:T(1,128)} %param.9) | copy-start | bytes 67588
  37.2 12.2 %copy-start.25 = (f32[1,5632]{1,0:T(1,128)S(1)}, f32[1,5632]{1,0:T(1,128)}, u32[]{:S(2)}) copy-start(f32[1,5632]{1,0:T(1,128)} %param.8) | copy-start | bytes 67588
  37.2 22.4 %copy-start.3 = (bf16[32,4224]{1,0:T(8,128)(2,1)S(1)}, bf16[32,4224]{1,0:T(8,128)(2,1)}, u32[]{:S(2)}) copy-start(bf16[32,4224]{1,0:T(8,128)(2,1)} %copy-done.2) | copy-start | bytes 811012
  37.2 22.4 %copy-start.17 = (bf16[2,64,4224]{2,1,0:T(8,128)(2,1)S(1)}, bf16[2,64,4224]{2,1,0:T(8,128)(2,1)}, u32[]{:S(2)}) copy-start(bf16[2,64,4224]{2,1,0:T(8,128)(2,1)} %param.6) | copy-start | bytes 3244036
  42.3 18.0 %copy-start.5 = (bf16[32,4224]{1,0:T(8,128)(2,1)}, bf16[32,4224]{1,0:T(8,128)(2,1)S(1)}, u32[]{:S(2)}) copy-start(bf16[32,4224]{1,0:T(8,128)(2,1)S(1)} %slice_select_fusion.1) | copy-start | bytes 811012
  42.4 18.0 %slice-start.1 = ((s8[6488064]{0:T(1024)(128)(4,1)}), s8[4194304]{0:T(1024)(128)(4,1)S(1)}, s32[]{:S(2)}) async-start(s8[6488064]{0:T(1024)(128)(4,1)} %bitcast.82), calls=%async_computation.6 | async-start | bytes 8388608
  48.0 11.5 %collective-permute-start.2 = (bf16[32,4224]{1,0:T(8,128)(2,1)S(1)}, bf16[32,4224]{1,0:T(8,128)(2,1)S(1)}, u32[]{:S(2)}, u32[]{:S(2)}) collective-permute-start(bf16[32,4224]{1,0:T(8,128)(2,1)S(1)} %add_convert_fusion.4), channel_id=1, source_target_pairs={{1,0},{2,1},{3,2},{5,4},{6,5},{7,6},{9,8},{10,9},{11,10},{13,12},{... | collective-permute-start | bytes 811016 | tf_op jit(solution)/shard_map/ppermute | solution.py:99
  63.6 10.2 %collective-permute-start.3 = (bf16[32,4224]{1,0:T(8,128)(2,1)}, bf16[32,4224]{1,0:T(8,128)(2,1)S(1)}, u32[]{:S(2)}, u32[]{:S(2)}) collective-permute-start(bf16[32,4224]{1,0:T(8,128)(2,1)} %add_convert_fusion.3), channel_id=1, source_target_pairs={{1,0},{2,1},{3,2},{5,4},{6,5},{7,6},{9,8},{10,9},{11,10},{13,12},{... | collective-permute-start | bytes 811016 | tf_op jit(solution)/shard_map/ppermute | solution.py:99
  66.4 14.2 %copy-start.4 = (bf16[32,4224]{1,0:T(8,128)(2,1)S(1)}, bf16[32,4224]{1,0:T(8,128)(2,1)}, u32[]{:S(2)}) copy-start(bf16[32,4224]{1,0:T(8,128)(2,1)} %copy-done.2) | copy-start | bytes 811012
  66.4 14.2 %copy-start.6 = (bf16[32,4224]{1,0:T(8,128)(2,1)S(1)}, bf16[32,4224]{1,0:T(8,128)(2,1)}, u32[]{:S(2)}) copy-start(bf16[32,4224]{1,0:T(8,128)(2,1)} %copy-done.5) | copy-start | bytes 811012
  66.4 14.2 %copy-start.8 = (bf16[32,4224]{1,0:T(8,128)(2,1)S(1)}, bf16[32,4224]{1,0:T(8,128)(2,1)}, u32[]{:S(2)}) copy-start(bf16[32,4224]{1,0:T(8,128)(2,1)} %copy-done.7) | copy-start | bytes 811012
  67.3 14.3 %copy-start.18 = (bf16[32,4224]{1,0:T(8,128)(2,1)S(1)}, bf16[32,4224]{1,0:T(8,128)(2,1)}, u32[]{:S(2)}) copy-start(bf16[32,4224]{1,0:T(8,128)(2,1)} %get-tuple-element.51) | copy-start | bytes 811012
  79.3 12.8 %collective-permute-start.4 = (bf16[32,4224]{1,0:T(8,128)(2,1)S(1)}, bf16[32,4224]{1,0:T(8,128)(2,1)S(1)}, u32[]{:S(2)}, u32[]{:S(2)}) collective-permute-start(bf16[32,4224]{1,0:T(8,128)(2,1)S(1)} %add_convert_fusion.2), channel_id=1, source_target_pairs={{1,0},{2,1},{3,2},{5,4},{6,5},{7,6},{9,8},{10,9},{11,10},{13,12},{... | collective-permute-start | bytes 811016 | tf_op jit(solution)/shard_map/ppermute | solution.py:99
  83.3 15.7 %copy-start.19 = (bf16[32,4224]{1,0:T(8,128)(2,1)S(1)}, bf16[32,4224]{1,0:T(8,128)(2,1)}, u32[]{:S(2)}) copy-start(bf16[32,4224]{1,0:T(8,128)(2,1)} %get-tuple-element.33) | copy-start | bytes 811012
  83.3 15.7 %copy-start.20 = (bf16[32,4224]{1,0:T(8,128)(2,1)S(1)}, bf16[32,4224]{1,0:T(8,128)(2,1)}, u32[]{:S(2)}) copy-start(bf16[32,4224]{1,0:T(8,128)(2,1)} %get-tuple-element.34) | copy-start | bytes 811012
  83.3 27.6 %all-to-all-start = ((bf16[8,64,528]{2,1,0:T(8,128)(2,1)}), bf16[8,64,528]{2,1,0:T(8,128)(2,1)S(1)}, u32[]{:S(2)}, u32[]{:S(2)}) async-start(bf16[8,64,528]{2,1,0:T(8,128)(2,1)} %bitcast.78), calls=%async_computation | async-start | bytes 1310720 | tf_op jit(solution)/shard_map/all_to_all | solution.py:33
  97.7 29.4 %copy-start.12 = (bf16[32,4224]{1,0:T(8,128)(2,1)}, bf16[32,4224]{1,0:T(8,128)(2,1)S(1)}, u32[]{:S(2)}) copy-start(bf16[32,4224]{1,0:T(8,128)(2,1)S(1)} %add_convert_fusion.1) | copy-start | bytes 811012
  97.7 10.3 %collective-permute-start.5 = (bf16[32,4224]{1,0:T(8,128)(2,1)S(1)}, bf16[32,4224]{1,0:T(8,128)(2,1)S(1)}, u32[]{:S(2)}, u32[]{:S(2)}) collective-permute-start(bf16[32,4224]{1,0:T(8,128)(2,1)S(1)} %add_convert_fusion.1), channel_id=1, source_target_pairs={{1,0},{2,1},{3,2},{5,4},{6,5},{7,6},{9,8},{10,9},{11,10},{13,12},{... | collective-permute-start | bytes 811016 | tf_op jit(solution)/shard_map/ppermute | solution.py:99
  110.9 16.2 %all-to-all-start.1 = ((bf16[8,32,528]{2,1,0:T(8,128)(2,1)}), bf16[8,32,528]{2,1,0:T(8,128)(2,1)S(1)}, u32[]{:S(2)}, u32[]{:S(2)}) async-start(bf16[8,32,528]{2,1,0:T(8,128)(2,1)} %bitcast.80), calls=%async_computation.1 | async-start | bytes 655360 | tf_op jit(solution)/shard_map/all_to_all | solution.py:33
  127.1 11.6 %all-to-all-start.2 = ((bf16[8,32,528]{2,1,0:T(8,128)(2,1)}), bf16[8,32,528]{2,1,0:T(8,128)(2,1)S(1)}, u32[]{:S(2)}, u32[]{:S(2)}) async-start(bf16[8,32,528]{2,1,0:T(8,128)(2,1)} %bitcast.79), calls=%async_computation.2 | async-start | bytes 655360 | tf_op jit(solution)/shard_map/all_to_all | solution.py:33
  135.3 26.8 %copy-start.11 = (bf16[32,4224]{1,0:T(8,128)(2,1)S(1)}, bf16[32,4224]{1,0:T(8,128)(2,1)}, u32[]{:S(2)}) copy-start(bf16[32,4224]{1,0:T(8,128)(2,1)} %copy-done.10) | copy-start | bytes 811012
  139.1 23.0 %copy-start.13 = (bf16[32,4224]{1,0:T(8,128)(2,1)S(1)}, bf16[32,4224]{1,0:T(8,128)(2,1)}, u32[]{:S(2)}) copy-start(bf16[32,4224]{1,0:T(8,128)(2,1)} %copy-done.12) | copy-start | bytes 811012
  139.1 23.0 %copy-start.14 = (bf16[32,4224]{1,0:T(8,128)(2,1)S(1)}, bf16[32,4224]{1,0:T(8,128)(2,1)}, u32[]{:S(2)}) copy-start(bf16[32,4224]{1,0:T(8,128)(2,1)} %add_convert_fusion) | copy-start | bytes 811012
  141.8 45.3 %copy-start.22 = (f32[5632]{0:T(1024)S(1)}, f32[5632]{0:T(1024)}, u32[]{:S(2)}) copy-start(f32[5632]{0:T(1024)} %get-tuple-element.73) | copy-start | bytes 67588
  141.8 45.3 %copy-start.23 = (f32[5632]{0:T(1024)S(1)}, f32[5632]{0:T(1024)}, u32[]{:S(2)}) copy-start(f32[5632]{0:T(1024)} %get-tuple-element.74) | copy-start | bytes 67588
  143.1 43.4 %all-to-all-start.4 = ((bf16[192,2,528]{2,1,0:T(2,128)(2,1)}), bf16[192,2,528]{2,1,0:T(2,128)(2,1)S(1)}, u32[]{:S(2)}, u32[]{:S(2)}) async-start(bf16[192,2,528]{2,1,0:T(2,128)(2,1)} %reshape.81), calls=%async_computation.4 | async-start | bytes 983040 | tf_op jit(solution)/shard_map/all_to_all | solution.py:121
  (7 other events, 16.8 us)

commit v4 on v3

v4 whole, which is shorter than its diff:
```python
import jax
import jax.numpy as jnp
from jax import lax
from jax.sharding import Mesh, PartitionSpec as P


CHUNKS = 8
DEPTH = 2
DP = ("x", "yl", "z", "core")
SIDE = ("x", "core")
F32 = jnp.float32
BF16 = jnp.bfloat16


def rows_dot(left, right):
    return lax.dot_general(left, right, (((0,), (0,)), ((), ())), preferred_element_type=F32)


def cols_dot(left, right):
    return lax.dot_general(left, right, (((1,), (1,)), ((), ())), preferred_element_type=F32)


def to_side(rows):
    count = lax.axis_size(SIDE)
    parts = rows.reshape(rows.shape[0], 3, count, -1).transpose(2, 0, 1, 3)
    parts = parts.reshape(count, rows.shape[0], -1)
    parts = lax.all_to_all(parts, SIDE, 0, 0, tiled=True)
    return parts.reshape(-1, parts.shape[2])


def step(acts, out_grad, params, moment, second):
    sections = lax.axis_size("pipe")
    section = lax.axis_index("pipe")
    places = lax.axis_size(DP)
    side = lax.axis_size(SIDE)
    width = acts.shape[-1]
    tokens = acts.shape[1] * acts.shape[2]
    rows = tokens // CHUNKS
    lead = sections - 1
    ticks = CHUNKS + DEPTH * lead
    first_chunk = (section * (DEPTH * rows)).astype(jnp.uint32)
    is_section = [section == at for at in range(sections)]
    acts, first_chunk, is_section = lax.optimization_barrier((acts, first_chunk, is_section))
    inputs = acts.reshape(-1, width)
    top = out_grad.reshape(-1, width)
    block = params.shape[1] // 3
    weights_in = params[0, : 2 * block]
    weights_down = params[0, 2 * block :]
    gate_up = cols_dot(inputs, weights_in)
    gate = gate_up[:, :block]
    up = gate_up[:, block:]
    sg = jax.nn.sigmoid(gate)
    activated = gate * sg
    factors = jnp.concatenate([up * sg * (1.0 + gate * (1.0 - sg)), activated], axis=1)
    hidden = (activated * up).astype(BF16)
    pad = jnp.zeros((DEPTH * lead * rows, 2 * block), F32)
    factors = lax.dynamic_slice(
        jnp.concatenate([pad, factors, pad], axis=0),
        (first_chunk, jnp.uint32(0)),
        (ticks * rows, 2 * block),
    )
    copies = jnp.broadcast_to(hidden[None], (side,) + hidden.shape)
    hidden = lax.all_to_all(copies, SIDE, 0, 0, tiled=True)
    top = jnp.where(is_section[lead], top, 0)
    tops = lax.optimization_barrier(
        [top[chunk * rows : (chunk + 1) * rows] for chunk in range(CHUNKS)]
    )
    down = [(s, s - 1) for s in range(1, sections)]
    cuts = (0, CHUNKS - 2, CHUNKS)

    def own(values, count):
        chunks = []
        for chunk in range(count):
            value = values[chunk]
            for behind in range(1, sections):
                value = jnp.where(is_section[lead - behind], values[chunk + DEPTH * behind], value)
            chunks.append(value)
        return jnp.concatenate(chunks, axis=0)

    moved = []
    grads = []
    passes = []
    sides = []
    for tick in range(ticks):
        grad = None if tick < DEPTH else moved[tick - DEPTH]
        if tick < CHUNKS:
            grad = tops[tick] if grad is None else grad + tops[tick]
        grads.append(grad)
        d_hidden = cols_dot(grad, weights_down)
        part = factors[tick * rows : (tick + 1) * rows]
        d_gate_up = (jnp.concatenate([d_hidden, d_hidden], axis=1) * part).astype(BF16)
        passed = grad.astype(F32) + jnp.dot(d_gate_up, weights_in, preferred_element_type=F32)
        passed = passed.astype(BF16)
        passes.append(passed)
        if tick + DEPTH < ticks:
            moved.append(lax.ppermute(passed, "pipe", down))
        done = tick + 1 - DEPTH * lead
        if done in cuts[1:]:
            begin = cuts[len(sides)]
            seen, _ = lax.optimization_barrier((grads[begin:], passed if done < CHUNKS else grad))
            arrived = own(seen, done - begin)
            sides.append(to_side(arrived))

    passes, sides = lax.optimization_barrier((passes, sides))
    terms = 0.0
    for begin, end, rows_of_side in zip(cuts[:-1], cuts[1:], sides):
        part = hidden[:, begin * rows : end * rows].reshape(-1, block)
        terms = terms + rows_dot(part, rows_of_side)

    in_grads = own(passes, CHUNKS)

    terms = terms.astype(BF16).reshape(places, 2, -1)
    terms = lax.all_to_all(terms, DP, 0, 0, tiled=True)
    sizes = tuple(lax.axis_size(name) for name in DP)
    summed = jnp.sum(terms.astype(F32).reshape(sizes + terms.shape[1:]), axis=(1, 2))
    summed = summed.reshape(side, 4, -1).transpose(1, 0, 2).reshape(-1)

    gradient = summed * float(tokens * places) ** (-0.5)
    new_moment = 0.9 * moment[0] + 0.1 * gradient
    new_second = 0.999 * second[0] + 0.001 * gradient * gradient
    update = new_moment / (1.0 - 0.9**10) / (jnp.sqrt(new_second / (1.0 - 0.999**10)) + 1e-08)
    return (in_grads.reshape(acts.shape), new_moment[None], new_second[None], update[None])


def solution(mesh):
    fine = Mesh(mesh.devices.reshape(4, 2, 12, 2, 4), DP + ("pipe",))
    placed = (
        P("pipe", None, DP, None),
        P(None, DP, None),
        P("pipe", None, None),
        P("pipe", DP),
        P("pipe", DP),
    )
    return jax.shard_map(
        step,
        mesh=fine,
        in_specs=placed,
        out_specs=(P("pipe", None, DP, None), P("pipe", DP), P("pipe", DP), P("pipe", DP)),
        check_vma=False,
    )
```

time: 193 us -> 199 us (1.031)
  the two profiles are of different devices: /device:TPU:1 before, /device:TPU:61 now
where the time goes in v4:
time: 199 us; the launch traced here: 197 us
  starting transfers between devices  90 us (45%)
  matrix products  57.3 us (29%)
  other arithmetic  19 us (10%)
  local copies, waits for them, and re-layouts  18.5 us (9%)
  waiting for transfers between devices  10.9 us (5%)
    ppermute x12, starting transfers between devices, step(): moved.append(lax.ppermute(passed, 'pipe', down))  41.1 us
    dot_general x14, matrix products, step(): jnp.dot(d_gate_up, weights_in, preferred_element_type=F32)  30.5 us
    all_to_all x1, starting transfers between devices, step(): terms = lax.all_to_all(terms, DP, 0, 0, tiled=True)  27.4 us
    dot_general x15, matrix products, cols_dot(): lax.dot_general(left, right, (((1,), (1,)), ((), ())), preferred_element_...  23.3 us
    all_to_all x2, starting transfers between devices, to_side(): parts = lax.all_to_all(parts, SIDE, 0, 0, tiled=True)  15.9 us
    unnamed x14, other arithmetic  11.5 us
    all_to_all x1, waiting for transfers between devices, step(): terms = lax.all_to_all(terms, DP, 0, 0, tiled=True)  8.21 us
    all_to_all x1, starting transfers between devices, step(): hidden = lax.all_to_all(copies, SIDE, 0, 0, tiled=True)  5.64 us
  transfers between devices with their start and end apart: 16, of which 4 were waited for; matrix products, arithmetic and copies ran while one was open for 40% of the time, Pallas kernels for 0%

profile of v4, /device:TPU:61, one launch (start us, length us, event | category | flops | bytes accessed | tf_op | source)
XLA Modules:
  0.0 197.0 jit_solution(2130901495951315535)
XLA Ops:
  3.0 4.4 %fusion.28 = f32[128,512]{1,0:T(8,128)S(1)} fusion(bf16[128,4224]{1,0:T(8,128)(2,1)S(1)} %bitcast.119, bf16[1,768,4224]{2,1,0:T(8,128)(2,1)} %param.7), kind=kOutput, calls=%fused_computation.30 | convolution fusion | flops 553648128 | bytes 5668864 | tf_op jit(solution)/shard_map/dot_general | solution.py:20
  9.9 3.6 %collective-permute-start = (bf16[16,4224]{1,0:T(8,128)(2,1)}, bf16[16,4224]{1,0:T(8,128)(2,1)}, u32[]{:S(2)}, u32[]{:S(2)}) collective-permute-start(bf16[16,4224]{1,0:T(8,128)(2,1)} %fusion), channel_id=1, source_target_pairs={{1,0},{2,1},{3,2},{5,4},{6,5},{7,6},{9,8},{10,9},{11,10},{13,12},{... | collective-permute-start | bytes 405512 | tf_op jit(solution)/shard_map/ppermute | solution.py:96
  15.5 2.9 %collective-permute-start.1 = (bf16[16,4224]{1,0:T(8,128)(2,1)}, bf16[16,4224]{1,0:T(8,128)(2,1)}, u32[]{:S(2)}, u32[]{:S(2)}) collective-permute-start(bf16[16,4224]{1,0:T(8,128)(2,1)} %fusion.1), channel_id=1, source_target_pairs={{1,0},{2,1},{3,2},{5,4},{6,5},{7,6},{9,8},{10,9},{11,10},{13,12},{... | collective-permute-start | bytes 405512 | tf_op jit(solution)/shard_map/ppermute | solution.py:96
  19.2 5.6 %all-to-all-start.2 = ((bf16[8,128,256]{2,1,0:T(8,128)(2,1)}), bf16[8,128,256]{2,1,0:T(8,128)(2,1)}, u32[]{:S(2)}, u32[]{:S(2)}) async-start(bf16[8,128,256]{2,1,0:T(8,128)(2,1)} %broadcast_in_dim.18), calls=%async_computation.2 | async-start | bytes 1048576 | tf_op jit(solution)/shard_map/all_to_all | solution.py:63
  25.9 2.4 %fusion.52 = f32[16,256]{1,0:T(8,128)S(1)} fusion(bf16[16,4224]{1,0:T(8,128)(2,1)S(1)} %add.90, bf16[1,768,4224]{2,1,0:T(8,128)(2,1)} %param.7), kind=kOutput, calls=%fused_computation.54 | convolution fusion | flops 34603008 | bytes 2314240 | tf_op jit(solution)/shard_map/dot_general | solution.py:20
  28.3 3.0 %add_convert_fusion.11 = bf16[16,4224]{1,0:T(8,128)(2,1)S(1)} fusion(bf16[16,4224]{1,0:T(8,128)(2,1)S(1)} %add.90, f32[224,512]{1,0:T(8,128)} %copy-done.22, f32[16,256]{1,0:T(8,128)S(1)} %fusion.52, bf16[1,768,4224]{2,1,0:T(8,128)(2,1)} %param.7), kind=kOutput, calls=%fused_computation.84 | convolution fusion | flops 69433344 | bytes 4644864 | tf_op jit(solution)/shard_map/dot_general | solution.py:92
  32.4 2.3 %fusion.50 = f32[16,256]{1,0:T(8,128)S(1)} fusion(bf16[16,4224]{1,0:T(8,128)(2,1)S(1)} %add.92, bf16[1,768,4224]{2,1,0:T(8,128)(2,1)} %param.7), kind=kOutput, calls=%fused_computation.52 | convolution fusion | flops 34603008 | bytes 2314240 | tf_op jit(solution)/shard_map/dot_general | solution.py:20
  42.7 5.0 %collective-permute-start.4 = (bf16[16,4224]{1,0:T(8,128)(2,1)S(1)}, bf16[16,4224]{1,0:T(8,128)(2,1)S(1)}, u32[]{:S(2)}, u32[]{:S(2)}) collective-permute-start(bf16[16,4224]{1,0:T(8,128)(2,1)S(1)} %add_convert_fusion.9), channel_id=1, source_target_pairs={{1,0},{2,1},{3,2},{5,4},{6,5},{7,6},{9,8},{10,9},{11,10},{13,12},{... | collective-permute-start | bytes 405512 | tf_op jit(solution)/shard_map/ppermute | solution.py:96
  49.1 3.5 %collective-permute-start.5 = (bf16[16,4224]{1,0:T(8,128)(2,1)S(1)}, bf16[16,4224]{1,0:T(8,128)(2,1)S(1)}, u32[]{:S(2)}, u32[]{:S(2)}) collective-permute-start(bf16[16,4224]{1,0:T(8,128)(2,1)S(1)} %add_convert_fusion.8), channel_id=1, source_target_pairs={{1,0},{2,1},{3,2},{5,4},{6,5},{7,6},{9,8},{10,9},{11,10},{13,12},{... | collective-permute-start | bytes 405512 | tf_op jit(solution)/shard_map/ppermute | solution.py:96
  53.4 2.1 %add_convert_fusion.7 = bf16[16,4224]{1,0:T(8,128)(2,1)} fusion(bf16[16,4224]{1,0:T(8,128)(2,1)S(1)} %add.98, f32[224,512]{1,0:T(8,128)} %copy-done.22, f32[16,256]{1,0:T(8,128)S(1)} %fusion.44, bf16[1,768,4224]{2,1,0:T(8,128)(2,1)S(1)} %bitcast.121), kind=kOutput, calls=%fused_computation.80 | convolution fusion | flops 69433344 | bytes 4644864 | tf_op jit(solution)/shard_map/dot_general | solution.py:92
  56.2 5.2 %collective-permute-start.6 = (bf16[16,4224]{1,0:T(8,128)(2,1)}, bf16[16,4224]{1,0:T(8,128)(2,1)}, u32[]{:S(2)}, u32[]{:S(2)}) collective-permute-start(bf16[16,4224]{1,0:T(8,128)(2,1)} %add_convert_fusion.7), channel_id=1, source_target_pairs={{1,0},{2,1},{3,2},{5,4},{6,5},{7,6},{9,8},{10,9},{11,10},{13,12},{... | collective-permute-start | bytes 405512 | tf_op jit(solution)/shard_map/ppermute | solution.py:96
  61.4 2.1 %add_convert_fusion.6 = bf16[16,4224]{1,0:T(8,128)(2,1)} fusion(bf16[16,4224]{1,0:T(8,128)(2,1)S(1)} %add.100, f32[224,512]{1,0:T(8,128)} %copy-done.22, f32[16,256]{1,0:T(8,128)S(1)} %fusion.42, bf16[1,768,4224]{2,1,0:T(8,128)(2,1)S(1)} %bitcast.121), kind=kOutput, calls=%fused_computation.79 | convolution fusion | flops 69433344 | bytes 4644864 | tf_op jit(solution)/shard_map/dot_general | solution.py:92
  63.5 5.6 %collective-permute-start.7 = (bf16[16,4224]{1,0:T(8,128)(2,1)}, bf16[16,4224]{1,0:T(8,128)(2,1)S(1)}, u32[]{:S(2)}, u32[]{:S(2)}) collective-permute-start(bf16[16,4224]{1,0:T(8,128)(2,1)} %add_convert_fusion.6), channel_id=1, source_target_pairs={{1,0},{2,1},{3,2},{5,4},{6,5},{7,6},{9,8},{10,9},{11,10},{13,12},{... | collective-permute-start | bytes 405512 | tf_op jit(solution)/shard_map/ppermute | solution.py:96
  72.6 2.3 %fusion.40 = f32[16,256]{1,0:T(8,128)S(1)} fusion(bf16[16,4224]{1,0:T(8,128)(2,1)} %collective-permute-done.6, bf16[1,768,4224]{2,1,0:T(8,128)(2,1)} %param.7), kind=kOutput, calls=%fused_computation.42 | convolution fusion | flops 34603008 | bytes 2314240 | tf_op jit(solution)/shard_map/dot_general | solution.py:20
  75.0 3.1 %add_convert_fusion.5 = bf16[16,4224]{1,0:T(8,128)(2,1)S(1)} fusion(bf16[16,4224]{1,0:T(8,128)(2,1)} %collective-permute-done.6, f32[224,512]{1,0:T(8,128)} %copy-done.22, f32[16,256]{1,0:T(8,128)S(1)} %fusion.40, bf16[1,768,4224]{2,1,0:T(8,128)(2,1)} %param.7), kind=kOutput, calls=%fused_computation.78 | convolution fusion | flops 69433344 | bytes 4644864 | tf_op jit(solution)/shard_map/dot_general | solution.py:92
  80.0 2.2 %fusion.38 = f32[16,256]{1,0:T(8,128)S(1)} fusion(bf16[16,4224]{1,0:T(8,128)(2,1)S(1)} %collective-permute-done.7, bf16[1,768,4224]{2,1,0:T(8,128)(2,1)} %param.7), kind=kOutput, calls=%fused_computation.40 | convolution fusion | flops 34603008 | bytes 2314240 | tf_op jit(solution)/shard_map/dot_general | solution.py:20
  82.3 3.0 %add_convert_fusion.4 = bf16[16,4224]{1,0:T(8,128)(2,1)S(1)} fusion(bf16[16,4224]{1,0:T(8,128)(2,1)S(1)} %collective-permute-done.7, f32[224,512]{1,0:T(8,128)} %copy-done.22, f32[16,256]{1,0:T(8,128)S(1)} %fusion.38, bf16[1,768,4224]{2,1,0:T(8,128)(2,1)} %param.7), kind=kOutput, calls=%fused_computation.77 | convolution fusion | flops 69433344 | bytes 4644864 | tf_op jit(solution)/shard_map/dot_general | solution.py:92
  85.2 4.9 %collective-permute-start.9 = (bf16[16,4224]{1,0:T(8,128)(2,1)S(1)}, bf16[16,4224]{1,0:T(8,128)(2,1)S(1)}, u32[]{:S(2)}, u32[]{:S(2)}) collective-permute-start(bf16[16,4224]{1,0:T(8,128)(2,1)S(1)} %add_convert_fusion.4), channel_id=1, source_target_pairs={{1,0},{2,1},{3,2},{5,4},{6,5},{7,6},{9,8},{10,9},{11,10},{13,12},{... | collective-permute-start | bytes 405512 | tf_op jit(solution)/shard_map/ppermute | solution.py:96
  92.4 3.2 %collective-permute-start.10 = (bf16[16,4224]{1,0:T(8,128)(2,1)S(1)}, bf16[16,4224]{1,0:T(8,128)(2,1)}, u32[]{:S(2)}, u32[]{:S(2)}) collective-permute-start(bf16[16,4224]{1,0:T(8,128)(2,1)S(1)} %add_convert_fusion.3), channel_id=1, source_target_pairs={{1,0},{2,1},{3,2},{5,4},{6,5},{7,6},{9,8},{10,9},{11,10},{13,12},{... | collective-permute-start | bytes 405512 | tf_op jit(solution)/shard_map/ppermute | solution.py:96
  97.7 2.0 collective-permute-start.11
  104.1 3.0 %reshape.102 = bf16[96,3,8,176]{3,2,1,0:T(8,128)(2,1)S(1)} reshape(bf16[96,4224]{1,0:T(8,128)(2,1)} %select_dynamic-update-slice_fusion.8) | data formatting | bytes 1622016 | tf_op jit(solution)/shard_map/reshape | solution.py:25
  107.0 2.3 %copy.18 = bf16[8,96,3,176]{1,3,2,0:T(8,128)(2,1)} copy(bf16[8,96,3,176]{3,0,2,1:T(8,128)(2,1)S(1)} %bitcast.124) | data formatting | bytes 1622016 | tf_op jit(solution)/shard_map/transpose | solution.py:25
  109.4 2.3 %copy.19 = bf16[8,96,528]{2,1,0:T(8,128)(2,1)} copy(bf16[8,96,528]{1,2,0:T(8,128)(2,1)} %bitcast.126) | data formatting | bytes 1622016 | tf_op jit(solution)/shard_map/reshape | solution.py:26
  111.7 8.6 %all-to-all-start = ((bf16[8,96,528]{2,1,0:T(8,128)(2,1)}), bf16[8,96,528]{2,1,0:T(8,128)(2,1)S(1)}, u32[]{:S(2)}, u32[]{:S(2)}) async-start(bf16[8,96,528]{2,1,0:T(8,128)(2,1)} %copy.19), calls=%async_computation | async-start | bytes 1966080 | tf_op jit(solution)/shard_map/all_to_all | solution.py:27
  120.5 2.3 %fusion.32 = f32[16,256]{1,0:T(8,128)S(1)} fusion(bf16[16,4224]{1,0:T(8,128)(2,1)} %collective-permute-done.10, bf16[1,768,4224]{2,1,0:T(8,128)(2,1)} %param.7), kind=kOutput, calls=%fused_computation.34 | convolution fusion | flops 34603008 | bytes 2314240 | tf_op jit(solution)/shard_map/dot_general | solution.py:20
  124.7 2.3 %fusion.30 = f32[16,256]{1,0:T(8,128)S(1)} fusion(bf16[16,4224]{1,0:T(8,128)(2,1)} %collective-permute-done.11, bf16[1,768,4224]{2,1,0:T(8,128)(2,1)} %param.7), kind=kOutput, calls=%fused_computation.32 | convolution fusion | flops 34603008 | bytes 2314240 | tf_op jit(solution)/shard_map/dot_general | solution.py:20
  127.0 3.6 %add_convert_fusion.1 = bf16[16,4224]{1,0:T(8,128)(2,1)} fusion(bf16[16,4224]{1,0:T(8,128)(2,1)} %collective-permute-done.10, f32[224,512]{1,0:T(8,128)} %copy-done.22, f32[16,256]{1,0:T(8,128)S(1)} %fusion.32, bf16[1,768,4224]{2,1,0:T(8,128)(2,1)} %param.7), kind=kOutput, calls=%fused_computation.74 | convolution fusion | flops 69433344 | bytes 4644864 | tf_op jit(solution)/shard_map/dot_general | solution.py:92
  132.2 7.3 %all-to-all-start.1 = ((bf16[8,32,528]{2,1,0:T(8,128)(2,1)}), bf16[8,32,528]{2,1,0:T(8,128)(2,1)}, u32[]{:S(2)}, u32[]{:S(2)}) async-start(bf16[8,32,528]{2,1,0:T(8,128)(2,1)} %reshape.106), calls=%async_computation.1 | async-start | bytes 655360 | tf_op jit(solution)/shard_map/all_to_all | solution.py:27
  139.5 3.6 %add_convert_fusion = bf16[16,4224]{1,0:T(8,128)(2,1)} fusion(bf16[16,4224]{1,0:T(8,128)(2,1)} %collective-permute-done.11, f32[224,512]{1,0:T(8,128)} %copy-done.22, f32[16,256]{1,0:T(8,128)S(1)} %fusion.30, bf16[1,768,4224]{2,1,0:T(8,128)(2,1)} %param.7), kind=kOutput, calls=%fused_computation.73 | convolution fusion | flops 69433344 | bytes 4644864 | tf_op jit(solution)/shard_map/dot_general | solution.py:92
  145.8 2.1 %fusion.58 = bf16[256,528]{0,1:T(8,128)(2,1)} fusion(f32[256,528]{0,1:T(8,128)S(1)} %fusion.183, bf16[768,528]{0,1:T(8,128)(2,1)S(1)} %copy.25, bf16[768,256]{1,0:T(8,128)(2,1)} %bitcast.129), kind=kOutput, calls=%fused_computation.61 | convolution fusion | flops 207888384 | bytes 2015232 | tf_op jit(solution)/shard_map/dot_general | solution.py:16
  150.3 27.4 %all-to-all-start.3 = ((bf16[192,2,352]{2,1,0:T(2,128)(2,1)}), bf16[192,2,352]{2,1,0:T(2,128)(2,1)S(1)}, u32[]{:S(2)}, u32[]{:S(2)}) async-start(bf16[192,2,352]{2,1,0:T(2,128)(2,1)} %reshape.111), calls=%async_computation.3 | async-start | bytes 589824 | tf_op jit(solution)/shard_map/all_to_all | solution.py:113
  187.3 8.2 %all-to-all-done.3 = bf16[192,2,352]{2,1,0:T(2,128)(2,1)S(1)} async-done(((bf16[192,2,352]{2,1,0:T(2,128)(2,1)}), bf16[192,2,352]{2,1,0:T(2,128)(2,1)S(1)}, u32[]{:S(2)}, u32[]{:S(2)}) %all-to-all-start.3) | async-done | bytes 270368 | tf_op jit(solution)/shard_map/all_to_all | solution.py:113
  (165 shorter events, 54.2 us)
Async XLA Ops:
  9.9 15.0 %collective-permute-start = (bf16[16,4224]{1,0:T(8,128)(2,1)}, bf16[16,4224]{1,0:T(8,128)(2,1)}, u32[]{:S(2)}, u32[]{:S(2)}) collective-permute-start(bf16[16,4224]{1,0:T(8,128)(2,1)} %fusion), channel_id=1, source_target_pairs={{1,0},{2,1},{3,2},{5,4},{6,5},{7,6},{9,8},{10,9},{11,10},{13,12},{... | collective-permute-start | bytes 405512 | tf_op jit(solution)/shard_map/ppermute | solution.py:96
  14.1 21.9 %slice-start = ((s8[6488064]{0:T(1024)(128)(4,1)}), s8[2293760]{0:T(1024)(128)(4,1)S(1)}, s32[]{:S(2)}) async-start(s8[6488064]{0:T(1024)(128)(4,1)} %bitcast.120), calls=%async_computation.4 | async-start | bytes 4587520
  15.5 15.8 %collective-permute-start.1 = (bf16[16,4224]{1,0:T(8,128)(2,1)}, bf16[16,4224]{1,0:T(8,128)(2,1)}, u32[]{:S(2)}, u32[]{:S(2)}) collective-permute-start(bf16[16,4224]{1,0:T(8,128)(2,1)} %fusion.1), channel_id=1, source_target_pairs={{1,0},{2,1},{3,2},{5,4},{6,5},{7,6},{9,8},{10,9},{11,10},{13,12},{... | collective-permute-start | bytes 405512 | tf_op jit(solution)/shard_map/ppermute | solution.py:96
  19.2 49.9 %all-to-all-start.2 = ((bf16[8,128,256]{2,1,0:T(8,128)(2,1)}), bf16[8,128,256]{2,1,0:T(8,128)(2,1)}, u32[]{:S(2)}, u32[]{:S(2)}) async-start(bf16[8,128,256]{2,1,0:T(8,128)(2,1)} %broadcast_in_dim.18), calls=%async_computation.2 | async-start | bytes 1048576 | tf_op jit(solution)/shard_map/all_to_all | solution.py:63
  34.7 4.8 %collective-permute-start.2 = (bf16[16,4224]{1,0:T(8,128)(2,1)S(1)}, bf16[16,4224]{1,0:T(8,128)(2,1)S(1)}, u32[]{:S(2)}, u32[]{:S(2)}) collective-permute-start(bf16[16,4224]{1,0:T(8,128)(2,1)S(1)} %add_convert_fusion.11), channel_id=1, source_target_pairs={{1,0},{2,1},{3,2},{5,4},{6,5},{7,6},{9,8},{10,9},{11,10},{13,12},{... | collective-permute-start | bytes 405512 | tf_op jit(solution)/shard_map/ppermute | solution.py:96
  37.5 4.5 %collective-permute-start.3 = (bf16[16,4224]{1,0:T(8,128)(2,1)S(1)}, bf16[16,4224]{1,0:T(8,128)(2,1)S(1)}, u32[]{:S(2)}, u32[]{:S(2)}) collective-permute-start(bf16[16,4224]{1,0:T(8,128)(2,1)S(1)} %add_convert_fusion.10), channel_id=1, source_target_pairs={{1,0},{2,1},{3,2},{5,4},{6,5},{7,6},{9,8},{10,9},{11,10},{13,12},{... | collective-permute-start | bytes 405512 | tf_op jit(solution)/shard_map/ppermute | solution.py:96
  41.6 11.8 %copy-start.16 = (bf16[16,4224]{1,0:T(8,128)(2,1)}, bf16[16,4224]{1,0:T(8,128)(2,1)S(1)}, u32[]{:S(2)}) copy-start(bf16[16,4224]{1,0:T(8,128)(2,1)S(1)} %add_convert_fusion.9) | copy-start | bytes 405508
  42.0 11.4 %copy-start.6 = (bf16[16,4224]{1,0:T(8,128)(2,1)}, bf16[16,4224]{1,0:T(8,128)(2,1)S(1)}, u32[]{:S(2)}) copy-start(bf16[16,4224]{1,0:T(8,128)(2,1)S(1)} %add.96) | copy-start | bytes 405508
  42.7 10.0 %collective-permute-start.4 = (bf16[16,4224]{1,0:T(8,128)(2,1)S(1)}, bf16[16,4224]{1,0:T(8,128)(2,1)S(1)}, u32[]{:S(2)}, u32[]{:S(2)}) collective-permute-start(bf16[16,4224]{1,0:T(8,128)(2,1)S(1)} %add_convert_fusion.9), channel_id=1, source_target_pairs={{1,0},{2,1},{3,2},{5,4},{6,5},{7,6},{9,8},{10,9},{11,10},{13,12},{... | collective-permute-start | bytes 405512 | tf_op jit(solution)/shard_map/ppermute | solution.py:96
  49.1 6.4 %collective-permute-start.5 = (bf16[16,4224]{1,0:T(8,128)(2,1)S(1)}, bf16[16,4224]{1,0:T(8,128)(2,1)S(1)}, u32[]{:S(2)}, u32[]{:S(2)}) collective-permute-start(bf16[16,4224]{1,0:T(8,128)(2,1)S(1)} %add_convert_fusion.8), channel_id=1, source_target_pairs={{1,0},{2,1},{3,2},{5,4},{6,5},{7,6},{9,8},{10,9},{11,10},{13,12},{... | collective-permute-start | bytes 405512 | tf_op jit(solution)/shard_map/ppermute | solution.py:96
  56.2 16.4 %collective-permute-start.6 = (bf16[16,4224]{1,0:T(8,128)(2,1)}, bf16[16,4224]{1,0:T(8,128)(2,1)}, u32[]{:S(2)}, u32[]{:S(2)}) collective-permute-start(bf16[16,4224]{1,0:T(8,128)(2,1)} %add_convert_fusion.7), channel_id=1, source_target_pairs={{1,0},{2,1},{3,2},{5,4},{6,5},{7,6},{9,8},{10,9},{11,10},{13,12},{... | collective-permute-start | bytes 405512 | tf_op jit(solution)/shard_map/ppermute | solution.py:96
  63.5 16.5 %collective-permute-start.7 = (bf16[16,4224]{1,0:T(8,128)(2,1)}, bf16[16,4224]{1,0:T(8,128)(2,1)S(1)}, u32[]{:S(2)}, u32[]{:S(2)}) collective-permute-start(bf16[16,4224]{1,0:T(8,128)(2,1)} %add_convert_fusion.6), channel_id=1, source_target_pairs={{1,0},{2,1},{3,2},{5,4},{6,5},{7,6},{9,8},{10,9},{11,10},{13,12},{... | collective-permute-start | bytes 405512 | tf_op jit(solution)/shard_map/ppermute | solution.py:96
  69.1 21.0 %slice-start.2 = ((s8[6488064]{0:T(1024)(128)(4,1)}), s8[4194304]{0:T(1024)(128)(4,1)S(1)}, s32[]{:S(2)}) async-start(s8[6488064]{0:T(1024)(128)(4,1)} %bitcast.122), calls=%async_computation.6 | async-start | bytes 8388608
  75.0 15.2 %slice-start.3 = ((s8[6488064]{0:T(1024)(128)(4,1)}), s8[2293760]{0:T(1024)(128)(4,1)S(1)}, s32[]{:S(2)}) async-start(s8[6488064]{0:T(1024)(128)(4,1)} %bitcast.122), calls=%async_computation.7 | async-start | bytes 4587520
  78.1 12.1 %collective-permute-start.8 = (bf16[16,4224]{1,0:T(8,128)(2,1)S(1)}, bf16[16,4224]{1,0:T(8,128)(2,1)S(1)}, u32[]{:S(2)}, u32[]{:S(2)}) collective-permute-start(bf16[16,4224]{1,0:T(8,128)(2,1)S(1)} %add_convert_fusion.5), channel_id=1, source_target_pairs={{1,0},{2,1},{3,2},{5,4},{6,5},{7,6},{9,8},{10,9},{11,10},{13,12},{... | collective-permute-start | bytes 405512 | tf_op jit(solution)/shard_map/ppermute | solution.py:96
  85.2 10.3 %collective-permute-start.9 = (bf16[16,4224]{1,0:T(8,128)(2,1)S(1)}, bf16[16,4224]{1,0:T(8,128)(2,1)S(1)}, u32[]{:S(2)}, u32[]{:S(2)}) collective-permute-start(bf16[16,4224]{1,0:T(8,128)(2,1)S(1)} %add_convert_fusion.4), channel_id=1, source_target_pairs={{1,0},{2,1},{3,2},{5,4},{6,5},{7,6},{9,8},{10,9},{11,10},{13,12},{... | collective-permute-start | bytes 405512 | tf_op jit(solution)/shard_map/ppermute | solution.py:96
  92.4 27.9 %collective-permute-start.10 = (bf16[16,4224]{1,0:T(8,128)(2,1)S(1)}, bf16[16,4224]{1,0:T(8,128)(2,1)}, u32[]{:S(2)}, u32[]{:S(2)}) collective-permute-start(bf16[16,4224]{1,0:T(8,128)(2,1)S(1)} %add_convert_fusion.3), channel_id=1, source_target_pairs={{1,0},{2,1},{3,2},{5,4},{6,5},{7,6},{9,8},{10,9},{11,10},{13,12},{... | collective-permute-start | bytes 405512 | tf_op jit(solution)/shard_map/ppermute | solution.py:96
  97.7 14.0 %copy-start.29 = (bf16[16,4224]{1,0:T(8,128)(2,1)}, bf16[16,4224]{1,0:T(8,128)(2,1)S(1)}, u32[]{:S(2)}) copy-start(bf16[16,4224]{1,0:T(8,128)(2,1)S(1)} %add_convert_fusion.2) | copy-start | bytes 405508
  97.7 22.6 %collective-permute-start.11 = (bf16[16,4224]{1,0:T(8,128)(2,1)S(1)}, bf16[16,4224]{1,0:T(8,128)(2,1)}, u32[]{:S(2)}, u32[]{:S(2)}) collective-permute-start(bf16[16,4224]{1,0:T(8,128)(2,1)S(1)} %add_convert_fusion.2), channel_id=1, source_target_pairs={{1,0},{2,1},{3,2},{5,4},{6,5},{7,6},{9,8},{10,9},{11,10},{13,12},{... | collective-permute-start | bytes 405512 | tf_op jit(solution)/shard_map/ppermute | solution.py:96
  111.7 20.5 %all-to-all-start = ((bf16[8,96,528]{2,1,0:T(8,128)(2,1)}), bf16[8,96,528]{2,1,0:T(8,128)(2,1)S(1)}, u32[]{:S(2)}, u32[]{:S(2)}) async-start(bf16[8,96,528]{2,1,0:T(8,128)(2,1)} %copy.19), calls=%async_computation | async-start | bytes 1966080 | tf_op jit(solution)/shard_map/all_to_all | solution.py:27
  132.2 12.2 %all-to-all-start.1 = ((bf16[8,32,528]{2,1,0:T(8,128)(2,1)}), bf16[8,32,528]{2,1,0:T(8,128)(2,1)}, u32[]{:S(2)}, u32[]{:S(2)}) async-start(bf16[8,32,528]{2,1,0:T(8,128)(2,1)} %reshape.106), calls=%async_computation.1 | async-start | bytes 655360 | tf_op jit(solution)/shard_map/all_to_all | solution.py:27
  143.1 34.7 %copy-start.17 = (bf16[16,4224]{1,0:T(8,128)(2,1)S(1)}, bf16[16,4224]{1,0:T(8,128)(2,1)}, u32[]{:S(2)}) copy-start(bf16[16,4224]{1,0:T(8,128)(2,1)} %copy-done.16) | copy-start | bytes 405508
  143.1 34.7 %copy-start.24 = (bf16[16,4224]{1,0:T(8,128)(2,1)S(1)}, bf16[16,4224]{1,0:T(8,128)(2,1)}, u32[]{:S(2)}) copy-start(bf16[16,4224]{1,0:T(8,128)(2,1)} %copy-done.23) | copy-start | bytes 405508
  143.1 36.3 %copy-start.19 = (bf16[16,4224]{1,0:T(8,128)(2,1)S(1)}, bf16[16,4224]{1,0:T(8,128)(2,1)}, u32[]{:S(2)}) copy-start(bf16[16,4224]{1,0:T(8,128)(2,1)} %copy-done.18) | copy-start | bytes 405508
  143.1 38.7 %copy-start.21 = (bf16[16,4224]{1,0:T(8,128)(2,1)S(1)}, bf16[16,4224]{1,0:T(8,128)(2,1)}, u32[]{:S(2)}) copy-start(bf16[16,4224]{1,0:T(8,128)(2,1)} %copy-done.20) | copy-start | bytes 405508
  143.7 35.8 %copy-start.26 = (bf16[16,4224]{1,0:T(8,128)(2,1)S(1)}, bf16[16,4224]{1,0:T(8,128)(2,1)}, u32[]{:S(2)}) copy-start(bf16[16,4224]{1,0:T(8,128)(2,1)} %copy-done.25) | copy-start | bytes 405508
  143.7 38.9 %copy-start.28 = (bf16[16,4224]{1,0:T(8,128)(2,1)S(1)}, bf16[16,4224]{1,0:T(8,128)(2,1)}, u32[]{:S(2)}) copy-start(bf16[16,4224]{1,0:T(8,128)(2,1)} %copy-done.27) | copy-start | bytes 405508
  143.7 39.6 %copy-start.30 = (bf16[16,4224]{1,0:T(8,128)(2,1)S(1)}, bf16[16,4224]{1,0:T(8,128)(2,1)}, u32[]{:S(2)}) copy-start(bf16[16,4224]{1,0:T(8,128)(2,1)} %copy-done.29) | copy-start | bytes 405508
  144.4 39.6 %copy-start.35 = (bf16[16,4224]{1,0:T(8,128)(2,1)S(1)}, bf16[16,4224]{1,0:T(8,128)(2,1)}, u32[]{:S(2)}) copy-start(bf16[16,4224]{1,0:T(8,128)(2,1)} %add_convert_fusion.1) | copy-start | bytes 405508
  147.9 48.4 %copy-start.36 = (f32[1,5632]{1,0:T(1,128)S(1)}, f32[1,5632]{1,0:T(1,128)}, u32[]{:S(2)}) copy-start(f32[1,5632]{1,0:T(1,128)} %param.9) | copy-start | bytes 67588
  147.9 48.4 %copy-start.37 = (f32[1,5632]{1,0:T(1,128)S(1)}, f32[1,5632]{1,0:T(1,128)}, u32[]{:S(2)}) copy-start(f32[1,5632]{1,0:T(1,128)} %param.8) | copy-start | bytes 67588
  150.3 45.2 %all-to-all-start.3 = ((bf16[192,2,352]{2,1,0:T(2,128)(2,1)}), bf16[192,2,352]{2,1,0:T(2,128)(2,1)S(1)}, u32[]{:S(2)}, u32[]{:S(2)}) async-start(bf16[192,2,352]{2,1,0:T(2,128)(2,1)} %reshape.111), calls=%async_computation.3 | async-start | bytes 589824 | tf_op jit(solution)/shard_map/all_to_all | solution.py:113
  (26 other events, 195.8 us)

commit v5 on v4

--- a/solution.py
+++ b/solution.py
@@ -20,12 +20,9 @@
     return lax.dot_general(left, right, (((1,), (1,)), ((), ())), preferred_element_type=F32)
 
 
-def to_side(rows):
-    count = lax.axis_size(SIDE)
+def side_parts(rows, count):
     parts = rows.reshape(rows.shape[0], 3, count, -1).transpose(2, 0, 1, 3)
-    parts = parts.reshape(count, rows.shape[0], -1)
-    parts = lax.all_to_all(parts, SIDE, 0, 0, tiled=True)
-    return parts.reshape(-1, parts.shape[2])
+    return parts.reshape(count, rows.shape[0], -1)
 
 
 def step(acts, out_grad, params, moment, second):
@@ -59,6 +56,9 @@
         (first_chunk, jnp.uint32(0)),
         (ticks * rows, 2 * block),
     )
+    factors = lax.optimization_barrier(
+        [factors[tick * rows : (tick + 1) * rows] for tick in range(ticks)]
+    )
     copies = jnp.broadcast_to(hidden[None], (side,) + hidden.shape)
     hidden = lax.all_to_all(copies, SIDE, 0, 0, tiled=True)
     top = jnp.where(is_section[lead], top, 0)
@@ -66,8 +66,6 @@
         [top[chunk * rows : (chunk + 1) * rows] for chunk in range(CHUNKS)]
     )
     down = [(s, s - 1) for s in range(1, sections)]
-    cuts = (0, CHUNKS - 2, CHUNKS)
-
     def own(values, count):
         chunks = []
         for chunk in range(count):
@@ -80,32 +78,28 @@
     moved = []
     grads = []
     passes = []
-    sides = []
+    parts = []
     for tick in range(ticks):
         grad = None if tick < DEPTH else moved[tick - DEPTH]
         if tick < CHUNKS:
             grad = tops[tick] if grad is None else grad + tops[tick]
         grads.append(grad)
         d_hidden = cols_dot(grad, weights_down)
-        part = factors[tick * rows : (tick + 1) * rows]
-        d_gate_up = (jnp.concatenate([d_hidden, d_hidden], axis=1) * part).astype(BF16)
+        d_gate_up = jnp.concatenate([d_hidden, d_hidden], axis=1) * factors[tick]
+        d_gate_up = d_gate_up.astype(BF16)
         passed = grad.astype(F32) + jnp.dot(d_gate_up, weights_in, preferred_element_type=F32)
         passed = passed.astype(BF16)
         passes.append(passed)
         if tick + DEPTH < ticks:
             moved.append(lax.ppermute(passed, "pipe", down))
         done = tick + 1 - DEPTH * lead
-        if done in cuts[1:]:
-            begin = cuts[len(sides)]
-            seen, _ = lax.optimization_barrier((grads[begin:], passed if done < CHUNKS else grad))
-            arrived = own(seen, done - begin)
-            sides.append(to_side(arrived))
-
-    passes, sides = lax.optimization_barrier((passes, sides))
-    terms = 0.0
-    for begin, end, rows_of_side in zip(cuts[:-1], cuts[1:], sides):
-        part = hidden[:, begin * rows : end * rows].reshape(-1, block)
-        terms = terms + rows_dot(part, rows_of_side)
+        if done == CHUNKS - DEPTH or done == CHUNKS:
+            begin = len(parts) * (CHUNKS - DEPTH)
+            seen, _ = lax.optimization_barrier((grads[begin:], passed if begin == 0 else grad))
+            parts.append(side_parts(own(seen, done - begin), side))
+    arrived = lax.all_to_all(jnp.concatenate(parts, axis=1), SIDE, 0, 0, tiled=True)
+    passes, arrived = lax.optimization_barrier((passes, arrived))
+    terms = rows_dot(hidden.reshape(-1, block), arrived.reshape(-1, arrived.shape[2]))
 
     in_grads = own(passes, CHUNKS)
 

time: 199 us -> 188 us (0.945)
  matrix products: 57.3 us -> 33.2 us
  starting transfers between devices: 90 us -> 104 us
  waiting for transfers between devices: 10.9 us -> 20.4 us
  other arithmetic: 19 us -> 13.6 us
  local copies, waits for them, and re-layouts: 18.5 us -> 14.8 us
    dot_general x14, matrix products: 30.5 us -> 15.5 us  [step(): jnp.dot(d_gate_up, weights_in, preferred_element_type=F32)]
    ppermute x12, starting transfers between devices: 41.1 us -> 54 us  [step(): moved.append(lax.ppermute(passed, 'pipe', down))]
    dot_general x15, matrix products: 23.3 us -> 16 us  [cols_dot(): lax.dot_general(left, right, (((1,), (1,)), ((), ())), preferred_element_...]
    all_to_all x2 -> x1, waiting for transfers between devices: 2.31 us -> 7.64 us  [step(): lax.all_to_all(jnp.concatenate(parts, axis=1), SIDE, 0, 0, tiled=True)]
    all_to_all x1, waiting for transfers between devices: 8.21 us -> 11.8 us  [step(): terms = lax.all_to_all(terms, DP, 0, 0, tiled=True)]
    reshape x6 -> x2, local copies, waits for them, and re-layouts: 7.76 us -> 4.34 us  [side_parts(): parts = rows.reshape(rows.shape[0], 3, count, -1).transpose(2, 0, 1, 3)]
    slice x2 -> x1, local copies, waits for them, and re-layouts: 3.51 us -> 0.66 us  [step(): factors[tick * rows:(tick + 1) * rows]]
    unnamed x84 -> x70, local copies, waits for them, and re-layouts: 0.27 us -> 3.04 us
  transfers between devices with their start and end apart: 16 -> 15, of which waited for: 4 -> 3; matrix products, arithmetic and copies ran while one was open for 40% -> 22% of each run, Pallas kernels for 0% -> 0%
where the time goes in v5:
time: 188 us; the launch traced here: 187 us
  starting transfers between devices  104 us (55%)
  matrix products  33.2 us (18%)
  waiting for transfers between devices  20.4 us (11%)
  local copies, waits for them, and re-layouts  14.8 us (8%)
  other arithmetic  13.6 us (7%)
    ppermute x12, starting transfers between devices, step(): moved.append(lax.ppermute(passed, 'pipe', down))  54 us
    all_to_all x1, starting transfers between devices, step(): terms = lax.all_to_all(terms, DP, 0, 0, tiled=True)  28.5 us
    dot_general x15, matrix products, cols_dot(): lax.dot_general(left, right, (((1,), (1,)), ((), ())), preferred_element_...  16 us
    dot_general x14, matrix products, step(): jnp.dot(d_gate_up, weights_in, preferred_element_type=F32)  15.5 us
    all_to_all x1, starting transfers between devices, step(): lax.all_to_all(jnp.concatenate(parts, axis=1), SIDE, 0, 0, tiled=True)  13.8 us
    all_to_all x1, waiting for transfers between devices, step(): terms = lax.all_to_all(terms, DP, 0, 0, tiled=True)  11.8 us
    unnamed x12, other arithmetic  8.75 us
    all_to_all x1, waiting for transfers between devices, step(): lax.all_to_all(jnp.concatenate(parts, axis=1), SIDE, 0, 0, tiled=True)  7.64 us
  transfers between devices with their start and end apart: 15, of which 3 were waited for; matrix products, arithmetic and copies ran while one was open for 22% of the time, Pallas kernels for 0%

profile of v5, /device:TPU:61, one launch (start us, length us, event | category | flops | bytes accessed | tf_op | source)
XLA Modules:
  0.0 187.1 jit_solution(12791462899890922733)
XLA Ops:
  0.7 1.2 copy-done
  1.9 3.8 %fusion.28 = f32[128,512]{1,0:T(8,128)S(1)} fusion(bf16[128,4224]{1,0:T(8,128)(2,1)S(1)} %bitcast.116, bf16[1,768,4224]{2,1,0:T(8,128)(2,1)} %param.7), kind=kOutput, calls=%fused_computation.30 | convolution fusion | flops 553648128 | bytes 5668864 | tf_op jit(solution)/shard_map/dot_general | solution.py:20
  7.0 1.6 copy-done.1
  9.9 3.8 %collective-permute-start.1 = (bf16[16,4224]{1,0:T(8,128)(2,1)S(1)}, bf16[16,4224]{1,0:T(8,128)(2,1)S(1)}, u32[]{:S(2)}, u32[]{:S(2)}) collective-permute-start(bf16[16,4224]{1,0:T(8,128)(2,1)S(1)} %fusion.1), channel_id=1, source_target_pairs={{1,0},{2,1},{3,2},{5,4},{6,5},{7,6},{9,8},{10,9},{11,10},{13,12},{... | collective-permute-start | bytes 405512 | tf_op jit(solution)/shard_map/ppermute | solution.py:94
  15.1 2.9 %collective-permute-start = (bf16[16,4224]{1,0:T(8,128)(2,1)S(1)}, bf16[16,4224]{1,0:T(8,128)(2,1)S(1)}, u32[]{:S(2)}, u32[]{:S(2)}) collective-permute-start(bf16[16,4224]{1,0:T(8,128)(2,1)S(1)} %fusion), channel_id=1, source_target_pairs={{1,0},{2,1},{3,2},{5,4},{6,5},{7,6},{9,8},{10,9},{11,10},{13,12},{... | collective-permute-start | bytes 405512 | tf_op jit(solution)/shard_map/ppermute | solution.py:94
  19.4 3.1 %collective-permute-start.3 = (bf16[16,4224]{1,0:T(8,128)(2,1)S(1)}, bf16[16,4224]{1,0:T(8,128)(2,1)S(1)}, u32[]{:S(2)}, u32[]{:S(2)}) collective-permute-start(bf16[16,4224]{1,0:T(8,128)(2,1)S(1)} %add_convert_fusion.10), channel_id=1, source_target_pairs={{1,0},{2,1},{3,2},{5,4},{6,5},{7,6},{9,8},{10,9},{11,10},{13,12},{... | collective-permute-start | bytes 405512 | tf_op jit(solution)/shard_map/ppermute | solution.py:94
  23.9 4.3 %collective-permute-start.2 = (bf16[16,4224]{1,0:T(8,128)(2,1)S(1)}, bf16[16,4224]{1,0:T(8,128)(2,1)S(1)}, u32[]{:S(2)}, u32[]{:S(2)}) collective-permute-start(bf16[16,4224]{1,0:T(8,128)(2,1)S(1)} %add_convert_fusion.11), channel_id=1, source_target_pairs={{1,0},{2,1},{3,2},{5,4},{6,5},{7,6},{9,8},{10,9},{11,10},{13,12},{... | collective-permute-start | bytes 405512 | tf_op jit(solution)/shard_map/ppermute | solution.py:94
  29.7 3.2 %collective-permute-start.5 = (bf16[16,4224]{1,0:T(8,128)(2,1)S(1)}, bf16[16,4224]{1,0:T(8,128)(2,1)S(1)}, u32[]{:S(2)}, u32[]{:S(2)}) collective-permute-start(bf16[16,4224]{1,0:T(8,128)(2,1)S(1)} %add_convert_fusion.8), channel_id=1, source_target_pairs={{1,0},{2,1},{3,2},{5,4},{6,5},{7,6},{9,8},{10,9},{11,10},{13,12},{... | collective-permute-start | bytes 405512 | tf_op jit(solution)/shard_map/ppermute | solution.py:94
  34.3 4.3 %collective-permute-start.4 = (bf16[16,4224]{1,0:T(8,128)(2,1)S(1)}, bf16[16,4224]{1,0:T(8,128)(2,1)S(1)}, u32[]{:S(2)}, u32[]{:S(2)}) collective-permute-start(bf16[16,4224]{1,0:T(8,128)(2,1)S(1)} %add_convert_fusion.9), channel_id=1, source_target_pairs={{1,0},{2,1},{3,2},{5,4},{6,5},{7,6},{9,8},{10,9},{11,10},{13,12},{... | collective-permute-start | bytes 405512 | tf_op jit(solution)/shard_map/ppermute | solution.py:94
  40.0 5.0 %collective-permute-start.7 = (bf16[16,4224]{1,0:T(8,128)(2,1)S(1)}, bf16[16,4224]{1,0:T(8,128)(2,1)S(1)}, u32[]{:S(2)}, u32[]{:S(2)}) collective-permute-start(bf16[16,4224]{1,0:T(8,128)(2,1)S(1)} %add_convert_fusion.6), channel_id=1, source_target_pairs={{1,0},{2,1},{3,2},{5,4},{6,5},{7,6},{9,8},{10,9},{11,10},{13,12},{... | collective-permute-start | bytes 405512 | tf_op jit(solution)/shard_map/ppermute | solution.py:94
  46.4 4.6 %collective-permute-start.6 = (bf16[16,4224]{1,0:T(8,128)(2,1)S(1)}, bf16[16,4224]{1,0:T(8,128)(2,1)S(1)}, u32[]{:S(2)}, u32[]{:S(2)}) collective-permute-start(bf16[16,4224]{1,0:T(8,128)(2,1)S(1)} %add_convert_fusion.7), channel_id=1, source_target_pairs={{1,0},{2,1},{3,2},{5,4},{6,5},{7,6},{9,8},{10,9},{11,10},{13,12},{... | collective-permute-start | bytes 405512 | tf_op jit(solution)/shard_map/ppermute | solution.py:94
  52.3 6.2 %collective-permute-start.9 = (bf16[16,4224]{1,0:T(8,128)(2,1)S(1)}, bf16[16,4224]{1,0:T(8,128)(2,1)S(1)}, u32[]{:S(2)}, u32[]{:S(2)}) collective-permute-start(bf16[16,4224]{1,0:T(8,128)(2,1)S(1)} %add_convert_fusion.4), channel_id=1, source_target_pairs={{1,0},{2,1},{3,2},{5,4},{6,5},{7,6},{9,8},{10,9},{11,10},{13,12},{... | collective-permute-start | bytes 405512 | tf_op jit(solution)/shard_map/ppermute | solution.py:94
  59.9 5.5 %collective-permute-start.8 = (bf16[16,4224]{1,0:T(8,128)(2,1)S(1)}, bf16[16,4224]{1,0:T(8,128)(2,1)S(1)}, u32[]{:S(2)}, u32[]{:S(2)}) collective-permute-start(bf16[16,4224]{1,0:T(8,128)(2,1)S(1)} %add_convert_fusion.5), channel_id=1, source_target_pairs={{1,0},{2,1},{3,2},{5,4},{6,5},{7,6},{9,8},{10,9},{11,10},{13,12},{... | collective-permute-start | bytes 405512 | tf_op jit(solution)/shard_map/ppermute | solution.py:94
  66.8 6.9 %collective-permute-start.11 = (bf16[16,4224]{1,0:T(8,128)(2,1)S(1)}, bf16[16,4224]{1,0:T(8,128)(2,1)}, u32[]{:S(2)}, u32[]{:S(2)}) collective-permute-start(bf16[16,4224]{1,0:T(8,128)(2,1)S(1)} %add_convert_fusion.2), channel_id=1, source_target_pairs={{1,0},{2,1},{3,2},{5,4},{6,5},{7,6},{9,8},{10,9},{11,10},{13,12},{... | collective-permute-start | bytes 405512 | tf_op jit(solution)/shard_map/ppermute | solution.py:94
  75.1 4.5 %collective-permute-start.10 = (bf16[16,4224]{1,0:T(8,128)(2,1)S(1)}, bf16[16,4224]{1,0:T(8,128)(2,1)S(1)}, u32[]{:S(2)}, u32[]{:S(2)}) collective-permute-start(bf16[16,4224]{1,0:T(8,128)(2,1)S(1)} %add_convert_fusion.3), channel_id=1, source_target_pairs={{1,0},{2,1},{3,2},{5,4},{6,5},{7,6},{9,8},{10,9},{11,10},{13,12},{... | collective-permute-start | bytes 405512 | tf_op jit(solution)/shard_map/ppermute | solution.py:94
  83.9 3.0 %reshape.92 = bf16[96,3,8,176]{3,2,1,0:T(8,128)(2,1)S(1)} reshape(bf16[96,4224]{1,0:T(8,128)(2,1)} %select_dynamic-update-slice_fusion.8) | data formatting | bytes 1622016 | tf_op jit(solution)/shard_map/reshape | solution.py:24
  86.9 2.3 %copy.13 = bf16[8,96,3,176]{1,3,2,0:T(8,128)(2,1)} copy(bf16[8,96,3,176]{3,0,2,1:T(8,128)(2,1)S(1)} %bitcast.117) | data formatting | bytes 1622016 | tf_op jit(solution)/shard_map/transpose | solution.py:24
  89.4 1.4 reshape.94
  90.8 1.5 copy.14
  92.3 1.6 pad_maximum_fusion
  93.9 13.8 %all-to-all-start = ((bf16[8,128,528]{1,2,0:T(8,128)(2,1)}), bf16[8,128,528]{1,2,0:T(8,128)(2,1)S(1)}, u32[]{:S(2)}, u32[]{:S(2)}) async-start(bf16[8,128,528]{1,2,0:T(8,128)(2,1)} %pad_maximum_fusion), calls=%async_computation | async-start | bytes 2162688 | tf_op jit(solution)/shard_map/all_to_all | solution.py:100
  107.7 2.4 %fusion.30 = f32[16,256]{1,0:T(8,128)S(1)} fusion(bf16[16,4224]{1,0:T(8,128)(2,1)} %collective-permute-done.11, bf16[1,768,4224]{2,1,0:T(8,128)(2,1)} %param.7), kind=kOutput, calls=%fused_computation.32 | convolution fusion | flops 34603008 | bytes 2314240 | tf_op jit(solution)/shard_map/dot_general | solution.py:20
  110.0 3.0 %add_convert_fusion = bf16[16,4224]{1,0:T(8,128)(2,1)S(1)} fusion(bf16[16,4224]{1,0:T(8,128)(2,1)} %collective-permute-done.11, f32[16,512]{1,0:T(8,128)} %get-tuple-element.92, f32[16,256]{1,0:T(8,128)S(1)} %fusion.30, bf16[1,768,4224]{2,1,0:T(8,128)(2,1)} %param.7), kind=kOutput, calls=%fused_computation.73 | convolution fusion | flops 69433344 | bytes 4644864 | tf_op jit(solution)/shard_map/dot_general | solution.py:90
  113.0 7.6 %all-to-all-done = bf16[8,128,528]{1,2,0:T(8,128)(2,1)S(1)} async-done(((bf16[8,128,528]{1,2,0:T(8,128)(2,1)}), bf16[8,128,528]{1,2,0:T(8,128)(2,1)S(1)}, u32[]{:S(2)}, u32[]{:S(2)}) %all-to-all-start) | async-done | bytes 1081376 | tf_op jit(solution)/shard_map/all_to_all | solution.py:100
  121.5 7.4 %all-to-all-start.1 = ((bf16[8,128,256]{2,1,0:T(8,128)(2,1)}), bf16[8,128,256]{2,1,0:T(8,128)(2,1)}, u32[]{:S(2)}, u32[]{:S(2)}) async-start(bf16[8,128,256]{2,1,0:T(8,128)(2,1)} %broadcast_in_dim.18), calls=%async_computation.1 | async-start | bytes 1048576 | tf_op jit(solution)/shard_map/all_to_all | solution.py:63
  128.9 2.2 %fusion.32 = f32[16,256]{1,0:T(8,128)S(1)} fusion(bf16[16,4224]{1,0:T(8,128)(2,1)S(1)} %copy-done.24, bf16[1,768,4224]{2,1,0:T(8,128)(2,1)} %param.7), kind=kOutput, calls=%fused_computation.34 | convolution fusion | flops 34603008 | bytes 2314240 | tf_op jit(solution)/shard_map/dot_general | solution.py:20
  131.3 3.7 %add_convert_fusion.1 = bf16[16,4224]{1,0:T(8,128)(2,1)} fusion(bf16[16,4224]{1,0:T(8,128)(2,1)S(1)} %copy-done.24, f32[16,512]{1,0:T(8,128)S(1)} %copy-done.32, f32[16,256]{1,0:T(8,128)S(1)} %fusion.32, bf16[1,768,4224]{2,1,0:T(8,128)(2,1)} %param.7), kind=kOutput, calls=%fused_computation.74 | convolution fusion | flops 69433344 | bytes 4644864 | tf_op jit(solution)/shard_map/dot_general | solution.py:90
  135.0 0.9 all-to-all-done.1
  135.9 1.8 fusion.58
  138.0 1.3 reshape.97
  139.3 28.5 %all-to-all-start.2 = ((bf16[192,2,352]{2,1,0:T(2,128)(2,1)}), bf16[192,2,352]{2,1,0:T(2,128)(2,1)S(1)}, u32[]{:S(2)}, u32[]{:S(2)}) async-start(bf16[192,2,352]{2,1,0:T(2,128)(2,1)} %reshape.97), calls=%async_computation.2 | async-start | bytes 589824 | tf_op jit(solution)/shard_map/all_to_all | solution.py:107
  173.7 11.8 %all-to-all-done.2 = bf16[192,2,352]{2,1,0:T(2,128)(2,1)S(1)} async-done(((bf16[192,2,352]{2,1,0:T(2,128)(2,1)}), bf16[192,2,352]{2,1,0:T(2,128)(2,1)S(1)}, u32[]{:S(2)}, u32[]{:S(2)}) %all-to-all-start.2) | async-done | bytes 270368 | tf_op jit(solution)/shard_map/all_to_all | solution.py:107
  (143 shorter events, 30.9 us)
Async XLA Ops:
  9.9 8.0 %collective-permute-start.1 = (bf16[16,4224]{1,0:T(8,128)(2,1)S(1)}, bf16[16,4224]{1,0:T(8,128)(2,1)S(1)}, u32[]{:S(2)}, u32[]{:S(2)}) collective-permute-start(bf16[16,4224]{1,0:T(8,128)(2,1)S(1)} %fusion.1), channel_id=1, source_target_pairs={{1,0},{2,1},{3,2},{5,4},{6,5},{7,6},{9,8},{10,9},{11,10},{13,12},{... | collective-permute-start | bytes 405512 | tf_op jit(solution)/shard_map/ppermute | solution.py:94
  15.1 7.4 %collective-permute-start = (bf16[16,4224]{1,0:T(8,128)(2,1)S(1)}, bf16[16,4224]{1,0:T(8,128)(2,1)S(1)}, u32[]{:S(2)}, u32[]{:S(2)}) collective-permute-start(bf16[16,4224]{1,0:T(8,128)(2,1)S(1)} %fusion), channel_id=1, source_target_pairs={{1,0},{2,1},{3,2},{5,4},{6,5},{7,6},{9,8},{10,9},{11,10},{13,12},{... | collective-permute-start | bytes 405512 | tf_op jit(solution)/shard_map/ppermute | solution.py:94
  19.4 8.9 %collective-permute-start.3 = (bf16[16,4224]{1,0:T(8,128)(2,1)S(1)}, bf16[16,4224]{1,0:T(8,128)(2,1)S(1)}, u32[]{:S(2)}, u32[]{:S(2)}) collective-permute-start(bf16[16,4224]{1,0:T(8,128)(2,1)S(1)} %add_convert_fusion.10), channel_id=1, source_target_pairs={{1,0},{2,1},{3,2},{5,4},{6,5},{7,6},{9,8},{10,9},{11,10},{13,12},{... | collective-permute-start | bytes 405512 | tf_op jit(solution)/shard_map/ppermute | solution.py:94
  23.9 8.9 %collective-permute-start.2 = (bf16[16,4224]{1,0:T(8,128)(2,1)S(1)}, bf16[16,4224]{1,0:T(8,128)(2,1)S(1)}, u32[]{:S(2)}, u32[]{:S(2)}) collective-permute-start(bf16[16,4224]{1,0:T(8,128)(2,1)S(1)} %add_convert_fusion.11), channel_id=1, source_target_pairs={{1,0},{2,1},{3,2},{5,4},{6,5},{7,6},{9,8},{10,9},{11,10},{13,12},{... | collective-permute-start | bytes 405512 | tf_op jit(solution)/shard_map/ppermute | solution.py:94
  29.7 8.9 %collective-permute-start.5 = (bf16[16,4224]{1,0:T(8,128)(2,1)S(1)}, bf16[16,4224]{1,0:T(8,128)(2,1)S(1)}, u32[]{:S(2)}, u32[]{:S(2)}) collective-permute-start(bf16[16,4224]{1,0:T(8,128)(2,1)S(1)} %add_convert_fusion.8), channel_id=1, source_target_pairs={{1,0},{2,1},{3,2},{5,4},{6,5},{7,6},{9,8},{10,9},{11,10},{13,12},{... | collective-permute-start | bytes 405512 | tf_op jit(solution)/shard_map/ppermute | solution.py:94
  34.3 10.7 %collective-permute-start.4 = (bf16[16,4224]{1,0:T(8,128)(2,1)S(1)}, bf16[16,4224]{1,0:T(8,128)(2,1)S(1)}, u32[]{:S(2)}, u32[]{:S(2)}) collective-permute-start(bf16[16,4224]{1,0:T(8,128)(2,1)S(1)} %add_convert_fusion.9), channel_id=1, source_target_pairs={{1,0},{2,1},{3,2},{5,4},{6,5},{7,6},{9,8},{10,9},{11,10},{13,12},{... | collective-permute-start | bytes 405512 | tf_op jit(solution)/shard_map/ppermute | solution.py:94
  40.0 11.0 %collective-permute-start.7 = (bf16[16,4224]{1,0:T(8,128)(2,1)S(1)}, bf16[16,4224]{1,0:T(8,128)(2,1)S(1)}, u32[]{:S(2)}, u32[]{:S(2)}) collective-permute-start(bf16[16,4224]{1,0:T(8,128)(2,1)S(1)} %add_convert_fusion.6), channel_id=1, source_target_pairs={{1,0},{2,1},{3,2},{5,4},{6,5},{7,6},{9,8},{10,9},{11,10},{13,12},{... | collective-permute-start | bytes 405512 | tf_op jit(solution)/shard_map/ppermute | solution.py:94
  46.4 12.2 %collective-permute-start.6 = (bf16[16,4224]{1,0:T(8,128)(2,1)S(1)}, bf16[16,4224]{1,0:T(8,128)(2,1)S(1)}, u32[]{:S(2)}, u32[]{:S(2)}) collective-permute-start(bf16[16,4224]{1,0:T(8,128)(2,1)S(1)} %add_convert_fusion.7), channel_id=1, source_target_pairs={{1,0},{2,1},{3,2},{5,4},{6,5},{7,6},{9,8},{10,9},{11,10},{13,12},{... | collective-permute-start | bytes 405512 | tf_op jit(solution)/shard_map/ppermute | solution.py:94
  52.3 13.1 %collective-permute-start.9 = (bf16[16,4224]{1,0:T(8,128)(2,1)S(1)}, bf16[16,4224]{1,0:T(8,128)(2,1)S(1)}, u32[]{:S(2)}, u32[]{:S(2)}) collective-permute-start(bf16[16,4224]{1,0:T(8,128)(2,1)S(1)} %add_convert_fusion.4), channel_id=1, source_target_pairs={{1,0},{2,1},{3,2},{5,4},{6,5},{7,6},{9,8},{10,9},{11,10},{13,12},{... | collective-permute-start | bytes 405512 | tf_op jit(solution)/shard_map/ppermute | solution.py:94
  59.9 13.8 %collective-permute-start.8 = (bf16[16,4224]{1,0:T(8,128)(2,1)S(1)}, bf16[16,4224]{1,0:T(8,128)(2,1)S(1)}, u32[]{:S(2)}, u32[]{:S(2)}) collective-permute-start(bf16[16,4224]{1,0:T(8,128)(2,1)S(1)} %add_convert_fusion.5), channel_id=1, source_target_pairs={{1,0},{2,1},{3,2},{5,4},{6,5},{7,6},{9,8},{10,9},{11,10},{13,12},{... | collective-permute-start | bytes 405512 | tf_op jit(solution)/shard_map/ppermute | solution.py:94
  66.8 22.4 %collective-permute-start.11 = (bf16[16,4224]{1,0:T(8,128)(2,1)S(1)}, bf16[16,4224]{1,0:T(8,128)(2,1)}, u32[]{:S(2)}, u32[]{:S(2)}) collective-permute-start(bf16[16,4224]{1,0:T(8,128)(2,1)S(1)} %add_convert_fusion.2), channel_id=1, source_target_pairs={{1,0},{2,1},{3,2},{5,4},{6,5},{7,6},{9,8},{10,9},{11,10},{13,12},{... | collective-permute-start | bytes 405512 | tf_op jit(solution)/shard_map/ppermute | solution.py:94
  75.1 14.2 %collective-permute-start.10 = (bf16[16,4224]{1,0:T(8,128)(2,1)S(1)}, bf16[16,4224]{1,0:T(8,128)(2,1)S(1)}, u32[]{:S(2)}, u32[]{:S(2)}) collective-permute-start(bf16[16,4224]{1,0:T(8,128)(2,1)S(1)} %add_convert_fusion.3), channel_id=1, source_target_pairs={{1,0},{2,1},{3,2},{5,4},{6,5},{7,6},{9,8},{10,9},{11,10},{13,12},{... | collective-permute-start | bytes 405512 | tf_op jit(solution)/shard_map/ppermute | solution.py:94
  93.9 26.8 %all-to-all-start = ((bf16[8,128,528]{1,2,0:T(8,128)(2,1)}), bf16[8,128,528]{1,2,0:T(8,128)(2,1)S(1)}, u32[]{:S(2)}, u32[]{:S(2)}) async-start(bf16[8,128,528]{1,2,0:T(8,128)(2,1)} %pad_maximum_fusion), calls=%async_computation | async-start | bytes 2162688 | tf_op jit(solution)/shard_map/all_to_all | solution.py:100
  107.7 21.3 %copy-start.24 = (bf16[16,4224]{1,0:T(8,128)(2,1)S(1)}, bf16[16,4224]{1,0:T(8,128)(2,1)}, u32[]{:S(2)}) copy-start(bf16[16,4224]{1,0:T(8,128)(2,1)} %copy-done.23) | copy-start | bytes 405508
  110.0 21.1 %copy-start.32 = (f32[16,512]{1,0:T(8,128)S(1)}, f32[16,512]{1,0:T(8,128)}, u32[]{:S(2)}) copy-start(f32[16,512]{1,0:T(8,128)} %get-tuple-element.91) | copy-start | bytes 98308
  121.5 14.4 %all-to-all-start.1 = ((bf16[8,128,256]{2,1,0:T(8,128)(2,1)}), bf16[8,128,256]{2,1,0:T(8,128)(2,1)}, u32[]{:S(2)}, u32[]{:S(2)}) async-start(bf16[8,128,256]{2,1,0:T(8,128)(2,1)} %broadcast_in_dim.18), calls=%async_computation.1 | async-start | bytes 1048576 | tf_op jit(solution)/shard_map/all_to_all | solution.py:63
  131.2 36.7 %copy-start.6 = (bf16[16,4224]{1,0:T(8,128)(2,1)S(1)}, bf16[16,4224]{1,0:T(8,128)(2,1)}, u32[]{:S(2)}) copy-start(bf16[16,4224]{1,0:T(8,128)(2,1)} %copy-done.5) | copy-start | bytes 405508
  131.2 36.6 %copy-start.10 = (bf16[16,4224]{1,0:T(8,128)(2,1)S(1)}, bf16[16,4224]{1,0:T(8,128)(2,1)}, u32[]{:S(2)}) copy-start(bf16[16,4224]{1,0:T(8,128)(2,1)} %copy-done.9) | copy-start | bytes 405508
  131.2 36.6 %copy-start.18 = (bf16[16,4224]{1,0:T(8,128)(2,1)S(1)}, bf16[16,4224]{1,0:T(8,128)(2,1)}, u32[]{:S(2)}) copy-start(bf16[16,4224]{1,0:T(8,128)(2,1)} %copy-done.17) | copy-start | bytes 405508
  131.3 36.6 %copy-start.30 = (bf16[16,4224]{1,0:T(8,128)(2,1)S(1)}, bf16[16,4224]{1,0:T(8,128)(2,1)}, u32[]{:S(2)}) copy-start(bf16[16,4224]{1,0:T(8,128)(2,1)} %copy-done.29) | copy-start | bytes 405508
  131.3 37.3 %copy-start.4 = (bf16[16,4224]{1,0:T(8,128)(2,1)S(1)}, bf16[16,4224]{1,0:T(8,128)(2,1)}, u32[]{:S(2)}) copy-start(bf16[16,4224]{1,0:T(8,128)(2,1)} %copy-done.3) | copy-start | bytes 405508
  131.3 37.3 %copy-start.8 = (bf16[16,4224]{1,0:T(8,128)(2,1)S(1)}, bf16[16,4224]{1,0:T(8,128)(2,1)}, u32[]{:S(2)}) copy-start(bf16[16,4224]{1,0:T(8,128)(2,1)} %copy-done.7) | copy-start | bytes 405508
  131.3 37.3 %copy-start.16 = (bf16[16,4224]{1,0:T(8,128)(2,1)S(1)}, bf16[16,4224]{1,0:T(8,128)(2,1)}, u32[]{:S(2)}) copy-start(bf16[16,4224]{1,0:T(8,128)(2,1)} %copy-done.15) | copy-start | bytes 405508
  131.3 37.3 %copy-start.28 = (bf16[16,4224]{1,0:T(8,128)(2,1)S(1)}, bf16[16,4224]{1,0:T(8,128)(2,1)}, u32[]{:S(2)}) copy-start(bf16[16,4224]{1,0:T(8,128)(2,1)} %copy-done.27) | copy-start | bytes 405508
  131.3 38.1 %copy-start.14 = (bf16[16,4224]{1,0:T(8,128)(2,1)S(1)}, bf16[16,4224]{1,0:T(8,128)(2,1)}, u32[]{:S(2)}) copy-start(bf16[16,4224]{1,0:T(8,128)(2,1)} %copy-done.13) | copy-start | bytes 405508
  131.3 38.8 %copy-start.12 = (bf16[16,4224]{1,0:T(8,128)(2,1)S(1)}, bf16[16,4224]{1,0:T(8,128)(2,1)}, u32[]{:S(2)}) copy-start(bf16[16,4224]{1,0:T(8,128)(2,1)} %copy-done.11) | copy-start | bytes 405508
  135.0 35.8 %copy-start.22 = (bf16[16,4224]{1,0:T(8,128)(2,1)S(1)}, bf16[16,4224]{1,0:T(8,128)(2,1)}, u32[]{:S(2)}) copy-start(bf16[16,4224]{1,0:T(8,128)(2,1)} %copy-done.21) | copy-start | bytes 405508
  135.0 36.5 %copy-start.20 = (bf16[16,4224]{1,0:T(8,128)(2,1)S(1)}, bf16[16,4224]{1,0:T(8,128)(2,1)}, u32[]{:S(2)}) copy-start(bf16[16,4224]{1,0:T(8,128)(2,1)} %copy-done.19) | copy-start | bytes 405508
  137.7 48.6 %copy-start.33 = (f32[1,5632]{1,0:T(1,128)S(1)}, f32[1,5632]{1,0:T(1,128)}, u32[]{:S(2)}) copy-start(f32[1,5632]{1,0:T(1,128)} %param.9) | copy-start | bytes 67588
  137.8 48.6 %copy-start.34 = (f32[1,5632]{1,0:T(1,128)S(1)}, f32[1,5632]{1,0:T(1,128)}, u32[]{:S(2)}) copy-start(f32[1,5632]{1,0:T(1,128)} %param.8) | copy-start | bytes 67588
  139.3 33.0 %copy-start.31 = (bf16[16,4224]{1,0:T(8,128)(2,1)S(1)}, bf16[16,4224]{1,0:T(8,128)(2,1)}, u32[]{:S(2)}) copy-start(bf16[16,4224]{1,0:T(8,128)(2,1)} %add_convert_fusion.1) | copy-start | bytes 405508
  139.3 46.3 %all-to-all-start.2 = ((bf16[192,2,352]{2,1,0:T(2,128)(2,1)}), bf16[192,2,352]{2,1,0:T(2,128)(2,1)S(1)}, u32[]{:S(2)}, u32[]{:S(2)}) async-start(bf16[192,2,352]{2,1,0:T(2,128)(2,1)} %reshape.97), calls=%async_computation.2 | async-start | bytes 589824 | tf_op jit(solution)/shard_map/all_to_all | solution.py:107
  (18 other events, 157.2 us)

commit v6 on v5

--- a/solution.py
+++ b/solution.py
@@ -1,6 +1,8 @@
 import jax
 import jax.numpy as jnp
 from jax import lax
+from jax.experimental import pallas as pl
+from jax.experimental.pallas import tpu as pltpu
 from jax.sharding import Mesh, PartitionSpec as P
 
 
@@ -20,9 +22,25 @@
     return lax.dot_general(left, right, (((1,), (1,)), ((), ())), preferred_element_type=F32)
 
 
-def side_parts(rows, count):
-    parts = rows.reshape(rows.shape[0], 3, count, -1).transpose(2, 0, 1, 3)
-    return parts.reshape(count, rows.shape[0], -1)
+def side_parts(chunks, count):
+    rows, width = chunks[0].shape
+    part = width // (3 * count)
+
+    def body(*refs):
+        out = refs[-1]
+        for at, chunk in enumerate(refs[:-1]):
+            for third in range(3):
+                for place in range(count):
+                    begin = (third * count + place) * part
+                    out[place, at * rows : (at + 1) * rows, third * part : (third + 1) * part] = (
+                        chunk[:, begin : begin + part]
+                    )
+
+    shape = jax.ShapeDtypeStruct((count, len(chunks) * rows, 3 * part), chunks[0].dtype)
+    spec = pl.BlockSpec(memory_space=pltpu.VMEM)
+    return pl.pallas_call(
+        body, out_shape=shape, in_specs=[spec] * len(chunks), out_specs=spec
+    )(*chunks)
 
 
 def step(acts, out_grad, params, moment, second):
@@ -66,6 +84,7 @@
         [top[chunk * rows : (chunk + 1) * rows] for chunk in range(CHUNKS)]
     )
     down = [(s, s - 1) for s in range(1, sections)]
+
     def own(values, count):
         chunks = []
         for chunk in range(count):
@@ -73,7 +92,7 @@
             for behind in range(1, sections):
                 value = jnp.where(is_section[lead - behind], values[chunk + DEPTH * behind], value)
             chunks.append(value)
-        return jnp.concatenate(chunks, axis=0)
+        return chunks
 
     moved = []
     grads = []
@@ -94,14 +113,15 @@
             moved.append(lax.ppermute(passed, "pipe", down))
         done = tick + 1 - DEPTH * lead
         if done == CHUNKS - DEPTH or done == CHUNKS:
-            begin = len(parts) * (CHUNKS - DEPTH)
+            begin = len(parts)
             seen, _ = lax.optimization_barrier((grads[begin:], passed if begin == 0 else grad))
-            parts.append(side_parts(own(seen, done - begin), side))
-    arrived = lax.all_to_all(jnp.concatenate(parts, axis=1), SIDE, 0, 0, tiled=True)
+            parts += own(seen, done - begin)
+    parts = side_parts(parts, side)
+    arrived = lax.all_to_all(parts, SIDE, 0, 0, tiled=True)
     passes, arrived = lax.optimization_barrier((passes, arrived))
     terms = rows_dot(hidden.reshape(-1, block), arrived.reshape(-1, arrived.shape[2]))
 
-    in_grads = own(passes, CHUNKS)
+    in_grads = jnp.concatenate(own(passes, CHUNKS), axis=0)
 
     terms = terms.astype(BF16).reshape(places, 2, -1)
     terms = lax.all_to_all(terms, DP, 0, 0, tiled=True)

time: 188 us -> 186 us (0.989)
  the two profiles are of different devices: /device:TPU:61 before, /device:TPU:1 now
where the time goes in v6:
time: 186 us; the launch traced here: 184 us
  waiting for transfers between devices  82 us (44%)
  starting transfers between devices  46 us (25%)
  matrix products  33.1 us (18%)
  local copies, waits for them, and re-layouts  9.67 us (5%)
  other arithmetic  9.26 us (5%)
  Pallas kernels  2.87 us (2%)
    ppermute x12, waiting for transfers between devices, step(): moved.append(lax.ppermute(passed, 'pipe', down))  55.2 us
    dot_general x15, matrix products, cols_dot(): lax.dot_general(left, right, (((1,), (1,)), ((), ())), preferred_element_...  15.8 us
    ppermute x12, starting transfers between devices, step(): moved.append(lax.ppermute(passed, 'pipe', down))  15.5 us
    dot_general x14, matrix products, step(): jnp.dot(d_gate_up, weights_in, preferred_element_type=F32)  14.7 us
    all_to_all x1, starting transfers between devices, step(): terms = lax.all_to_all(terms, DP, 0, 0, tiled=True)  13.2 us
    all_to_all x1, waiting for transfers between devices, step(): terms = lax.all_to_all(terms, DP, 0, 0, tiled=True)  12.3 us
    all_to_all x1, starting transfers between devices, step(): arrived = lax.all_to_all(parts, SIDE, 0, 0, tiled=True)  12.2 us
    all_to_all x1, waiting for transfers between devices, step(): arrived = lax.all_to_all(parts, SIDE, 0, 0, tiled=True)  10.3 us
  transfers between devices with their start and end apart: 15, of which 13 were waited for; matrix products, arithmetic and copies ran while one was open for 18% of the time, Pallas kernels for 0%

profile of v6, /device:TPU:1, one launch (start us, length us, event | category | flops | bytes accessed | tf_op | source)
XLA Modules:
  0.0 183.9 jit_solution(262054498540874329)
XLA Ops:
  1.9 3.8 %fusion.28 = f32[128,512]{1,0:T(8,128)S(1)} fusion(bf16[128,4224]{1,0:T(8,128)(2,1)S(1)} %bitcast.112, bf16[1,768,4224]{2,1,0:T(8,128)(2,1)} %param.7), kind=kOutput, calls=%fused_computation.30 | convolution fusion | flops 553648128 | bytes 5668864 | tf_op jit(solution)/shard_map/dot_general | solution.py:22
  6.3 2.2 %copy-done.1 = bf16[1,768,4224]{2,1,0:T(8,128)(2,1)S(1)} copy-done((bf16[1,768,4224]{2,1,0:T(8,128)(2,1)S(1)}, bf16[1,768,4224]{2,1,0:T(8,128)(2,1)}, u32[]{:S(2)}) %copy-start.1) | copy-done | bytes 6488088
  9.9 1.3 collective-permute-start.1
  12.6 1.3 collective-permute-start
  13.9 5.7 %collective-permute-done.1 = bf16[16,4224]{1,0:T(8,128)(2,1)S(1)} collective-permute-done((bf16[16,4224]{1,0:T(8,128)(2,1)S(1)}, bf16[16,4224]{1,0:T(8,128)(2,1)S(1)}, u32[]{:S(2)}, u32[]{:S(2)}) %collective-permute-start.1) | collective-permute-done | bytes 135200 | tf_op jit(solution)/shard_map/ppermute | solution.py:113
  21.0 1.3 collective-permute-start.3
  22.3 2.3 %collective-permute-done = bf16[16,4224]{1,0:T(8,128)(2,1)S(1)} collective-permute-done((bf16[16,4224]{1,0:T(8,128)(2,1)S(1)}, bf16[16,4224]{1,0:T(8,128)(2,1)S(1)}, u32[]{:S(2)}, u32[]{:S(2)}) %collective-permute-start) | collective-permute-done | bytes 135200 | tf_op jit(solution)/shard_map/ppermute | solution.py:113
  26.0 1.3 collective-permute-start.2
  27.3 10.4 %collective-permute-done.3 = bf16[16,4224]{1,0:T(8,128)(2,1)S(1)} collective-permute-done((bf16[16,4224]{1,0:T(8,128)(2,1)S(1)}, bf16[16,4224]{1,0:T(8,128)(2,1)S(1)}, u32[]{:S(2)}, u32[]{:S(2)}) %collective-permute-start.3) | collective-permute-done | bytes 135200 | tf_op jit(solution)/shard_map/ppermute | solution.py:113
  39.1 1.3 collective-permute-start.5
  40.4 1.3 collective-permute-done.2
  43.1 1.3 collective-permute-start.4
  44.4 5.2 %collective-permute-done.5 = bf16[16,4224]{1,0:T(8,128)(2,1)S(1)} collective-permute-done((bf16[16,4224]{1,0:T(8,128)(2,1)S(1)}, bf16[16,4224]{1,0:T(8,128)(2,1)S(1)}, u32[]{:S(2)}, u32[]{:S(2)}) %collective-permute-start.5) | collective-permute-done | bytes 135200 | tf_op jit(solution)/shard_map/ppermute | solution.py:113
  51.1 1.3 collective-permute-start.7
  52.4 2.9 %collective-permute-done.4 = bf16[16,4224]{1,0:T(8,128)(2,1)S(1)} collective-permute-done((bf16[16,4224]{1,0:T(8,128)(2,1)S(1)}, bf16[16,4224]{1,0:T(8,128)(2,1)S(1)}, u32[]{:S(2)}, u32[]{:S(2)}) %collective-permute-start.4) | collective-permute-done | bytes 135200 | tf_op jit(solution)/shard_map/ppermute | solution.py:113
  61.2 7.7 %collective-permute-done.6 = bf16[16,4224]{1,0:T(8,128)(2,1)S(1)} collective-permute-done((bf16[16,4224]{1,0:T(8,128)(2,1)S(1)}, bf16[16,4224]{1,0:T(8,128)(2,1)S(1)}, u32[]{:S(2)}, u32[]{:S(2)}) %collective-permute-start.6) | collective-permute-done | bytes 135200 | tf_op jit(solution)/shard_map/ppermute | solution.py:113
  74.2 9.9 %collective-permute-done.8 = bf16[16,4224]{1,0:T(8,128)(2,1)S(1)} collective-permute-done((bf16[16,4224]{1,0:T(8,128)(2,1)S(1)}, bf16[16,4224]{1,0:T(8,128)(2,1)S(1)}, u32[]{:S(2)}, u32[]{:S(2)}) %collective-permute-start.8) | collective-permute-done | bytes 135200 | tf_op jit(solution)/shard_map/ppermute | solution.py:113
  87.8 9.2 %collective-permute-done.10 = bf16[16,4224]{1,0:T(8,128)(2,1)S(1)} collective-permute-done((bf16[16,4224]{1,0:T(8,128)(2,1)S(1)}, bf16[16,4224]{1,0:T(8,128)(2,1)S(1)}, u32[]{:S(2)}, u32[]{:S(2)}) %collective-permute-start.10) | collective-permute-done | bytes 135200 | tf_op jit(solution)/shard_map/ppermute | solution.py:113
  97.8 2.9 %shard_map.84 = bf16[8,128,528]{2,1,0:T(8,128)(2,1)} custom-call(bf16[16,4224]{1,0:T(8,128)(2,1)} %get-tuple-element.168.refs_0_, bf16[16,4224]{1,0:T(8,128)(2,1)} %get-tuple-element.157.refs_1_, bf16[16,4224]{1,0:T(8,128)(2,1)} %get-tuple-element.169.refs_2_, bf16[16,4224]{1,0:T(8,128)(2,1)} %get-tuple-element.156.refs_3_, ...), custom_call_target="tpu_custom_call" | custom-call | tf_op jit(solution)/shard_map/pallas_call | solution.py:41
  100.6 2.4 %copy.16 = bf16[8,128,528]{1,2,0:T(8,128)(2,1)} copy(bf16[8,128,528]{2,1,0:T(8,128)(2,1)} %shard_map.84) | data formatting | bytes 2162688 | tf_op jit(solution)/shard_map/pallas_call | solution.py:41
  103.0 12.2 %all-to-all-start = ((bf16[8,128,528]{1,2,0:T(8,128)(2,1)}), bf16[8,128,528]{1,2,0:T(8,128)(2,1)}, u32[]{:S(2)}, u32[]{:S(2)}) async-start(bf16[8,128,528]{1,2,0:T(8,128)(2,1)} %copy.16), calls=%async_computation | async-start | bytes 2162688 | tf_op jit(solution)/shard_map/all_to_all | solution.py:120
  115.3 2.2 %fusion.30 = f32[16,256]{1,0:T(8,128)S(1)} fusion(bf16[16,4224]{1,0:T(8,128)(2,1)S(1)} %collective-permute-done.11, bf16[1,768,4224]{2,1,0:T(8,128)(2,1)} %param.7), kind=kOutput, calls=%fused_computation.32 | convolution fusion | flops 34603008 | bytes 2314240 | tf_op jit(solution)/shard_map/dot_general | solution.py:22
  117.5 3.0 %add_convert_fusion = bf16[16,4224]{1,0:T(8,128)(2,1)S(1)} fusion(bf16[16,4224]{1,0:T(8,128)(2,1)S(1)} %collective-permute-done.11, f32[16,512]{1,0:T(8,128)S(1)} %get-tuple-element.92, f32[16,256]{1,0:T(8,128)S(1)} %fusion.30, bf16[1,768,4224]{2,1,0:T(8,128)(2,1)} %param.7), kind=kOutput, calls=%fused_computation.71 | convolution fusion | flops 69433344 | bytes 4644864 | tf_op jit(solution)/shard_map/dot_general | solution.py:109
  120.5 10.3 %all-to-all-done = bf16[8,128,528]{1,2,0:T(8,128)(2,1)} async-done(((bf16[8,128,528]{1,2,0:T(8,128)(2,1)}), bf16[8,128,528]{1,2,0:T(8,128)(2,1)}, u32[]{:S(2)}, u32[]{:S(2)}) %all-to-all-start) | async-done | bytes 1081376 | tf_op jit(solution)/shard_map/all_to_all | solution.py:120
  131.6 5.0 %all-to-all-start.1 = ((bf16[8,128,256]{2,1,0:T(8,128)(2,1)}), bf16[8,128,256]{2,1,0:T(8,128)(2,1)}, u32[]{:S(2)}, u32[]{:S(2)}) async-start(bf16[8,128,256]{2,1,0:T(8,128)(2,1)} %broadcast_in_dim.18), calls=%async_computation.1 | async-start | bytes 1048576 | tf_op jit(solution)/shard_map/all_to_all | solution.py:81
  136.5 2.2 %fusion.32 = f32[16,256]{1,0:T(8,128)S(1)} fusion(bf16[16,4224]{1,0:T(8,128)(2,1)S(1)} %collective-permute-done.10, bf16[1,768,4224]{2,1,0:T(8,128)(2,1)} %param.7), kind=kOutput, calls=%fused_computation.34 | convolution fusion | flops 34603008 | bytes 2314240 | tf_op jit(solution)/shard_map/dot_general | solution.py:22
  138.8 3.0 %add_convert_fusion.1 = bf16[16,4224]{1,0:T(8,128)(2,1)S(1)} fusion(bf16[16,4224]{1,0:T(8,128)(2,1)S(1)} %collective-permute-done.10, f32[16,512]{1,0:T(8,128)S(1)} %get-tuple-element.91, f32[16,256]{1,0:T(8,128)S(1)} %fusion.32, bf16[1,768,4224]{2,1,0:T(8,128)(2,1)} %param.7), kind=kOutput, calls=%fused_computation.72 | convolution fusion | flops 69433344 | bytes 4644864 | tf_op jit(solution)/shard_map/dot_general | solution.py:109
  141.7 4.3 %all-to-all-done.1 = bf16[8,128,256]{2,1,0:T(8,128)(2,1)} async-done(((bf16[8,128,256]{2,1,0:T(8,128)(2,1)}), bf16[8,128,256]{2,1,0:T(8,128)(2,1)}, u32[]{:S(2)}, u32[]{:S(2)}) %all-to-all-start.1) | async-done | bytes 524320 | tf_op jit(solution)/shard_map/all_to_all | solution.py:81
  146.0 2.5 %fusion.58 = bf16[256,528]{0,1:T(8,128)(2,1)} fusion(bf16[8,128,528]{1,2,0:T(8,128)(2,1)} %all-to-all-done, bf16[8,128,256]{2,1,0:T(8,128)(2,1)} %all-to-all-done.1), kind=kOutput, calls=%fused_computation.61 | convolution fusion | flops 276959232 | bytes 1875968 | tf_op jit(solution)/shard_map/dot_general | solution.py:18
  149.7 1.3 reshape.81
  151.0 13.2 %all-to-all-start.2 = ((bf16[192,2,352]{2,1,0:T(2,128)(2,1)}), bf16[192,2,352]{2,1,0:T(2,128)(2,1)S(1)}, u32[]{:S(2)}, u32[]{:S(2)}) async-start(bf16[192,2,352]{2,1,0:T(2,128)(2,1)} %reshape.81), calls=%async_computation.2 | async-start | bytes 589824 | tf_op jit(solution)/shard_map/all_to_all | solution.py:127
  170.1 12.3 %all-to-all-done.2 = bf16[192,2,352]{2,1,0:T(2,128)(2,1)S(1)} async-done(((bf16[192,2,352]{2,1,0:T(2,128)(2,1)}), bf16[192,2,352]{2,1,0:T(2,128)(2,1)S(1)}, u32[]{:S(2)}, u32[]{:S(2)}) %all-to-all-start.2) | async-done | bytes 270368 | tf_op jit(solution)/shard_map/all_to_all | solution.py:127
  (74 shorter events, 36.4 us)
Async XLA Ops:
  0.6 1.2 copy-start
  1.9 4.3 %copy-start.2 = (bf16[2,64,4224]{2,1,0:T(8,128)(2,1)S(1)}, bf16[2,64,4224]{2,1,0:T(8,128)(2,1)}, u32[]{:S(2)}) copy-start(bf16[2,64,4224]{2,1,0:T(8,128)(2,1)} %param.6) | copy-start | bytes 3244036
  5.7 2.8 %copy-start.1 = (bf16[1,768,4224]{2,1,0:T(8,128)(2,1)S(1)}, bf16[1,768,4224]{2,1,0:T(8,128)(2,1)}, u32[]{:S(2)}) copy-start(bf16[1,768,4224]{2,1,0:T(8,128)(2,1)} %param.7) | copy-start | bytes 19464196
  9.9 9.7 %collective-permute-start.1 = (bf16[16,4224]{1,0:T(8,128)(2,1)S(1)}, bf16[16,4224]{1,0:T(8,128)(2,1)S(1)}, u32[]{:S(2)}, u32[]{:S(2)}) collective-permute-start(bf16[16,4224]{1,0:T(8,128)(2,1)S(1)} %fusion.1), channel_id=1, source_target_pairs={{1,0},{2,1},{3,2},{5,4},{6,5},{7,6},{9,8},{10,9},{11,10},{13,12},{... | collective-permute-start | bytes 405512 | tf_op jit(solution)/shard_map/ppermute | solution.py:113
  12.6 12.0 %collective-permute-start = (bf16[16,4224]{1,0:T(8,128)(2,1)S(1)}, bf16[16,4224]{1,0:T(8,128)(2,1)S(1)}, u32[]{:S(2)}, u32[]{:S(2)}) collective-permute-start(bf16[16,4224]{1,0:T(8,128)(2,1)S(1)} %fusion), channel_id=1, source_target_pairs={{1,0},{2,1},{3,2},{5,4},{6,5},{7,6},{9,8},{10,9},{11,10},{13,12},{... | collective-permute-start | bytes 405512 | tf_op jit(solution)/shard_map/ppermute | solution.py:113
  21.0 16.7 %collective-permute-start.3 = (bf16[16,4224]{1,0:T(8,128)(2,1)S(1)}, bf16[16,4224]{1,0:T(8,128)(2,1)S(1)}, u32[]{:S(2)}, u32[]{:S(2)}) collective-permute-start(bf16[16,4224]{1,0:T(8,128)(2,1)S(1)} %add_convert_fusion.10), channel_id=1, source_target_pairs={{1,0},{2,1},{3,2},{5,4},{6,5},{7,6},{9,8},{10,9},{11,10},{13,12},{... | collective-permute-start | bytes 405512 | tf_op jit(solution)/shard_map/ppermute | solution.py:113
  26.0 15.7 %collective-permute-start.2 = (bf16[16,4224]{1,0:T(8,128)(2,1)S(1)}, bf16[16,4224]{1,0:T(8,128)(2,1)S(1)}, u32[]{:S(2)}, u32[]{:S(2)}) collective-permute-start(bf16[16,4224]{1,0:T(8,128)(2,1)S(1)} %add_convert_fusion.11), channel_id=1, source_target_pairs={{1,0},{2,1},{3,2},{5,4},{6,5},{7,6},{9,8},{10,9},{11,10},{13,12},{... | collective-permute-start | bytes 405512 | tf_op jit(solution)/shard_map/ppermute | solution.py:113
  39.1 10.6 %collective-permute-start.5 = (bf16[16,4224]{1,0:T(8,128)(2,1)S(1)}, bf16[16,4224]{1,0:T(8,128)(2,1)S(1)}, u32[]{:S(2)}, u32[]{:S(2)}) collective-permute-start(bf16[16,4224]{1,0:T(8,128)(2,1)S(1)} %add_convert_fusion.8), channel_id=1, source_target_pairs={{1,0},{2,1},{3,2},{5,4},{6,5},{7,6},{9,8},{10,9},{11,10},{13,12},{... | collective-permute-start | bytes 405512 | tf_op jit(solution)/shard_map/ppermute | solution.py:113
  43.1 12.1 %collective-permute-start.4 = (bf16[16,4224]{1,0:T(8,128)(2,1)S(1)}, bf16[16,4224]{1,0:T(8,128)(2,1)S(1)}, u32[]{:S(2)}, u32[]{:S(2)}) collective-permute-start(bf16[16,4224]{1,0:T(8,128)(2,1)S(1)} %add_convert_fusion.9), channel_id=1, source_target_pairs={{1,0},{2,1},{3,2},{5,4},{6,5},{7,6},{9,8},{10,9},{11,10},{13,12},{... | collective-permute-start | bytes 405512 | tf_op jit(solution)/shard_map/ppermute | solution.py:113
  51.1 7.4 %collective-permute-start.7 = (bf16[16,4224]{1,0:T(8,128)(2,1)S(1)}, bf16[16,4224]{1,0:T(8,128)(2,1)S(1)}, u32[]{:S(2)}, u32[]{:S(2)}) collective-permute-start(bf16[16,4224]{1,0:T(8,128)(2,1)S(1)} %add_convert_fusion.6), channel_id=1, source_target_pairs={{1,0},{2,1},{3,2},{5,4},{6,5},{7,6},{9,8},{10,9},{11,10},{13,12},{... | collective-permute-start | bytes 405512 | tf_op jit(solution)/shard_map/ppermute | solution.py:113
  56.7 12.2 %collective-permute-start.6 = (bf16[16,4224]{1,0:T(8,128)(2,1)S(1)}, bf16[16,4224]{1,0:T(8,128)(2,1)S(1)}, u32[]{:S(2)}, u32[]{:S(2)}) collective-permute-start(bf16[16,4224]{1,0:T(8,128)(2,1)S(1)} %add_convert_fusion.7), channel_id=1, source_target_pairs={{1,0},{2,1},{3,2},{5,4},{6,5},{7,6},{9,8},{10,9},{11,10},{13,12},{... | collective-permute-start | bytes 405512 | tf_op jit(solution)/shard_map/ppermute | solution.py:113
  59.9 11.7 %collective-permute-start.9 = (bf16[16,4224]{1,0:T(8,128)(2,1)S(1)}, bf16[16,4224]{1,0:T(8,128)(2,1)S(1)}, u32[]{:S(2)}, u32[]{:S(2)}) collective-permute-start(bf16[16,4224]{1,0:T(8,128)(2,1)S(1)} %add_convert_fusion.4), channel_id=1, source_target_pairs={{1,0},{2,1},{3,2},{5,4},{6,5},{7,6},{9,8},{10,9},{11,10},{13,12},{... | collective-permute-start | bytes 405512 | tf_op jit(solution)/shard_map/ppermute | solution.py:113
  70.2 13.9 %collective-permute-start.8 = (bf16[16,4224]{1,0:T(8,128)(2,1)S(1)}, bf16[16,4224]{1,0:T(8,128)(2,1)S(1)}, u32[]{:S(2)}, u32[]{:S(2)}) collective-permute-start(bf16[16,4224]{1,0:T(8,128)(2,1)S(1)} %add_convert_fusion.5), channel_id=1, source_target_pairs={{1,0},{2,1},{3,2},{5,4},{6,5},{7,6},{9,8},{10,9},{11,10},{13,12},{... | collective-permute-start | bytes 405512 | tf_op jit(solution)/shard_map/ppermute | solution.py:113
  72.9 14.9 %collective-permute-start.11 = (bf16[16,4224]{1,0:T(8,128)(2,1)S(1)}, bf16[16,4224]{1,0:T(8,128)(2,1)S(1)}, u32[]{:S(2)}, u32[]{:S(2)}) collective-permute-start(bf16[16,4224]{1,0:T(8,128)(2,1)S(1)} %add_convert_fusion.2), channel_id=1, source_target_pairs={{1,0},{2,1},{3,2},{5,4},{6,5},{7,6},{9,8},{10,9},{11,10},{13,12},{... | collective-permute-start | bytes 405512 | tf_op jit(solution)/shard_map/ppermute | solution.py:113
  85.5 11.5 %collective-permute-start.10 = (bf16[16,4224]{1,0:T(8,128)(2,1)S(1)}, bf16[16,4224]{1,0:T(8,128)(2,1)S(1)}, u32[]{:S(2)}, u32[]{:S(2)}) collective-permute-start(bf16[16,4224]{1,0:T(8,128)(2,1)S(1)} %add_convert_fusion.3), channel_id=1, source_target_pairs={{1,0},{2,1},{3,2},{5,4},{6,5},{7,6},{9,8},{10,9},{11,10},{13,12},{... | collective-permute-start | bytes 405512 | tf_op jit(solution)/shard_map/ppermute | solution.py:113
  103.0 27.7 %all-to-all-start = ((bf16[8,128,528]{1,2,0:T(8,128)(2,1)}), bf16[8,128,528]{1,2,0:T(8,128)(2,1)}, u32[]{:S(2)}, u32[]{:S(2)}) async-start(bf16[8,128,528]{1,2,0:T(8,128)(2,1)} %copy.16), calls=%async_computation | async-start | bytes 2162688 | tf_op jit(solution)/shard_map/all_to_all | solution.py:120
  131.6 14.5 %all-to-all-start.1 = ((bf16[8,128,256]{2,1,0:T(8,128)(2,1)}), bf16[8,128,256]{2,1,0:T(8,128)(2,1)}, u32[]{:S(2)}, u32[]{:S(2)}) async-start(bf16[8,128,256]{2,1,0:T(8,128)(2,1)} %broadcast_in_dim.18), calls=%async_computation.1 | async-start | bytes 1048576 | tf_op jit(solution)/shard_map/all_to_all | solution.py:81
  148.5 34.6 %copy-start.3 = (f32[1,5632]{1,0:T(1,128)S(1)}, f32[1,5632]{1,0:T(1,128)}, u32[]{:S(2)}) copy-start(f32[1,5632]{1,0:T(1,128)} %param.9) | copy-start | bytes 67588
  148.5 34.6 %copy-start.4 = (f32[1,5632]{1,0:T(1,128)S(1)}, f32[1,5632]{1,0:T(1,128)}, u32[]{:S(2)}) copy-start(f32[1,5632]{1,0:T(1,128)} %param.8) | copy-start | bytes 67588
  151.0 31.3 %all-to-all-start.2 = ((bf16[192,2,352]{2,1,0:T(2,128)(2,1)}), bf16[192,2,352]{2,1,0:T(2,128)(2,1)S(1)}, u32[]{:S(2)}, u32[]{:S(2)}) async-start(bf16[192,2,352]{2,1,0:T(2,128)(2,1)} %reshape.81), calls=%async_computation.2 | async-start | bytes 589824 | tf_op jit(solution)/shard_map/all_to_all | solution.py:127

commit v7 on v6

--- a/solution.py
+++ b/solution.py
@@ -83,7 +83,6 @@
     tops = lax.optimization_barrier(
         [top[chunk * rows : (chunk + 1) * rows] for chunk in range(CHUNKS)]
     )
-    down = [(s, s - 1) for s in range(1, sections)]
 
     def own(values, count):
         chunks = []
@@ -110,6 +109,11 @@
         passed = passed.astype(BF16)
         passes.append(passed)
         if tick + DEPTH < ticks:
+            down = [
+                (s, s - 1)
+                for s in range(1, sections)
+                if 0 <= tick - DEPTH * (lead - s) < CHUNKS
+            ]
             moved.append(lax.ppermute(passed, "pipe", down))
         done = tick + 1 - DEPTH * lead
         if done == CHUNKS - DEPTH or done == CHUNKS:
@@ -127,13 +131,14 @@
     terms = lax.all_to_all(terms, DP, 0, 0, tiled=True)
     sizes = tuple(lax.axis_size(name) for name in DP)
     summed = jnp.sum(terms.astype(F32).reshape(sizes + terms.shape[1:]), axis=(1, 2))
-    summed = summed.reshape(side, 4, -1).transpose(1, 0, 2).reshape(-1)
+    summed = summed.reshape(side, 4, -1).transpose(1, 0, 2).reshape(moment.shape)
+    summed = lax.optimization_barrier(summed)
 
     gradient = summed * float(tokens * places) ** (-0.5)
-    new_moment = 0.9 * moment[0] + 0.1 * gradient
-    new_second = 0.999 * second[0] + 0.001 * gradient * gradient
+    new_moment = 0.9 * moment + 0.1 * gradient
+    new_second = 0.999 * second + 0.001 * gradient * gradient
     update = new_moment / (1.0 - 0.9**10) / (jnp.sqrt(new_second / (1.0 - 0.999**10)) + 1e-08)
-    return (in_grads.reshape(acts.shape), new_moment[None], new_second[None], update[None])
+    return (in_grads.reshape(acts.shape), new_moment, new_second, update)
 
 
 def solution(mesh):

time: 186 us -> 183 us (0.984)
  waiting for transfers between devices: 82 us -> 79.3 us
    all_to_all x1, starting transfers between devices: 13.2 us -> 18.9 us  [step(): terms = lax.all_to_all(terms, DP, 0, 0, tiled=True)]
    ppermute x12, waiting for transfers between devices: 55.2 us -> 52.4 us  [step(): moved.append(lax.ppermute(passed, 'pipe', down))]
    ppermute x12, starting transfers between devices: 15.5 us -> 13 us  [step(): moved.append(lax.ppermute(passed, 'pipe', down))]
    all_to_all x1, starting transfers between devices: 12.2 us -> 10.1 us  [step(): arrived = lax.all_to_all(parts, SIDE, 0, 0, tiled=True)]
  transfers between devices with their start and end apart: 15 -> 15, of which waited for: 13 -> 10; matrix products, arithmetic and copies ran while one was open for 18% -> 18% of each run, Pallas kernels for 0% -> 0%
where the time goes in v7:
time: 183 us; the launch traced here: 182 us
  waiting for transfers between devices  79.3 us (43%)
  starting transfers between devices  47 us (26%)
  matrix products  33.1 us (18%)
  local copies, waits for them, and re-layouts  9.47 us (5%)
  other arithmetic  9.24 us (5%)
  Pallas kernels  2.87 us (2%)
    ppermute x12, waiting for transfers between devices, step(): moved.append(lax.ppermute(passed, 'pipe', down))  52.4 us
    all_to_all x1, starting transfers between devices, step(): terms = lax.all_to_all(terms, DP, 0, 0, tiled=True)  18.9 us
    dot_general x15, matrix products, cols_dot(): lax.dot_general(left, right, (((1,), (1,)), ((), ())), preferred_element_...  15.8 us
    dot_general x14, matrix products, step(): jnp.dot(d_gate_up, weights_in, preferred_element_type=F32)  14.7 us
    ppermute x12, starting transfers between devices, step(): moved.append(lax.ppermute(passed, 'pipe', down))  13 us
    all_to_all x1, waiting for transfers between devices, step(): terms = lax.all_to_all(terms, DP, 0, 0, tiled=True)  12.3 us
    all_to_all x1, waiting for transfers between devices, step(): arrived = lax.all_to_all(parts, SIDE, 0, 0, tiled=True)  10.3 us
    all_to_all x1, starting transfers between devices, step(): arrived = lax.all_to_all(parts, SIDE, 0, 0, tiled=True)  10.1 us
  transfers between devices with their start and end apart: 15, of which 10 were waited for; matrix products, arithmetic and copies ran while one was open for 18% of the time, Pallas kernels for 0%

profile of v7, /device:TPU:1, one launch (start us, length us, event | category | flops | bytes accessed | tf_op | source)
XLA Modules:
  0.0 181.9 jit_solution(13986304041003850754)
XLA Ops:
  0.7 1.2 copy-done
  1.9 3.8 %fusion.28 = f32[128,512]{1,0:T(8,128)S(1)} fusion(bf16[128,4224]{1,0:T(8,128)(2,1)S(1)} %bitcast.111, bf16[1,768,4224]{2,1,0:T(8,128)(2,1)} %param.7), kind=kOutput, calls=%fused_computation.30 | convolution fusion | flops 553648128 | bytes 5668864 | tf_op jit(solution)/shard_map/dot_general | solution.py:22
  6.3 2.2 %copy-done.1 = bf16[1,768,4224]{2,1,0:T(8,128)(2,1)S(1)} copy-done((bf16[1,768,4224]{2,1,0:T(8,128)(2,1)S(1)}, bf16[1,768,4224]{2,1,0:T(8,128)(2,1)}, u32[]{:S(2)}) %copy-start.1) | copy-done | bytes 6488088
  18.3 1.3 collective-permute-start.4
  21.0 1.3 collective-permute-start.5
  22.3 26.4 %collective-permute-done.4 = bf16[16,4224]{1,0:T(8,128)(2,1)S(1)} collective-permute-done((bf16[16,4224]{1,0:T(8,128)(2,1)S(1)}, bf16[16,4224]{1,0:T(8,128)(2,1)S(1)}, u32[]{:S(2)}, u32[]{:S(2)}) %collective-permute-start.4) | collective-permute-done | bytes 135200 | tf_op jit(solution)/shard_map/ppermute | solution.py:117
  50.1 1.3 collective-permute-start.6
  51.4 2.5 %collective-permute-done.5 = bf16[16,4224]{1,0:T(8,128)(2,1)S(1)} collective-permute-done((bf16[16,4224]{1,0:T(8,128)(2,1)S(1)}, bf16[16,4224]{1,0:T(8,128)(2,1)S(1)}, u32[]{:S(2)}, u32[]{:S(2)}) %collective-permute-start.5) | collective-permute-done | bytes 135200 | tf_op jit(solution)/shard_map/ppermute | solution.py:117
  55.3 1.3 collective-permute-start.7
  56.6 7.1 %collective-permute-done.6 = bf16[16,4224]{1,0:T(8,128)(2,1)S(1)} collective-permute-done((bf16[16,4224]{1,0:T(8,128)(2,1)S(1)}, bf16[16,4224]{1,0:T(8,128)(2,1)S(1)}, u32[]{:S(2)}, u32[]{:S(2)}) %collective-permute-start.6) | collective-permute-done | bytes 135200 | tf_op jit(solution)/shard_map/ppermute | solution.py:117
  65.0 1.3 collective-permute-start.8
  67.7 1.3 collective-permute-start.9
  69.0 4.1 %collective-permute-done.8 = bf16[16,4224]{1,0:T(8,128)(2,1)S(1)} collective-permute-done((bf16[16,4224]{1,0:T(8,128)(2,1)S(1)}, bf16[16,4224]{1,0:T(8,128)(2,1)S(1)}, u32[]{:S(2)}, u32[]{:S(2)}) %collective-permute-start.8) | collective-permute-done | bytes 135200 | tf_op jit(solution)/shard_map/ppermute | solution.py:117
  74.5 1.3 collective-permute-start.10
  77.8 1.3 collective-permute-start.11
  80.1 7.3 %collective-permute-done.10 = bf16[16,4224]{1,0:T(8,128)(2,1)S(1)} collective-permute-done((bf16[16,4224]{1,0:T(8,128)(2,1)S(1)}, bf16[16,4224]{1,0:T(8,128)(2,1)S(1)}, u32[]{:S(2)}, u32[]{:S(2)}) %collective-permute-start.10) | collective-permute-done | bytes 135200 | tf_op jit(solution)/shard_map/ppermute | solution.py:117
  87.4 4.3 %collective-permute-done.11 = bf16[16,4224]{1,0:T(8,128)(2,1)S(1)} collective-permute-done((bf16[16,4224]{1,0:T(8,128)(2,1)S(1)}, bf16[16,4224]{1,0:T(8,128)(2,1)S(1)}, u32[]{:S(2)}, u32[]{:S(2)}) %collective-permute-start.11) | collective-permute-done | bytes 135200 | tf_op jit(solution)/shard_map/ppermute | solution.py:117
  92.5 2.9 %shard_map.84 = bf16[8,128,528]{2,1,0:T(8,128)(2,1)} custom-call(bf16[16,4224]{1,0:T(8,128)(2,1)} %get-tuple-element.166.refs_0_, bf16[16,4224]{1,0:T(8,128)(2,1)} %get-tuple-element.157.refs_1_, bf16[16,4224]{1,0:T(8,128)(2,1)} %get-tuple-element.167.refs_2_, bf16[16,4224]{1,0:T(8,128)(2,1)} %get-tuple-element.156.refs_3_, ...), custom_call_target="tpu_custom_call" | custom-call | tf_op jit(solution)/shard_map/pallas_call | solution.py:41
  95.4 2.4 %copy.15 = bf16[8,128,528]{1,2,0:T(8,128)(2,1)} copy(bf16[8,128,528]{2,1,0:T(8,128)(2,1)} %shard_map.84) | data formatting | bytes 2162688 | tf_op jit(solution)/shard_map/pallas_call | solution.py:41
  97.8 10.1 %all-to-all-start = ((bf16[8,128,528]{1,2,0:T(8,128)(2,1)}), bf16[8,128,528]{1,2,0:T(8,128)(2,1)}, u32[]{:S(2)}, u32[]{:S(2)}) async-start(bf16[8,128,528]{1,2,0:T(8,128)(2,1)} %copy.15), calls=%async_computation | async-start | bytes 2162688 | tf_op jit(solution)/shard_map/all_to_all | solution.py:124
  107.9 2.2 %fusion.32 = f32[16,256]{1,0:T(8,128)S(1)} fusion(bf16[16,4224]{1,0:T(8,128)(2,1)S(1)} %collective-permute-done.10, bf16[1,768,4224]{2,1,0:T(8,128)(2,1)} %param.7), kind=kOutput, calls=%fused_computation.34 | convolution fusion | flops 34603008 | bytes 2314240 | tf_op jit(solution)/shard_map/dot_general | solution.py:22
  110.1 3.0 %add_convert_fusion.1 = bf16[16,4224]{1,0:T(8,128)(2,1)S(1)} fusion(bf16[16,4224]{1,0:T(8,128)(2,1)S(1)} %collective-permute-done.10, f32[16,512]{1,0:T(8,128)S(1)} %get-tuple-element.91, f32[16,256]{1,0:T(8,128)S(1)} %fusion.32, bf16[1,768,4224]{2,1,0:T(8,128)(2,1)} %param.7), kind=kOutput, calls=%fused_computation.72 | convolution fusion | flops 69433344 | bytes 4644864 | tf_op jit(solution)/shard_map/dot_general | solution.py:108
  113.1 10.3 %all-to-all-done = bf16[8,128,528]{1,2,0:T(8,128)(2,1)} async-done(((bf16[8,128,528]{1,2,0:T(8,128)(2,1)}), bf16[8,128,528]{1,2,0:T(8,128)(2,1)}, u32[]{:S(2)}, u32[]{:S(2)}) %all-to-all-start) | async-done | bytes 1081376 | tf_op jit(solution)/shard_map/all_to_all | solution.py:124
  124.1 5.0 %all-to-all-start.1 = ((bf16[8,128,256]{2,1,0:T(8,128)(2,1)}), bf16[8,128,256]{2,1,0:T(8,128)(2,1)}, u32[]{:S(2)}, u32[]{:S(2)}) async-start(bf16[8,128,256]{2,1,0:T(8,128)(2,1)} %broadcast_in_dim.15), calls=%async_computation.1 | async-start | bytes 1048576 | tf_op jit(solution)/shard_map/all_to_all | solution.py:81
  129.1 2.2 %fusion.30 = f32[16,256]{1,0:T(8,128)S(1)} fusion(bf16[16,4224]{1,0:T(8,128)(2,1)S(1)} %collective-permute-done.11, bf16[1,768,4224]{2,1,0:T(8,128)(2,1)} %param.7), kind=kOutput, calls=%fused_computation.32 | convolution fusion | flops 34603008 | bytes 2314240 | tf_op jit(solution)/shard_map/dot_general | solution.py:22
  131.4 3.0 %add_convert_fusion = bf16[16,4224]{1,0:T(8,128)(2,1)S(1)} fusion(bf16[16,4224]{1,0:T(8,128)(2,1)S(1)} %collective-permute-done.11, f32[16,512]{1,0:T(8,128)S(1)} %get-tuple-element.92, f32[16,256]{1,0:T(8,128)S(1)} %fusion.30, bf16[1,768,4224]{2,1,0:T(8,128)(2,1)} %param.7), kind=kOutput, calls=%fused_computation.71 | convolution fusion | flops 69433344 | bytes 4644864 | tf_op jit(solution)/shard_map/dot_general | solution.py:108
  134.3 4.3 %all-to-all-done.1 = bf16[8,128,256]{2,1,0:T(8,128)(2,1)} async-done(((bf16[8,128,256]{2,1,0:T(8,128)(2,1)}), bf16[8,128,256]{2,1,0:T(8,128)(2,1)}, u32[]{:S(2)}, u32[]{:S(2)}) %all-to-all-start.1) | async-done | bytes 524320 | tf_op jit(solution)/shard_map/all_to_all | solution.py:81
  138.6 2.5 %fusion.58 = bf16[256,528]{0,1:T(8,128)(2,1)} fusion(bf16[8,128,528]{1,2,0:T(8,128)(2,1)} %all-to-all-done, bf16[8,128,256]{2,1,0:T(8,128)(2,1)} %all-to-all-done.1), kind=kOutput, calls=%fused_computation.61 | convolution fusion | flops 276959232 | bytes 1875968 | tf_op jit(solution)/shard_map/dot_general | solution.py:18
  141.1 1.2 copy.16
  142.3 1.3 reshape.38
  143.6 18.9 %all-to-all-start.2 = ((bf16[192,2,352]{2,1,0:T(2,128)(2,1)}), bf16[192,2,352]{2,1,0:T(2,128)(2,1)S(1)}, u32[]{:S(2)}, u32[]{:S(2)}) async-start(bf16[192,2,352]{2,1,0:T(2,128)(2,1)} %reshape.38), calls=%async_computation.2 | async-start | bytes 589824 | tf_op jit(solution)/shard_map/all_to_all | solution.py:131
  168.4 12.3 %all-to-all-done.2 = bf16[192,2,352]{2,1,0:T(2,128)(2,1)S(1)} async-done(((bf16[192,2,352]{2,1,0:T(2,128)(2,1)}), bf16[192,2,352]{2,1,0:T(2,128)(2,1)S(1)}, u32[]{:S(2)}, u32[]{:S(2)}) %all-to-all-start.2) | async-done | bytes 270368 | tf_op jit(solution)/shard_map/all_to_all | solution.py:131
  (70 shorter events, 30.1 us)
Async XLA Ops:
  0.6 1.2 copy-start
  1.9 4.3 %copy-start.2 = (bf16[2,64,4224]{2,1,0:T(8,128)(2,1)S(1)}, bf16[2,64,4224]{2,1,0:T(8,128)(2,1)}, u32[]{:S(2)}) copy-start(bf16[2,64,4224]{2,1,0:T(8,128)(2,1)} %param.6) | copy-start | bytes 3244036
  5.7 2.8 %copy-start.1 = (bf16[1,768,4224]{2,1,0:T(8,128)(2,1)S(1)}, bf16[1,768,4224]{2,1,0:T(8,128)(2,1)}, u32[]{:S(2)}) copy-start(bf16[1,768,4224]{2,1,0:T(8,128)(2,1)} %param.7) | copy-start | bytes 19464196
  9.9 2.7 %collective-permute-start = (bf16[16,4224]{1,0:T(8,128)(2,1)S(1)}, bf16[16,4224]{1,0:T(8,128)(2,1)S(1)}, u32[]{:S(2)}, u32[]{:S(2)}) collective-permute-start(bf16[16,4224]{1,0:T(8,128)(2,1)S(1)} %fusion), channel_id=1, source_target_pairs={{3,2},{7,6},{11,10},{15,14},{19,18},{23,22},{27,26},{31,30},{35,34... | collective-permute-start | bytes 405512 | tf_op jit(solution)/shard_map/ppermute | solution.py:117
  12.0 2.8 %collective-permute-start.1 = (bf16[16,4224]{1,0:T(8,128)(2,1)S(1)}, bf16[16,4224]{1,0:T(8,128)(2,1)S(1)}, u32[]{:S(2)}, u32[]{:S(2)}) collective-permute-start(bf16[16,4224]{1,0:T(8,128)(2,1)S(1)} %fusion.1), channel_id=1, source_target_pairs={{3,2},{7,6},{11,10},{15,14},{19,18},{23,22},{27,26},{31,30},{35,34... | collective-permute-start | bytes 405512 | tf_op jit(solution)/shard_map/ppermute | solution.py:117
  14.1 2.8 %collective-permute-start.2 = (bf16[16,4224]{1,0:T(8,128)(2,1)S(1)}, bf16[16,4224]{1,0:T(8,128)(2,1)S(1)}, u32[]{:S(2)}, u32[]{:S(2)}) collective-permute-start(bf16[16,4224]{1,0:T(8,128)(2,1)S(1)} %add_convert_fusion.11), channel_id=1, source_target_pairs={{2,1},{3,2},{6,5},{7,6},{10,9},{11,10},{14,13},{15,14},{18,17},{19... | collective-permute-start | bytes 405512 | tf_op jit(solution)/shard_map/ppermute | solution.py:117
  16.2 3.4 %collective-permute-start.3 = (bf16[16,4224]{1,0:T(8,128)(2,1)S(1)}, bf16[16,4224]{1,0:T(8,128)(2,1)S(1)}, u32[]{:S(2)}, u32[]{:S(2)}) collective-permute-start(bf16[16,4224]{1,0:T(8,128)(2,1)S(1)} %add_convert_fusion.10), channel_id=1, source_target_pairs={{2,1},{3,2},{6,5},{7,6},{10,9},{11,10},{14,13},{15,14},{18,17},{19... | collective-permute-start | bytes 405512 | tf_op jit(solution)/shard_map/ppermute | solution.py:117
  18.3 30.5 %collective-permute-start.4 = (bf16[16,4224]{1,0:T(8,128)(2,1)S(1)}, bf16[16,4224]{1,0:T(8,128)(2,1)S(1)}, u32[]{:S(2)}, u32[]{:S(2)}) collective-permute-start(bf16[16,4224]{1,0:T(8,128)(2,1)S(1)} %add_convert_fusion.9), channel_id=1, source_target_pairs={{1,0},{2,1},{3,2},{5,4},{6,5},{7,6},{9,8},{10,9},{11,10},{13,12},{... | collective-permute-start | bytes 405512 | tf_op jit(solution)/shard_map/ppermute | solution.py:117
  21.0 32.9 %collective-permute-start.5 = (bf16[16,4224]{1,0:T(8,128)(2,1)S(1)}, bf16[16,4224]{1,0:T(8,128)(2,1)S(1)}, u32[]{:S(2)}, u32[]{:S(2)}) collective-permute-start(bf16[16,4224]{1,0:T(8,128)(2,1)S(1)} %add_convert_fusion.8), channel_id=1, source_target_pairs={{1,0},{2,1},{3,2},{5,4},{6,5},{7,6},{9,8},{10,9},{11,10},{13,12},{... | collective-permute-start | bytes 405512 | tf_op jit(solution)/shard_map/ppermute | solution.py:117
  50.1 13.6 %collective-permute-start.6 = (bf16[16,4224]{1,0:T(8,128)(2,1)S(1)}, bf16[16,4224]{1,0:T(8,128)(2,1)S(1)}, u32[]{:S(2)}, u32[]{:S(2)}) collective-permute-start(bf16[16,4224]{1,0:T(8,128)(2,1)S(1)} %add_convert_fusion.7), channel_id=1, source_target_pairs={{1,0},{2,1},{3,2},{5,4},{6,5},{7,6},{9,8},{10,9},{11,10},{13,12},{... | collective-permute-start | bytes 405512 | tf_op jit(solution)/shard_map/ppermute | solution.py:117
  55.3 11.0 %collective-permute-start.7 = (bf16[16,4224]{1,0:T(8,128)(2,1)S(1)}, bf16[16,4224]{1,0:T(8,128)(2,1)S(1)}, u32[]{:S(2)}, u32[]{:S(2)}) collective-permute-start(bf16[16,4224]{1,0:T(8,128)(2,1)S(1)} %add_convert_fusion.6), channel_id=1, source_target_pairs={{1,0},{2,1},{3,2},{5,4},{6,5},{7,6},{9,8},{10,9},{11,10},{13,12},{... | collective-permute-start | bytes 405512 | tf_op jit(solution)/shard_map/ppermute | solution.py:117
  65.0 8.1 %collective-permute-start.8 = (bf16[16,4224]{1,0:T(8,128)(2,1)S(1)}, bf16[16,4224]{1,0:T(8,128)(2,1)S(1)}, u32[]{:S(2)}, u32[]{:S(2)}) collective-permute-start(bf16[16,4224]{1,0:T(8,128)(2,1)S(1)} %add_convert_fusion.5), channel_id=1, source_target_pairs={{1,0},{2,1},{5,4},{6,5},{9,8},{10,9},{13,12},{14,13},{17,16},{18,1... | collective-permute-start | bytes 405512 | tf_op jit(solution)/shard_map/ppermute | solution.py:117
  67.7 8.7 %collective-permute-start.9 = (bf16[16,4224]{1,0:T(8,128)(2,1)S(1)}, bf16[16,4224]{1,0:T(8,128)(2,1)S(1)}, u32[]{:S(2)}, u32[]{:S(2)}) collective-permute-start(bf16[16,4224]{1,0:T(8,128)(2,1)S(1)} %add_convert_fusion.4), channel_id=1, source_target_pairs={{1,0},{2,1},{5,4},{6,5},{9,8},{10,9},{13,12},{14,13},{17,16},{18,1... | collective-permute-start | bytes 405512 | tf_op jit(solution)/shard_map/ppermute | solution.py:117
  74.5 12.9 %collective-permute-start.10 = (bf16[16,4224]{1,0:T(8,128)(2,1)S(1)}, bf16[16,4224]{1,0:T(8,128)(2,1)S(1)}, u32[]{:S(2)}, u32[]{:S(2)}) collective-permute-start(bf16[16,4224]{1,0:T(8,128)(2,1)S(1)} %add_convert_fusion.3), channel_id=1, source_target_pairs={{1,0},{5,4},{9,8},{13,12},{17,16},{21,20},{25,24},{29,28},{33,32},... | collective-permute-start | bytes 405512 | tf_op jit(solution)/shard_map/ppermute | solution.py:117
  77.8 14.0 %collective-permute-start.11 = (bf16[16,4224]{1,0:T(8,128)(2,1)S(1)}, bf16[16,4224]{1,0:T(8,128)(2,1)S(1)}, u32[]{:S(2)}, u32[]{:S(2)}) collective-permute-start(bf16[16,4224]{1,0:T(8,128)(2,1)S(1)} %add_convert_fusion.2), channel_id=1, source_target_pairs={{1,0},{5,4},{9,8},{13,12},{17,16},{21,20},{25,24},{29,28},{33,32},... | collective-permute-start | bytes 405512 | tf_op jit(solution)/shard_map/ppermute | solution.py:117
  97.8 25.5 %all-to-all-start = ((bf16[8,128,528]{1,2,0:T(8,128)(2,1)}), bf16[8,128,528]{1,2,0:T(8,128)(2,1)}, u32[]{:S(2)}, u32[]{:S(2)}) async-start(bf16[8,128,528]{1,2,0:T(8,128)(2,1)} %copy.15), calls=%async_computation | async-start | bytes 2162688 | tf_op jit(solution)/shard_map/all_to_all | solution.py:124
  124.1 14.5 %all-to-all-start.1 = ((bf16[8,128,256]{2,1,0:T(8,128)(2,1)}), bf16[8,128,256]{2,1,0:T(8,128)(2,1)}, u32[]{:S(2)}, u32[]{:S(2)}) async-start(bf16[8,128,256]{2,1,0:T(8,128)(2,1)} %broadcast_in_dim.15), calls=%async_computation.1 | async-start | bytes 1048576 | tf_op jit(solution)/shard_map/all_to_all | solution.py:81
  141.1 40.0 %copy-start.3 = (f32[1,5632]{1,0:T(1,128)S(1)}, f32[1,5632]{1,0:T(1,128)}, u32[]{:S(2)}) copy-start(f32[1,5632]{1,0:T(1,128)} %param.9) | copy-start | bytes 67588
  141.1 40.0 %copy-start.4 = (f32[1,5632]{1,0:T(1,128)S(1)}, f32[1,5632]{1,0:T(1,128)}, u32[]{:S(2)}) copy-start(f32[1,5632]{1,0:T(1,128)} %param.8) | copy-start | bytes 67588
  143.6 37.0 %all-to-all-start.2 = ((bf16[192,2,352]{2,1,0:T(2,128)(2,1)}), bf16[192,2,352]{2,1,0:T(2,128)(2,1)S(1)}, u32[]{:S(2)}, u32[]{:S(2)}) async-start(bf16[192,2,352]{2,1,0:T(2,128)(2,1)} %reshape.38), calls=%async_computation.2 | async-start | bytes 589824 | tf_op jit(solution)/shard_map/all_to_all | solution.py:131

commit v8 on v7

--- a/solution.py
+++ b/solution.py
@@ -24,19 +24,20 @@
 
 def side_parts(chunks, count):
     rows, width = chunks[0].shape
-    part = width // (3 * count)
+    third = width // 3
+    part = third // count
 
     def body(*refs):
         out = refs[-1]
-        for at, chunk in enumerate(refs[:-1]):
-            for third in range(3):
-                for place in range(count):
-                    begin = (third * count + place) * part
-                    out[place, at * rows : (at + 1) * rows, third * part : (third + 1) * part] = (
-                        chunk[:, begin : begin + part]
-                    )
+        for at in range(3):
+            span = slice(at * third, (at + 1) * third)
+            turned = jnp.concatenate([chunk[:, span] for chunk in refs[:-1]], axis=0).T
+            for place in range(count):
+                out[place, at * part : (at + 1) * part, :] = (
+                    turned[place * part : (place + 1) * part]
+                )
 
-    shape = jax.ShapeDtypeStruct((count, len(chunks) * rows, 3 * part), chunks[0].dtype)
+    shape = jax.ShapeDtypeStruct((count, 3 * part, len(chunks) * rows), chunks[0].dtype)
     spec = pl.BlockSpec(memory_space=pltpu.VMEM)
     return pl.pallas_call(
         body, out_shape=shape, in_specs=[spec] * len(chunks), out_specs=spec
@@ -123,6 +124,7 @@
     parts = side_parts(parts, side)
     arrived = lax.all_to_all(parts, SIDE, 0, 0, tiled=True)
     passes, arrived = lax.optimization_barrier((passes, arrived))
+    arrived = arrived.transpose(0, 2, 1)
     terms = rows_dot(hidden.reshape(-1, block), arrived.reshape(-1, arrived.shape[2]))
 
     in_grads = jnp.concatenate(own(passes, CHUNKS), axis=0)

time: 183 us -> 180 us (0.984)
  local copies, waits for them, and re-layouts: 9.47 us -> 7.09 us
    pallas_call x1 -> x0, local copies, waits for them, and re-layouts: 2.38 us -> none  [side_parts(): pl.pallas_call(body, out_shape=shape, in_specs=[spec] * len(chunks), out_...]
where the time goes in v8:
time: 180 us; the launch traced here: 179 us
  waiting for transfers between devices  79.2 us (44%)
  starting transfers between devices  47 us (26%)
  matrix products  33.1 us (18%)
  other arithmetic  9.34 us (5%)
  local copies, waits for them, and re-layouts  7.09 us (4%)
  Pallas kernels  2.61 us (1%)
    ppermute x12, waiting for transfers between devices, step(): moved.append(lax.ppermute(passed, 'pipe', down))  52.4 us
    all_to_all x1, starting transfers between devices, step(): terms = lax.all_to_all(terms, DP, 0, 0, tiled=True)  18.9 us
    dot_general x15, matrix products, cols_dot(): lax.dot_general(left, right, (((1,), (1,)), ((), ())), preferred_element_...  15.8 us
    dot_general x14, matrix products, step(): jnp.dot(d_gate_up, weights_in, preferred_element_type=F32)  14.7 us
    ppermute x12, starting transfers between devices, step(): moved.append(lax.ppermute(passed, 'pipe', down))  13 us
    all_to_all x1, waiting for transfers between devices, step(): terms = lax.all_to_all(terms, DP, 0, 0, tiled=True)  12.3 us
    all_to_all x1, waiting for transfers between devices, step(): arrived = lax.all_to_all(parts, SIDE, 0, 0, tiled=True)  10.3 us
    all_to_all x1, starting transfers between devices, step(): arrived = lax.all_to_all(parts, SIDE, 0, 0, tiled=True)  10.1 us
  transfers between devices with their start and end apart: 15, of which 10 were waited for; matrix products, arithmetic and copies ran while one was open for 18% of the time, Pallas kernels for 0%

profile of v8, /device:TPU:1, one launch (start us, length us, event | category | flops | bytes accessed | tf_op | source)
XLA Modules:
  0.0 179.3 jit_solution(15662528707513622656)
XLA Ops:
  0.7 1.2 copy-done
  1.9 3.8 %fusion.28 = f32[128,512]{1,0:T(8,128)S(1)} fusion(bf16[128,4224]{1,0:T(8,128)(2,1)S(1)} %bitcast.113, bf16[1,768,4224]{2,1,0:T(8,128)(2,1)} %param.7), kind=kOutput, calls=%fused_computation.30 | convolution fusion | flops 553648128 | bytes 5668864 | tf_op jit(solution)/shard_map/dot_general | solution.py:22
  6.3 2.2 %copy-done.1 = bf16[1,768,4224]{2,1,0:T(8,128)(2,1)S(1)} copy-done((bf16[1,768,4224]{2,1,0:T(8,128)(2,1)S(1)}, bf16[1,768,4224]{2,1,0:T(8,128)(2,1)}, u32[]{:S(2)}) %copy-start.1) | copy-done | bytes 6488088
  18.3 1.3 collective-permute-start.4
  21.0 1.3 collective-permute-start.5
  22.3 26.4 %collective-permute-done.4 = bf16[16,4224]{1,0:T(8,128)(2,1)S(1)} collective-permute-done((bf16[16,4224]{1,0:T(8,128)(2,1)S(1)}, bf16[16,4224]{1,0:T(8,128)(2,1)S(1)}, u32[]{:S(2)}, u32[]{:S(2)}) %collective-permute-start.4) | collective-permute-done | bytes 135200 | tf_op jit(solution)/shard_map/ppermute | solution.py:118
  50.1 1.3 collective-permute-start.6
  51.4 2.5 %collective-permute-done.5 = bf16[16,4224]{1,0:T(8,128)(2,1)S(1)} collective-permute-done((bf16[16,4224]{1,0:T(8,128)(2,1)S(1)}, bf16[16,4224]{1,0:T(8,128)(2,1)S(1)}, u32[]{:S(2)}, u32[]{:S(2)}) %collective-permute-start.5) | collective-permute-done | bytes 135200 | tf_op jit(solution)/shard_map/ppermute | solution.py:118
  55.3 1.3 collective-permute-start.7
  56.6 7.1 %collective-permute-done.6 = bf16[16,4224]{1,0:T(8,128)(2,1)S(1)} collective-permute-done((bf16[16,4224]{1,0:T(8,128)(2,1)S(1)}, bf16[16,4224]{1,0:T(8,128)(2,1)S(1)}, u32[]{:S(2)}, u32[]{:S(2)}) %collective-permute-start.6) | collective-permute-done | bytes 135200 | tf_op jit(solution)/shard_map/ppermute | solution.py:118
  65.0 1.3 collective-permute-start.8
  67.7 1.3 collective-permute-start.9
  69.0 4.1 %collective-permute-done.8 = bf16[16,4224]{1,0:T(8,128)(2,1)S(1)} collective-permute-done((bf16[16,4224]{1,0:T(8,128)(2,1)S(1)}, bf16[16,4224]{1,0:T(8,128)(2,1)S(1)}, u32[]{:S(2)}, u32[]{:S(2)}) %collective-permute-start.8) | collective-permute-done | bytes 135200 | tf_op jit(solution)/shard_map/ppermute | solution.py:118
  74.5 1.3 collective-permute-start.10
  77.8 1.3 collective-permute-start.11
  79.1 1.0 select_select_fusion.2
  80.2 7.3 %collective-permute-done.10 = bf16[16,4224]{1,0:T(8,128)(2,1)S(1)} collective-permute-done((bf16[16,4224]{1,0:T(8,128)(2,1)S(1)}, bf16[16,4224]{1,0:T(8,128)(2,1)S(1)}, u32[]{:S(2)}, u32[]{:S(2)}) %collective-permute-start.10) | collective-permute-done | bytes 135200 | tf_op jit(solution)/shard_map/ppermute | solution.py:118
  87.4 4.3 %collective-permute-done.11 = bf16[16,4224]{1,0:T(8,128)(2,1)S(1)} collective-permute-done((bf16[16,4224]{1,0:T(8,128)(2,1)S(1)}, bf16[16,4224]{1,0:T(8,128)(2,1)S(1)}, u32[]{:S(2)}, u32[]{:S(2)}) %collective-permute-start.11) | collective-permute-done | bytes 135200 | tf_op jit(solution)/shard_map/ppermute | solution.py:118
  92.6 2.6 %shard_map.84 = bf16[8,528,128]{2,1,0:T(8,128)(2,1)} custom-call(bf16[16,4224]{1,0:T(8,128)(2,1)} %get-tuple-element.166.refs_0_, bf16[16,4224]{1,0:T(8,128)(2,1)} %get-tuple-element.157.refs_1_, bf16[16,4224]{1,0:T(8,128)(2,1)} %get-tuple-element.167.refs_2_, bf16[16,4224]{1,0:T(8,128)(2,1)} %get-tuple-element.156.refs_3_, ...), custom_call_target="tpu_custom_call" | custom-call | tf_op jit(solution)/shard_map/pallas_call | solution.py:42
  95.2 10.1 %all-to-all-start = ((bf16[8,528,128]{2,1,0:T(8,128)(2,1)}), bf16[8,528,128]{2,1,0:T(8,128)(2,1)}, u32[]{:S(2)}, u32[]{:S(2)}) async-start(bf16[8,528,128]{2,1,0:T(8,128)(2,1)} %shard_map.84), calls=%async_computation | async-start | bytes 2162688 | tf_op jit(solution)/shard_map/all_to_all | solution.py:125
  105.3 2.2 %fusion.32 = f32[16,256]{1,0:T(8,128)S(1)} fusion(bf16[16,4224]{1,0:T(8,128)(2,1)S(1)} %collective-permute-done.10, bf16[1,768,4224]{2,1,0:T(8,128)(2,1)} %param.7), kind=kOutput, calls=%fused_computation.34 | convolution fusion | flops 34603008 | bytes 2314240 | tf_op jit(solution)/shard_map/dot_general | solution.py:22
  107.5 3.0 %add_convert_fusion.1 = bf16[16,4224]{1,0:T(8,128)(2,1)S(1)} fusion(bf16[16,4224]{1,0:T(8,128)(2,1)S(1)} %collective-permute-done.10, f32[16,512]{1,0:T(8,128)S(1)} %get-tuple-element.91, f32[16,256]{1,0:T(8,128)S(1)} %fusion.32, bf16[1,768,4224]{2,1,0:T(8,128)(2,1)} %param.7), kind=kOutput, calls=%fused_computation.73 | convolution fusion | flops 69433344 | bytes 4644864 | tf_op jit(solution)/shard_map/dot_general | solution.py:109
  110.4 10.3 %all-to-all-done = bf16[8,528,128]{2,1,0:T(8,128)(2,1)} async-done(((bf16[8,528,128]{2,1,0:T(8,128)(2,1)}), bf16[8,528,128]{2,1,0:T(8,128)(2,1)}, u32[]{:S(2)}, u32[]{:S(2)}) %all-to-all-start) | async-done | bytes 1081376 | tf_op jit(solution)/shard_map/all_to_all | solution.py:125
  121.5 5.0 %all-to-all-start.1 = ((bf16[8,128,256]{2,1,0:T(8,128)(2,1)}), bf16[8,128,256]{2,1,0:T(8,128)(2,1)}, u32[]{:S(2)}, u32[]{:S(2)}) async-start(bf16[8,128,256]{2,1,0:T(8,128)(2,1)} %broadcast_in_dim.15), calls=%async_computation.1 | async-start | bytes 1048576 | tf_op jit(solution)/shard_map/all_to_all | solution.py:82
  126.5 2.2 %fusion.30 = f32[16,256]{1,0:T(8,128)S(1)} fusion(bf16[16,4224]{1,0:T(8,128)(2,1)S(1)} %collective-permute-done.11, bf16[1,768,4224]{2,1,0:T(8,128)(2,1)} %param.7), kind=kOutput, calls=%fused_computation.32 | convolution fusion | flops 34603008 | bytes 2314240 | tf_op jit(solution)/shard_map/dot_general | solution.py:22
  128.8 3.0 %add_convert_fusion = bf16[16,4224]{1,0:T(8,128)(2,1)S(1)} fusion(bf16[16,4224]{1,0:T(8,128)(2,1)S(1)} %collective-permute-done.11, f32[16,512]{1,0:T(8,128)S(1)} %get-tuple-element.92, f32[16,256]{1,0:T(8,128)S(1)} %fusion.30, bf16[1,768,4224]{2,1,0:T(8,128)(2,1)} %param.7), kind=kOutput, calls=%fused_computation.72 | convolution fusion | flops 69433344 | bytes 4644864 | tf_op jit(solution)/shard_map/dot_general | solution.py:109
  131.7 4.3 %all-to-all-done.1 = bf16[8,128,256]{2,1,0:T(8,128)(2,1)} async-done(((bf16[8,128,256]{2,1,0:T(8,128)(2,1)}), bf16[8,128,256]{2,1,0:T(8,128)(2,1)}, u32[]{:S(2)}, u32[]{:S(2)}) %all-to-all-start.1) | async-done | bytes 524320 | tf_op jit(solution)/shard_map/all_to_all | solution.py:82
  136.0 2.5 %fusion.58 = bf16[256,528]{0,1:T(8,128)(2,1)} fusion(bf16[8,128,256]{2,1,0:T(8,128)(2,1)} %all-to-all-done.1, bf16[8,528,128]{2,1,0:T(8,128)(2,1)} %all-to-all-done), kind=kOutput, calls=%fused_computation.61 | convolution fusion | flops 276959232 | bytes 1875968 | tf_op jit(solution)/shard_map/dot_general | solution.py:18
  138.5 1.2 copy.10
  139.7 1.3 reshape.38
  141.0 18.9 %all-to-all-start.2 = ((bf16[192,2,352]{2,1,0:T(2,128)(2,1)}), bf16[192,2,352]{2,1,0:T(2,128)(2,1)S(1)}, u32[]{:S(2)}, u32[]{:S(2)}) async-start(bf16[192,2,352]{2,1,0:T(2,128)(2,1)} %reshape.38), calls=%async_computation.2 | async-start | bytes 589824 | tf_op jit(solution)/shard_map/all_to_all | solution.py:133
  165.8 12.3 %all-to-all-done.2 = bf16[192,2,352]{2,1,0:T(2,128)(2,1)S(1)} async-done(((bf16[192,2,352]{2,1,0:T(2,128)(2,1)}), bf16[192,2,352]{2,1,0:T(2,128)(2,1)S(1)}, u32[]{:S(2)}, u32[]{:S(2)}) %all-to-all-start.2) | async-done | bytes 270368 | tf_op jit(solution)/shard_map/all_to_all | solution.py:133
  (69 shorter events, 29.2 us)
Async XLA Ops:
  0.6 1.2 copy-start
  1.9 4.3 %copy-start.2 = (bf16[2,64,4224]{2,1,0:T(8,128)(2,1)S(1)}, bf16[2,64,4224]{2,1,0:T(8,128)(2,1)}, u32[]{:S(2)}) copy-start(bf16[2,64,4224]{2,1,0:T(8,128)(2,1)} %param.6) | copy-start | bytes 3244036
  5.7 2.8 %copy-start.1 = (bf16[1,768,4224]{2,1,0:T(8,128)(2,1)S(1)}, bf16[1,768,4224]{2,1,0:T(8,128)(2,1)}, u32[]{:S(2)}) copy-start(bf16[1,768,4224]{2,1,0:T(8,128)(2,1)} %param.7) | copy-start | bytes 19464196
  9.9 2.7 %collective-permute-start = (bf16[16,4224]{1,0:T(8,128)(2,1)S(1)}, bf16[16,4224]{1,0:T(8,128)(2,1)S(1)}, u32[]{:S(2)}, u32[]{:S(2)}) collective-permute-start(bf16[16,4224]{1,0:T(8,128)(2,1)S(1)} %fusion), channel_id=1, source_target_pairs={{3,2},{7,6},{11,10},{15,14},{19,18},{23,22},{27,26},{31,30},{35,34... | collective-permute-start | bytes 405512 | tf_op jit(solution)/shard_map/ppermute | solution.py:118
  12.0 2.8 %collective-permute-start.1 = (bf16[16,4224]{1,0:T(8,128)(2,1)S(1)}, bf16[16,4224]{1,0:T(8,128)(2,1)S(1)}, u32[]{:S(2)}, u32[]{:S(2)}) collective-permute-start(bf16[16,4224]{1,0:T(8,128)(2,1)S(1)} %fusion.1), channel_id=1, source_target_pairs={{3,2},{7,6},{11,10},{15,14},{19,18},{23,22},{27,26},{31,30},{35,34... | collective-permute-start | bytes 405512 | tf_op jit(solution)/shard_map/ppermute | solution.py:118
  14.1 2.8 %collective-permute-start.2 = (bf16[16,4224]{1,0:T(8,128)(2,1)S(1)}, bf16[16,4224]{1,0:T(8,128)(2,1)S(1)}, u32[]{:S(2)}, u32[]{:S(2)}) collective-permute-start(bf16[16,4224]{1,0:T(8,128)(2,1)S(1)} %add_convert_fusion.11), channel_id=1, source_target_pairs={{2,1},{3,2},{6,5},{7,6},{10,9},{11,10},{14,13},{15,14},{18,17},{19... | collective-permute-start | bytes 405512 | tf_op jit(solution)/shard_map/ppermute | solution.py:118
  16.2 3.4 %collective-permute-start.3 = (bf16[16,4224]{1,0:T(8,128)(2,1)S(1)}, bf16[16,4224]{1,0:T(8,128)(2,1)S(1)}, u32[]{:S(2)}, u32[]{:S(2)}) collective-permute-start(bf16[16,4224]{1,0:T(8,128)(2,1)S(1)} %add_convert_fusion.10), channel_id=1, source_target_pairs={{2,1},{3,2},{6,5},{7,6},{10,9},{11,10},{14,13},{15,14},{18,17},{19... | collective-permute-start | bytes 405512 | tf_op jit(solution)/shard_map/ppermute | solution.py:118
  18.3 30.5 %collective-permute-start.4 = (bf16[16,4224]{1,0:T(8,128)(2,1)S(1)}, bf16[16,4224]{1,0:T(8,128)(2,1)S(1)}, u32[]{:S(2)}, u32[]{:S(2)}) collective-permute-start(bf16[16,4224]{1,0:T(8,128)(2,1)S(1)} %add_convert_fusion.9), channel_id=1, source_target_pairs={{1,0},{2,1},{3,2},{5,4},{6,5},{7,6},{9,8},{10,9},{11,10},{13,12},{... | collective-permute-start | bytes 405512 | tf_op jit(solution)/shard_map/ppermute | solution.py:118
  21.0 32.9 %collective-permute-start.5 = (bf16[16,4224]{1,0:T(8,128)(2,1)S(1)}, bf16[16,4224]{1,0:T(8,128)(2,1)S(1)}, u32[]{:S(2)}, u32[]{:S(2)}) collective-permute-start(bf16[16,4224]{1,0:T(8,128)(2,1)S(1)} %add_convert_fusion.8), channel_id=1, source_target_pairs={{1,0},{2,1},{3,2},{5,4},{6,5},{7,6},{9,8},{10,9},{11,10},{13,12},{... | collective-permute-start | bytes 405512 | tf_op jit(solution)/shard_map/ppermute | solution.py:118
  50.1 13.6 %collective-permute-start.6 = (bf16[16,4224]{1,0:T(8,128)(2,1)S(1)}, bf16[16,4224]{1,0:T(8,128)(2,1)S(1)}, u32[]{:S(2)}, u32[]{:S(2)}) collective-permute-start(bf16[16,4224]{1,0:T(8,128)(2,1)S(1)} %add_convert_fusion.7), channel_id=1, source_target_pairs={{1,0},{2,1},{3,2},{5,4},{6,5},{7,6},{9,8},{10,9},{11,10},{13,12},{... | collective-permute-start | bytes 405512 | tf_op jit(solution)/shard_map/ppermute | solution.py:118
  55.3 11.0 %collective-permute-start.7 = (bf16[16,4224]{1,0:T(8,128)(2,1)S(1)}, bf16[16,4224]{1,0:T(8,128)(2,1)S(1)}, u32[]{:S(2)}, u32[]{:S(2)}) collective-permute-start(bf16[16,4224]{1,0:T(8,128)(2,1)S(1)} %add_convert_fusion.6), channel_id=1, source_target_pairs={{1,0},{2,1},{3,2},{5,4},{6,5},{7,6},{9,8},{10,9},{11,10},{13,12},{... | collective-permute-start | bytes 405512 | tf_op jit(solution)/shard_map/ppermute | solution.py:118
  65.0 8.1 %collective-permute-start.8 = (bf16[16,4224]{1,0:T(8,128)(2,1)S(1)}, bf16[16,4224]{1,0:T(8,128)(2,1)S(1)}, u32[]{:S(2)}, u32[]{:S(2)}) collective-permute-start(bf16[16,4224]{1,0:T(8,128)(2,1)S(1)} %add_convert_fusion.5), channel_id=1, source_target_pairs={{1,0},{2,1},{5,4},{6,5},{9,8},{10,9},{13,12},{14,13},{17,16},{18,1... | collective-permute-start | bytes 405512 | tf_op jit(solution)/shard_map/ppermute | solution.py:118
  67.7 8.7 %collective-permute-start.9 = (bf16[16,4224]{1,0:T(8,128)(2,1)S(1)}, bf16[16,4224]{1,0:T(8,128)(2,1)S(1)}, u32[]{:S(2)}, u32[]{:S(2)}) collective-permute-start(bf16[16,4224]{1,0:T(8,128)(2,1)S(1)} %add_convert_fusion.4), channel_id=1, source_target_pairs={{1,0},{2,1},{5,4},{6,5},{9,8},{10,9},{13,12},{14,13},{17,16},{18,1... | collective-permute-start | bytes 405512 | tf_op jit(solution)/shard_map/ppermute | solution.py:118
  74.5 12.9 %collective-permute-start.10 = (bf16[16,4224]{1,0:T(8,128)(2,1)S(1)}, bf16[16,4224]{1,0:T(8,128)(2,1)S(1)}, u32[]{:S(2)}, u32[]{:S(2)}) collective-permute-start(bf16[16,4224]{1,0:T(8,128)(2,1)S(1)} %add_convert_fusion.3), channel_id=1, source_target_pairs={{1,0},{5,4},{9,8},{13,12},{17,16},{21,20},{25,24},{29,28},{33,32},... | collective-permute-start | bytes 405512 | tf_op jit(solution)/shard_map/ppermute | solution.py:118
  77.8 14.0 %collective-permute-start.11 = (bf16[16,4224]{1,0:T(8,128)(2,1)S(1)}, bf16[16,4224]{1,0:T(8,128)(2,1)S(1)}, u32[]{:S(2)}, u32[]{:S(2)}) collective-permute-start(bf16[16,4224]{1,0:T(8,128)(2,1)S(1)} %add_convert_fusion.2), channel_id=1, source_target_pairs={{1,0},{5,4},{9,8},{13,12},{17,16},{21,20},{25,24},{29,28},{33,32},... | collective-permute-start | bytes 405512 | tf_op jit(solution)/shard_map/ppermute | solution.py:118
  95.2 25.5 %all-to-all-start = ((bf16[8,528,128]{2,1,0:T(8,128)(2,1)}), bf16[8,528,128]{2,1,0:T(8,128)(2,1)}, u32[]{:S(2)}, u32[]{:S(2)}) async-start(bf16[8,528,128]{2,1,0:T(8,128)(2,1)} %shard_map.84), calls=%async_computation | async-start | bytes 2162688 | tf_op jit(solution)/shard_map/all_to_all | solution.py:125
  121.5 14.5 %all-to-all-start.1 = ((bf16[8,128,256]{2,1,0:T(8,128)(2,1)}), bf16[8,128,256]{2,1,0:T(8,128)(2,1)}, u32[]{:S(2)}, u32[]{:S(2)}) async-start(bf16[8,128,256]{2,1,0:T(8,128)(2,1)} %broadcast_in_dim.15), calls=%async_computation.1 | async-start | bytes 1048576 | tf_op jit(solution)/shard_map/all_to_all | solution.py:82
  138.5 40.0 %copy-start.3 = (f32[1,5632]{1,0:T(1,128)S(1)}, f32[1,5632]{1,0:T(1,128)}, u32[]{:S(2)}) copy-start(f32[1,5632]{1,0:T(1,128)} %param.9) | copy-start | bytes 67588
  138.5 40.0 %copy-start.4 = (f32[1,5632]{1,0:T(1,128)S(1)}, f32[1,5632]{1,0:T(1,128)}, u32[]{:S(2)}) copy-start(f32[1,5632]{1,0:T(1,128)} %param.8) | copy-start | bytes 67588
  141.0 37.0 %all-to-all-start.2 = ((bf16[192,2,352]{2,1,0:T(2,128)(2,1)}), bf16[192,2,352]{2,1,0:T(2,128)(2,1)S(1)}, u32[]{:S(2)}, u32[]{:S(2)}) async-start(bf16[192,2,352]{2,1,0:T(2,128)(2,1)} %reshape.38), calls=%async_computation.2 | async-start | bytes 589824 | tf_op jit(solution)/shard_map/all_to_all | solution.py:133
